TPU v7x, 32 devices: a whole 2x2x4 slice. The times are simulated.
32 devices in a mesh: seq: 8 (over z, y), head: 4 (over x, core).
Axes of the slice: x: 2, y: 2, z: 4, core: 2. Of those that a mesh axis runs over, the one named last changes fastest.
Arguments:
- inputs: bfloat16 [2048, 768], P('seq', 'head'), may hold values from -6 to 6
- pre_gain: float32 [768], replicated, may hold values from 0.5 to 1.5
- w_query: bfloat16 [768, 768], P(None, 'head'), may hold values from -0.21875 to 0.21875
- w_key: bfloat16 [768, 768], P(None, 'head'), may hold values from -0.21875 to 0.21875
- w_value: bfloat16 [768, 768], P(None, 'head'), may hold values from -0.21875 to 0.21875
- mix_gate: bfloat16 [768, 768], P(None, 'head'), may hold values from -0.21875 to 0.21875
- w_rate: bfloat16 [768, 12], P(None, 'head'), may hold values from -0.21875 to 0.21875
- rate_bias: float32 [12], P('head'), may hold values from -1.5 to 1.5
- inner_gain: float32 [12, 64], P('head'), may hold values from 0.5 to 1.5
- inner_bias: float32 [12, 64], P('head'), may hold values from -1.8 to 1.8
- init_w_one: float32 [12, 64, 256], P('head'), may hold values from -0.75 to 0.75
- init_b_one: float32 [12, 256], P('head'), may hold values from -1.8 to 1.8
- init_w_two: float32 [12, 256, 64], P('head'), may hold values from -0.375 to 0.375
- init_b_two: float32 [12, 64], P('head'), may hold values from -3 to 3
- post_gain: float32 [768], P('head'), may hold values from 0.5 to 1.5
- post_bias: float32 [768], P('head'), may hold values from -3 to 3
- w_out: bfloat16 [768, 768], P('head'), may hold values from -0.21875 to 0.21875
- ffn_gain: float32 [768], replicated, may hold values from 0.5 to 1.5
- w_gate: bfloat16 [768, 2048], P(None, 'head'), may hold values from -0.21875 to 0.21875
- w_up: bfloat16 [768, 2048], P(None, 'head'), may hold values from -0.21875 to 0.21875
- w_down: bfloat16 [2048, 768], P('head'), may hold values from -0.125 to 0.125
- cotangent: bfloat16 [2048, 768], P('seq', 'head'), may hold values from -6 to 6
Outputs:
- outputs: float32 [2048, 768], P('seq', 'head')
- grad_inputs: float32 [2048, 768], P('seq', 'head')
- grad_pre_gain: float32 [768], P('head')
- grad_w_query: float32 [768, 768], P('seq', 'head')
- grad_w_key: float32 [768, 768], P('seq', 'head')
- grad_w_value: float32 [768, 768], P('seq', 'head')
- grad_mix_gate: float32 [768, 768], P('seq', 'head')
- grad_w_rate: float32 [768, 12], P(None, 'head')
- grad_rate_bias: float32 [12], P('head')
- grad_inner_gain: float32 [12, 64], P('head')
- grad_inner_bias: float32 [12, 64], P('head')
- grad_init_w_one: float32 [12, 64, 256], P('head')
- grad_init_b_one: float32 [12, 256], P('head')
- grad_init_w_two: float32 [12, 256, 64], P('head')
- grad_init_b_two: float32 [12, 64], P('head')
- grad_post_gain: float32 [768], P('head')
- grad_post_bias: float32 [768], P('head')
- grad_w_out: float32 [768, 768], P('head', 'seq')
- grad_ffn_gain: float32 [768], replicated
- grad_w_gate: float32 [768, 2048], P('seq', 'head')
- grad_w_up: float32 [768, 2048], P('seq', 'head')
- grad_w_down: float32 [2048, 768], P('head', 'seq')
All inputs are finite; a program needn't handle non-finite values.
Results may differ from a plain program's by a relative error of at most 0.028.
Values may be sent and summed in bfloat16 or wider, within the bound.
A program may use at most 128 MiB of HBM per device.

v0:
```python
import jax
import jax.numpy as jnp
from jax import lax
from jax.sharding import PartitionSpec as P

MINI = 16
CHAIN = 8


eps_norm = 1e-06
gelu_scale = 0.7978845608028654
highest = lax.Precision.HIGHEST


def shifted(block, axis, distance):
    devices = range(lax.axis_size(axis))
    route = [(i - distance, i) for i in devices if i - distance in devices]
    return lax.ppermute(block, axis, route)


def gelu_tanh(arg_value):
    cubic = arg_value + 0.044715 * arg_value * arg_value * arg_value
    return 0.5 * arg_value * (1.0 + jnp.tanh(gelu_scale * cubic))


def gelu_derivative(arg_value):
    tangent = jnp.tanh(gelu_scale * (arg_value + 0.044715 * arg_value * arg_value * arg_value))
    return 0.5 * (1.0 + tangent) + 0.5 * arg_value * (1.0 - tangent * tangent) * gelu_scale * (
        1.0 + 0.134145 * arg_value * arg_value
    )


def head_norm(values_in, gain_vec, bias_vec):
    centre = jnp.mean(values_in, axis=-1, keepdims=True)
    centred = values_in - centre
    inv_scale = lax.rsqrt(jnp.mean(centred * centred, axis=-1, keepdims=True) + eps_norm)
    normed = centred * inv_scale
    return (normed, inv_scale, normed * gain_vec + bias_vec)


def mixing_contraction(form, left, right):
    return jnp.einsum(form, left, right, precision=highest)


def bf_product(form, left, right):
    return jnp.einsum(form, left, right, preferred_element_type=jnp.float32)


def inner_update(state_now, mini_batch, gain_vec, bias_vec):
    first_weight, first_bias, second_weight, second_bias = state_now
    query_mb, key_minibatch, value_mb, rate_mb = mini_batch
    first_preactivation = (
        mixing_contraction("uwf,ufo->uwo", key_minibatch, first_weight) + first_bias[:, None, :]
    )
    hidden_activation = gelu_tanh(first_preactivation)
    second_preactivation = (
        mixing_contraction("aeq,aqj->aej", hidden_activation, second_weight)
        + second_bias[:, None, :]
    )
    normed, inv_scale, predicted = head_norm(
        second_preactivation, gain_vec[:, None, :], bias_vec[:, None, :]
    )
    recon_err = predicted - (value_mb - key_minibatch)
    grad_normed = recon_err * gain_vec[:, None, :]
    second_gradient = inv_scale * (
        grad_normed
        - jnp.mean(grad_normed, axis=-1, keepdims=True)
        - normed * jnp.mean(grad_normed * normed, axis=-1, keepdims=True)
    )
    first_gradient = mixing_contraction(
        "tfu,tvu->tfv", second_gradient, second_weight
    ) * gelu_derivative(first_preactivation)
    first_update_step = rate_mb[:, :, None] * first_gradient
    second_update_step = rate_mb[:, :, None] * second_gradient
    updated_state = (
        first_weight - mixing_contraction("pgw,pgy->pwy", key_minibatch, first_update_step),
        first_bias - jnp.sum(first_update_step, axis=1),
        second_weight - mixing_contraction("voj,von->vjn", hidden_activation, second_update_step),
        second_bias - jnp.sum(second_update_step, axis=1),
    )
    return (updated_state, hidden_activation, first_update_step, second_update_step)


def inner_step(state_now, mini_batch, gain_vec, bias_vec):
    updated_state, hidden_activation, first_update_step, second_update_step = inner_update(
        state_now, mini_batch, gain_vec, bias_vec
    )
    first_weight, first_bias, second_weight, second_bias = state_now
    query_mb = mini_batch[0]
    key_minibatch = mini_batch[1]
    rows_mini = query_mb.shape[1]
    causal = jnp.tril(jnp.ones((rows_mini, rows_mini), jnp.float32))
    attend_one = (
        bf_product(
            "htd,hsd->hts", query_mb.astype(jnp.bfloat16), key_minibatch.astype(jnp.bfloat16)
        )
        * causal
        + causal
    )
    bar_one = (
        mixing_contraction("htd,hdi->hti", query_mb, first_weight)
        + first_bias[:, None, :]
        - mixing_contraction("hts,hsi->hti", attend_one, first_update_step)
    )
    hidden_bar = gelu_tanh(bar_one)
    attend_two = mixing_contraction("hti,hsi->hts", hidden_bar, hidden_activation) * causal + causal
    bar_two = (
        mixing_contraction("hti,hid->htd", hidden_bar, second_weight)
        + second_bias[:, None, :]
        - mixing_contraction("hts,hsd->htd", attend_two, second_update_step)
    )
    shaped = head_norm(bar_two, gain_vec[:, None, :], bias_vec[:, None, :])[2]
    return (updated_state, query_mb + shaped)


def split_blocks(row_data, mini, head_count):
    total_rows = row_data.shape[0]
    return row_data.reshape(total_rows // mini, mini, head_count, -1).transpose(0, 2, 1, 3)


def prepare_blocks(query_rows, key_rows, value_rows, logit_rows, mini):
    total_rows, head_count = logit_rows.shape
    head_dim = query_rows.shape[1] // head_count
    rate_rows = jax.nn.sigmoid(logit_rows) / head_dim
    rate_blocks = rate_rows.reshape(total_rows // mini, mini, head_count).transpose(0, 2, 1)
    return (
        split_blocks(query_rows, mini, head_count),
        split_blocks(key_rows, mini, head_count),
        split_blocks(value_rows, mini, head_count),
        rate_blocks,
    )


def run_block(query_rows, key_rows, value_rows, logit_rows, state_now, gain_vec, bias_vec):
    blocks = prepare_blocks(query_rows, key_rows, value_rows, logit_rows, MINI)

    def advance(carry, mini_batch):
        return inner_step(carry, mini_batch, gain_vec, bias_vec)

    final_state, block_out = lax.scan(jax.checkpoint(advance), state_now, blocks)
    merged = block_out.transpose(0, 2, 1, 3).reshape(query_rows.shape)
    return (merged, final_state)


def run_states(query_rows, key_rows, value_rows, logit_rows, state_now, gain_vec, bias_vec):
    blocks = prepare_blocks(query_rows, key_rows, value_rows, logit_rows, MINI)

    def advance(carry, mini_batch):
        return (inner_update(carry, mini_batch, gain_vec, bias_vec)[0], None)

    final_state, _ = lax.scan(advance, state_now, blocks)
    return final_state


def local(
    inputs,
    pre_gain,
    w_query,
    w_key,
    w_value,
    mix_gate,
    w_rate,
    rate_bias,
    inner_gain,
    inner_bias,
    init_w_one,
    init_b_one,
    init_w_two,
    init_b_two,
    post_gain,
    post_bias,
    w_out,
    ffn_gain,
    w_gate,
    w_up,
    w_down,
    cotangent,
):
    full_width = pre_gain.shape[0]
    local_cols = inputs.shape[1]
    head_index = lax.axis_index("head")
    position = lax.axis_index("seq") % CHAIN
    whole_in = lax.all_gather(inputs, "head", axis=1, tiled=True).astype(jnp.float32)
    rms_one = lax.rsqrt(jnp.mean(whole_in * whole_in, axis=1, keepdims=True) + eps_norm)
    normed_one = (whole_in * rms_one * pre_gain).astype(jnp.bfloat16)
    queries = bf_product("rd,dc->rc", normed_one, w_query).astype(jnp.bfloat16).astype(jnp.float32)
    keys_in = bf_product("rd,dc->rc", normed_one, w_key).astype(jnp.bfloat16).astype(jnp.float32)
    values_in = (
        bf_product("rd,dc->rc", normed_one, w_value).astype(jnp.bfloat16).astype(jnp.float32)
    )
    gate_pre = bf_product("rd,dc->rc", normed_one, mix_gate)
    logits = bf_product("rd,dc->rc", normed_one, w_rate) + rate_bias
    init_state = (init_w_one, init_b_one, init_w_two, init_b_two)
    state_in = init_state
    for rounds in range(CHAIN - 1):
        state_out = run_states(
            queries, keys_in, values_in, logits, state_in, inner_gain, inner_bias
        )
        passed = shifted((state_out[0], state_out[1], state_out[2], state_out[3]), "seq", 1)
        state_in = tuple(
            (
                jnp.where(position == 0, start_part, got_part)
                for start_part, got_part in zip(init_state, passed)
            )
        )
    mixed = run_block(queries, keys_in, values_in, logits, state_in, inner_gain, inner_bias)[0]
    totals = lax.psum((jnp.sum(mixed, axis=1), jnp.sum(mixed * mixed, axis=1)), "head")
    mean_z = totals[0][:, None] / full_width
    var_z = totals[1][:, None] / full_width - mean_z * mean_z
    inv_z = lax.rsqrt(var_z + eps_norm)
    z_hat = (mixed - mean_z) * inv_z
    post_out = z_hat * post_gain + post_bias
    gate_act = gelu_tanh(gate_pre)
    gated_low = (post_out * gate_act).astype(jnp.bfloat16)
    out_whole = lax.psum(bf_product("rc,cd->rd", gated_low, w_out), "head")
    resid = whole_in + out_whole
    rms_two = lax.rsqrt(jnp.mean(resid * resid, axis=1, keepdims=True) + eps_norm)
    normed_two = (resid * rms_two * ffn_gain).astype(jnp.bfloat16)
    gate_val = bf_product("rd,df->rf", normed_two, w_gate)
    up_val = bf_product("rd,df->rf", normed_two, w_up)
    silu_gate = jax.nn.silu(gate_val)
    hidden_ffn = (silu_gate * up_val).astype(jnp.bfloat16)
    down_local = lax.psum_scatter(
        bf_product("rf,fd->rd", hidden_ffn, w_down).astype(jnp.bfloat16),
        "head",
        scatter_dimension=1,
        tiled=True,
    ).astype(jnp.float32)
    resid_local = lax.dynamic_slice_in_dim(resid, head_index * local_cols, local_cols, 1)
    outputs = resid_local + down_local
    grad_whole = lax.all_gather(cotangent, "head", axis=1, tiled=True)
    grad_down_t = bf_product("rd,rf->df", grad_whole, hidden_ffn)
    grad_hidden = bf_product("rd,fd->rf", grad_whole, w_down)
    sig_gate = jax.nn.sigmoid(gate_val)
    grad_gate_val = (grad_hidden * up_val * sig_gate * (1.0 + gate_val * (1.0 - sig_gate))).astype(
        jnp.bfloat16
    )
    grad_up_val = (grad_hidden * silu_gate).astype(jnp.bfloat16)
    gate_term = bf_product("rd,rf->df", normed_two, grad_gate_val)
    up_term = bf_product("rd,rf->df", normed_two, grad_up_val)
    grad_normed_two = bf_product("rf,df->rd", grad_gate_val, w_gate) + bf_product(
        "rf,df->rd", grad_up_val, w_up
    )
    scaled_two = grad_normed_two * ffn_gain
    resid_back = rms_two * (
        scaled_two - resid * rms_two * rms_two * jnp.mean(scaled_two * resid, axis=1, keepdims=True)
    )
    gain_two_term = jnp.sum(grad_normed_two * resid * rms_two, axis=0)
    resid_sum, gain_two = (
        lax.psum(resid_back.astype(jnp.bfloat16), "head").astype(jnp.float32),
        lax.psum(gain_two_term.astype(jnp.bfloat16), "head").astype(jnp.float32),
    )
    grad_resid = grad_whole.astype(jnp.float32) + resid_sum
    grad_out_val = grad_resid.astype(jnp.bfloat16)
    grad_out_t = bf_product("rd,rc->dc", grad_out_val, gated_low)
    grad_gated = bf_product("rd,cd->rc", grad_out_val, w_out)
    grad_post = grad_gated * gate_act
    grad_gate_pre = (grad_gated * post_out * gelu_derivative(gate_pre)).astype(jnp.bfloat16)
    post_gain_term = jnp.sum(grad_post * z_hat, axis=0)
    post_bias_term = jnp.sum(grad_post, axis=0)
    grad_zhat = grad_post * post_gain
    sums_back = lax.psum((jnp.sum(grad_zhat, axis=1), jnp.sum(grad_zhat * z_hat, axis=1)), "head")
    grad_mixed = inv_z * (
        grad_zhat - sums_back[0][:, None] / full_width - z_hat * sums_back[1][:, None] / full_width
    )
    block_result, pullback = jax.vjp(
        run_block, queries, keys_in, values_in, logits, state_in, inner_gain, inner_bias
    )
    carried = tuple((jnp.zeros_like(part_now) for part_now in state_in))
    for rounds in range(CHAIN - 1):
        state_grads = pullback((grad_mixed, carried))[4]
        passed_back = (
            shifted(state_grads[0].astype(jnp.bfloat16), "seq", -1).astype(jnp.float32),
            shifted(state_grads[1].astype(jnp.bfloat16), "seq", -1).astype(jnp.float32),
            shifted(state_grads[2].astype(jnp.bfloat16), "seq", -1).astype(jnp.float32),
            shifted(state_grads[3].astype(jnp.bfloat16), "seq", -1).astype(jnp.float32),
        )
        carried = tuple(
            (
                jnp.where(position == CHAIN - 1, jnp.zeros_like(got_part), got_part)
                for got_part in passed_back
            )
        )
    grad_q, grad_k, grad_v, grad_logits, grad_state, grad_inner_gain, grad_inner_bias = pullback(
        (grad_mixed, carried)
    )
    rate_bias_term = jnp.sum(grad_logits, axis=0)
    grad_q_low = grad_q.astype(jnp.bfloat16)
    grad_k_low = grad_k.astype(jnp.bfloat16)
    grad_v_low = grad_v.astype(jnp.bfloat16)
    grad_logit_low = grad_logits.astype(jnp.bfloat16)
    query_term = bf_product("rd,rc->dc", normed_one, grad_q_low)
    key_term = bf_product("rd,rc->dc", normed_one, grad_k_low)
    value_term = bf_product("rd,rc->dc", normed_one, grad_v_low)
    mixgate_term = bf_product("rd,rc->dc", normed_one, grad_gate_pre)
    rate_weight_term = bf_product("rd,rc->dc", normed_one, grad_logit_low)
    grad_normed_one = (
        bf_product("rc,dc->rd", grad_q_low, w_query)
        + bf_product("rc,dc->rd", grad_k_low, w_key)
        + bf_product("rc,dc->rd", grad_v_low, w_value)
        + bf_product("rc,dc->rd", grad_gate_pre, mix_gate)
        + bf_product("rc,dc->rd", grad_logit_low, w_rate)
    )
    scaled_one = grad_normed_one * pre_gain
    input_back = rms_one * (
        scaled_one
        - whole_in * rms_one * rms_one * jnp.mean(scaled_one * whole_in, axis=1, keepdims=True)
    )
    gain_one_term = jnp.sum(grad_normed_one * whole_in * rms_one, axis=0)
    input_local, gain_one = (
        lax.psum_scatter(
            input_back.astype(jnp.bfloat16), "head", scatter_dimension=1, tiled=True
        ).astype(jnp.float32),
        lax.psum_scatter(
            gain_one_term[None, :].astype(jnp.bfloat16), "head", scatter_dimension=1, tiled=True
        ).astype(jnp.float32),
    )
    grad_inputs = (
        lax.dynamic_slice_in_dim(grad_resid, head_index * local_cols, local_cols, 1) + input_local
    )
    init_terms = tuple(
        (jnp.where(position == 0, grad_part, jnp.zeros_like(grad_part)) for grad_part in grad_state)
    )
    small_sums = lax.psum(
        (
            gain_one[0],
            gain_two,
            post_gain_term,
            post_bias_term,
            rate_weight_term,
            rate_bias_term,
            grad_inner_gain,
            grad_inner_bias,
            init_terms[0],
            init_terms[1],
            init_terms[2],
            init_terms[3],
        ),
        "seq",
    )
    big_sums = (
        lax.psum_scatter(
            query_term.astype(jnp.bfloat16), "seq", scatter_dimension=0, tiled=True
        ).astype(jnp.float32),
        lax.psum_scatter(
            key_term.astype(jnp.bfloat16), "seq", scatter_dimension=0, tiled=True
        ).astype(jnp.float32),
        lax.psum_scatter(
            value_term.astype(jnp.bfloat16), "seq", scatter_dimension=0, tiled=True
        ).astype(jnp.float32),
        lax.psum_scatter(
            mixgate_term.astype(jnp.bfloat16), "seq", scatter_dimension=0, tiled=True
        ).astype(jnp.float32),
        lax.psum_scatter(
            grad_out_t.astype(jnp.bfloat16), "seq", scatter_dimension=0, tiled=True
        ).astype(jnp.float32),
        lax.psum_scatter(
            gate_term.astype(jnp.bfloat16), "seq", scatter_dimension=0, tiled=True
        ).astype(jnp.float32),
        lax.psum_scatter(
            up_term.astype(jnp.bfloat16), "seq", scatter_dimension=0, tiled=True
        ).astype(jnp.float32),
        lax.psum_scatter(
            grad_down_t.astype(jnp.bfloat16), "seq", scatter_dimension=0, tiled=True
        ).astype(jnp.float32),
    )
    return (
        outputs,
        grad_inputs,
        small_sums[0],
        big_sums[0],
        big_sums[1],
        big_sums[2],
        big_sums[3],
        small_sums[4],
        small_sums[5],
        small_sums[6],
        small_sums[7],
        small_sums[8],
        small_sums[9],
        small_sums[10],
        small_sums[11],
        small_sums[2],
        small_sums[3],
        big_sums[4].T,
        small_sums[1],
        big_sums[5],
        big_sums[6],
        big_sums[7].T,
    )


def solution(mesh):
    in_specs = (
        P("seq", "head"),
        P(),
        P(None, "head"),
        P(None, "head"),
        P(None, "head"),
        P(None, "head"),
        P(None, "head"),
        P("head"),
        P("head", None),
        P("head", None),
        P("head", None, None),
        P("head", None),
        P("head", None, None),
        P("head", None),
        P("head"),
        P("head"),
        P("head", None),
        P(),
        P(None, "head"),
        P(None, "head"),
        P("head", None),
        P("seq", "head"),
    )
    out_specs = (
        P("seq", "head"),
        P("seq", "head"),
        P("head"),
        P("seq", "head"),
        P("seq", "head"),
        P("seq", "head"),
        P("seq", "head"),
        P(None, "head"),
        P("head"),
        P("head", None),
        P("head", None),
        P("head", None, None),
        P("head", None),
        P("head", None, None),
        P("head", None),
        P("head"),
        P("head"),
        P("head", "seq"),
        P(),
        P("seq", "head"),
        P("seq", "head"),
        P("head", "seq"),
    )
    return jax.shard_map(local, mesh=mesh, in_specs=in_specs, out_specs=out_specs, check_vma=False)
```

profile of v0, /device:TPU:0, one launch (start us, length us, event | category | flops | bytes accessed | tf_op | source)
XLA Modules:
  0.0 3201.3 jit_solution(5874086660933849345)
XLA Ops:
  7.3 8.2 all_gather.6
  23.0 36.5 %while.346 = (s32[]{:T(128)}, f32[3,64,256]{2,1,0:T(8,128)S(1)}, f32[3,256]{1,0:T(4,128)S(1)}, f32[3,256,64]{1,2,0:T(8,128)S(1)}, f32[3,64]{1,0:T(4,128)S(1)}, /...) while((s32[]{:T(128)}, f32[3,64,256]{2,1,0:T(8,128)S(1)}, ...), condition=%wide.region_8.9_spmd.clone, body=%wide.region_1.8_spmd.sunk.clone | while | flops 47812656 | bytes 1881981 | solution.py:151
  59.5 3.4 collective-permute-start.3
  63.0 3.4 collective-permute-start.1
  66.4 3.4 collective-permute-start
  69.8 3.4 collective-permute-start.2
  74.9 3.2 collective-permute-done.2
  78.2 36.5 %while.347 = (s32[]{:T(128)}, f32[3,64,256]{2,1,0:T(8,128)S(1)}, f32[3,256]{1,0:T(4,128)S(1)}, f32[3,256,64]{1,2,0:T(8,128)S(1)}, f32[3,64]{1,0:T(4,128)S(1)}, /...) while((s32[]{:T(128)}, f32[3,64,256]{2,1,0:T(8,128)S(1)}, ...), condition=%wide.region_16.17_spmd.clone, body=%wide.region_9.16_spmd.sunk.clone | while | flops 47812656 | bytes 1881981 | solution.py:151
  114.7 4.4 collective-permute-start.7
  120.2 4.3 collective-permute-start.5
  127.0 4.3 collective-permute-start.6
  131.5 3.1 collective-permute-done.6
  134.6 36.5 %while.348 = (s32[]{:T(128)}, f32[3,64,256]{2,1,0:T(8,128)S(1)}, f32[3,256]{1,0:T(4,128)S(1)}, f32[3,256,64]{1,2,0:T(8,128)S(1)}, f32[3,64]{1,0:T(4,128)S(1)}, /...) while((s32[]{:T(128)}, f32[3,64,256]{2,1,0:T(8,128)S(1)}, ...), condition=%wide.region_24.25_spmd.clone, body=%wide.region_17.24_spmd.sunk.clone | while | flops 47812656 | bytes 1881981 | solution.py:151
  171.7 4.4 collective-permute-start.11
  176.1 6.1 all_gather.7
  182.3 4.8 collective-permute-start.9
  189.0 3.8 collective-permute-start.10
  194.3 3.6 collective-permute-done.10
  197.9 47.2 %while.349 = (s32[]{:T(128)}, f32[3,64,256]{2,1,0:T(8,128)S(1)}, f32[3,256]{1,0:T(4,128)S(1)}, f32[3,256,64]{1,2,0:T(8,128)S(1)}, f32[3,64]{1,0:T(4,128)S(1)}, /...) while((s32[]{:T(128)}, f32[3,64,256]{2,1,0:T(8,128)S(1)}, ...), condition=%wide.region_32.33_spmd.clone, body=%wide.region_25.32_spmd.sunk.clone | while | flops 47812656 | bytes 1881981 | solution.py:151
  245.1 4.4 collective-permute-start.15
  249.5 4.4 collective-permute-start.13
  263.4 47.2 %while.350 = (s32[]{:T(128)}, f32[3,64,256]{2,1,0:T(8,128)S(1)}, f32[3,256]{1,0:T(4,128)S(1)}, f32[3,256,64]{1,2,0:T(8,128)S(1)}, f32[3,64]{1,0:T(4,128)S(1)}, /...) while((s32[]{:T(128)}, f32[3,64,256]{2,1,0:T(8,128)S(1)}, ...), condition=%wide.region_40.41_spmd.clone, body=%wide.region_33.40_spmd.sunk.clone | while | flops 47812656 | bytes 1881981 | solution.py:151
  310.6 4.4 collective-permute-start.19
  315.0 3.1 collective-permute-start.17
  320.0 3.5 collective-permute-start.18
  326.9 47.2 %while.351 = (s32[]{:T(128)}, f32[3,64,256]{2,1,0:T(8,128)S(1)}, f32[3,256]{1,0:T(4,128)S(1)}, f32[3,256,64]{1,2,0:T(8,128)S(1)}, f32[3,64]{1,0:T(4,128)S(1)}, /...) while((s32[]{:T(128)}, f32[3,64,256]{2,1,0:T(8,128)S(1)}, ...), condition=%wide.region_48.49_spmd.clone, body=%wide.region_41.48_spmd.sunk.clone | while | flops 47812656 | bytes 1881981 | solution.py:151
  374.2 4.4 collective-permute-start.23
  380.0 3.3 collective-permute-start.21
  385.2 3.1 collective-permute-start.22
  391.5 47.2 %while.352 = (s32[]{:T(128)}, f32[3,64,256]{2,1,0:T(8,128)S(1)}, f32[3,256]{1,0:T(4,128)S(1)}, f32[3,256,64]{1,2,0:T(8,128)S(1)}, f32[3,64]{1,0:T(4,128)S(1)}, /...) while((s32[]{:T(128)}, f32[3,64,256]{2,1,0:T(8,128)S(1)}, ...), condition=%wide.region_56.57_spmd.clone, body=%wide.region_49.56_spmd.sunk.clone | while | flops 47812656 | bytes 1881981 | solution.py:151
  438.7 4.4 collective-permute-start.27
  447.3 3.2 collective-permute-start.25
  452.4 3.0 collective-permute-start.26
  458.7 124.6 %while.353 = (s32[]{:T(128)}, f32[3,64,256]{2,1,0:T(8,128)S(1)}, f32[3,256]{1,0:T(4,128)S(1)}, f32[3,256,64]{1,2,0:T(8,128)S(1)}, f32[3,64]{1,0:T(4,128)}, /*ind...) while((s32[]{:T(128)}, f32[3,64,256]{2,1,0:T(8,128)S(1)}, ...), condition=%wide.region_66.67_spmd.clone, body=%wide.region_57.66_spmd.sunk.clone | while | flops 72355424 | bytes 2810901 | solution.py:140
  588.3 5.7 all-reduce.3
  598.4 88.0 %while.354 = (s32[]{:T(128)}, f32[3,64,256]{2,1,0:T(8,128)S(1)}, f32[3,256]{1,0:T(4,128)S(1)}, f32[3,256,64]{1,2,0:T(8,128)S(1)}, f32[3,64]{1,0:T(4,128)S(1)}, /...) while((s32[]{:T(128)}, f32[3,64,256]{2,1,0:T(8,128)S(1)}, ...), condition=%wide.region_87.88_spmd.clone, body=%wide.region_80.87_spmd.sunk.clone | while | flops 47812656 | bytes 2678445 | solution.py:140
  695.8 29.4 all-reduce.10.cloned.1.call-done
  725.2 3.0 multiply_reduce_fusion.103
  728.2 5.9 all-reduce.2
  740.3 209.6 %while.361 = (s32[]{:T(128)}, f32[3,64,256]{2,1,0:T(8,128)S(1)}, f32[3,256]{1,0:T(4,128)S(1)}, f32[3,256,64]{1,2,0:T(8,128)S(1)}, f32[3,64]{1,0:T(4,128)S(1)}, /...) while((s32[]{:T(128)}, f32[3,64,256]{2,1,0:T(8,128)S(1)}, ...), condition=%wide.region_106.107_spmd.clone.clone, body=%wide.region_88.106_spmd.clone.sunk.clone | while | flops 168192752 | bytes 8404690 | solution.py:140
  957.4 4.5 collective-permute-done.30
  963.7 220.2 %while.355 = (s32[]{:T(128)}, f32[3,64,256]{2,1,0:T(8,128)S(1)}, f32[3,256]{1,0:T(4,128)S(1)}, f32[3,256,64]{1,2,0:T(8,128)S(1)}, f32[3,64]{1,0:T(4,128)S(1)}, /...) while((s32[]{:T(128)}, f32[3,64,256]{2,1,0:T(8,128)S(1)}, ...), condition=%wide.region_125.126_spmd.clone, body=%wide.region_107.125_spmd.sunk.clone | while | flops 168093488 | bytes 7610557 | solution.py:140
  1192.2 3.7 collective-permute-done.34
  1197.4 220.2 %while.356 = (s32[]{:T(128)}, f32[3,64,256]{2,1,0:T(8,128)S(1)}, f32[3,256]{1,0:T(4,128)S(1)}, f32[3,256,64]{1,2,0:T(8,128)S(1)}, f32[3,64]{1,0:T(4,128)S(1)}, /...) while((s32[]{:T(128)}, f32[3,64,256]{2,1,0:T(8,128)S(1)}, ...), condition=%wide.region_144.145_spmd.clone, body=%wide.region_126.144_spmd.sunk.clone | while | flops 168093488 | bytes 7610557 | solution.py:140
  1425.9 3.7 collective-permute-done.38
  1431.1 220.2 %while.357 = (s32[]{:T(128)}, f32[3,64,256]{2,1,0:T(8,128)S(1)}, f32[3,256]{1,0:T(4,128)S(1)}, f32[3,256,64]{1,2,0:T(8,128)S(1)}, f32[3,64]{1,0:T(4,128)S(1)}, /...) while((s32[]{:T(128)}, f32[3,64,256]{2,1,0:T(8,128)S(1)}, ...), condition=%wide.region_163.164_spmd.clone, body=%wide.region_145.163_spmd.sunk.clone | while | flops 168093488 | bytes 7610557 | solution.py:140
  1659.6 3.7 collective-permute-done.42
  1664.7 220.2 %while.358 = (s32[]{:T(128)}, f32[3,64,256]{2,1,0:T(8,128)S(1)}, f32[3,256]{1,0:T(4,128)S(1)}, f32[3,256,64]{1,2,0:T(8,128)S(1)}, f32[3,64]{1,0:T(4,128)S(1)}, /...) while((s32[]{:T(128)}, f32[3,64,256]{2,1,0:T(8,128)S(1)}, ...), condition=%wide.region_182.183_spmd.clone, body=%wide.region_164.182_spmd.sunk.clone | while | flops 168093488 | bytes 7610557 | solution.py:140
  1893.3 3.7 collective-permute-done.46
  1898.4 220.2 %while.359 = (s32[]{:T(128)}, f32[3,64,256]{2,1,0:T(8,128)S(1)}, f32[3,256]{1,0:T(4,128)S(1)}, f32[3,256,64]{1,2,0:T(8,128)S(1)}, f32[3,64]{1,0:T(4,128)S(1)}, /...) while((s32[]{:T(128)}, f32[3,64,256]{2,1,0:T(8,128)S(1)}, ...), condition=%wide.region_201.202_spmd.clone, body=%wide.region_183.201_spmd.sunk.clone | while | flops 168093488 | bytes 7610557 | solution.py:140
  2127.0 3.7 collective-permute-done.50
  2132.1 220.2 %while.360 = (s32[]{:T(128)}, f32[3,64,256]{2,1,0:T(8,128)S(1)}, f32[3,256]{1,0:T(4,128)S(1)}, f32[3,256,64]{1,2,0:T(8,128)S(1)}, f32[3,64]{1,0:T(4,128)S(1)}, /...) while((s32[]{:T(128)}, f32[3,64,256]{2,1,0:T(8,128)S(1)}, ...), condition=%wide.region_220.221_spmd.clone, body=%wide.region_202.220_spmd.sunk.clone | while | flops 168093488 | bytes 7610557 | solution.py:140
  2360.7 3.7 collective-permute-done.54
  2366.4 306.1 %while.362 = (s32[]{:T(128)}, f32[3,64]{1,0:T(4,128)}, f32[3,64]{1,0:T(4,128)}, f32[3,64,256]{2,1,0:T(8,128)S(1)}, f32[3,256]{1,0:T(4,128)S(1)}, /*index=5*/f32[...) while((s32[]{:T(128)}, f32[3,64]{1,0:T(4,128)}, ...), condition=%wide.region_246.247_spmd.clone.clone, body=%wide.region_221.246_spmd.clone.sunk.clone | while | flops 199153376 | bytes 8836864 | solution.py:140
  2692.9 6.5 psum.150
  2714.5 41.6 %all-reduce = (f32[192]{0:T(256)}, f32[768,3]{0,1:T(4,128)}, f32[3]{0:T(128)}, f32[3,64]{1,0:T(4,128)}, f32[3,64]{1,0:T(4,128)}, /*index=5*/f32[3,256]{1,0:T(4,1...) all-reduce(f32[192]{0:T(256)S(1)} %bitcast.1623, ...), channel_id=1, replica_groups=mesh['seq'=8,'head'=4] {'seq'}, use_global_device_ids=true, to_apply=%region_251.252 | all-reduce | flops 4995 | bytes 38424 | tf_op jit(solution)/shard_map/psum | solution.py:324
  2756.1 14.9 reduce-scatter.24.cloned.1.call-done
  2772.4 62.5 %reduce-scatter.22.cloned.1.call-done = bf16[96,192]{1,0:T(8,128)(2,1)} async-done(((bf16[768,192]{1,0:T(8,128)(2,1)}), bf16[96,192]{1,0:T(8,128)(2,1)}) %reduce-scatter.22.cloned.1.call-update) | async-done | bytes 36880 | tf_op jit(solution)/shard_map/reduce_scatter | solution.py:345
  2836.4 62.6 %reduce-scatter.20.cloned.1.call-done = bf16[96,192]{1,0:T(8,128)(2,1)} async-done(((bf16[768,192]{1,0:T(8,128)(2,1)}), bf16[96,192]{1,0:T(8,128)(2,1)}) %reduce-scatter.20.cloned.1.call-update) | async-done | bytes 36880 | tf_op jit(solution)/shard_map/reduce_scatter | solution.py:342
  2900.4 63.5 %reduce-scatter.40.cloned.1.call-done = bf16[96,512]{1,0:T(8,128)(2,1)} async-done(((bf16[768,512]{1,0:T(8,128)(2,1)}), bf16[96,512]{1,0:T(8,128)(2,1)}) %reduce-scatter.40.cloned.1.call-update) | async-done | bytes 98320
  2965.8 62.8 %reduce-scatter.32.cloned.1.call-done = bf16[96,512]{1,0:T(8,128)(2,1)} async-done(((bf16[768,512]{1,0:T(8,128)(2,1)}), bf16[96,512]{1,0:T(8,128)(2,1)}) %reduce-scatter.32.cloned.1.call-update) | async-done | bytes 98320 | tf_op jit(solution)/shard_map/reduce_scatter | solution.py:360
  3030.2 63.5 %reduce-scatter.30.cloned.1.call-done = bf16[96,512]{1,0:T(8,128)(2,1)} async-done(((bf16[768,512]{1,0:T(8,128)(2,1)}), bf16[96,512]{1,0:T(8,128)(2,1)}) %reduce-scatter.30.cloned.1.call-update) | async-done | bytes 98320 | tf_op jit(solution)/shard_map/reduce_scatter | solution.py:357
  3095.2 20.7 reduce-scatter.36.cloned.1.call-done
  3118.9 72.4 %all-reduce.12.cloned.1.call-done = (f32[3,64,256]{2,1,0:T(8,128)}, f32[3,256,64]{1,2,0:T(8,128)}) async-done(((f32[3,64,256]{2,1,0:T(8,128)}, f32[3,256,64]{1,2,0:T(8,128)}), (f32[3,64,256]{2,1,0:T(8,128)}, f32[3,256,64]{1,2,0:T(8,128)})) %all-reduce.12.cloned.1.call-update) | async-done | bytes 393232 | tf_op jit(solution)/shard_map/psum | solution.py:324
  (10408 shorter events, 2492.7 us)
Async XLA Ops:
  7.2 679.2 %all-reduce.8.cloned.1.call-start = ((), (), s32[]{:S(2)}) async-start(), calls=%async_computation.11 | async-start | bytes 1572864 | tf_op jit(solution)/shard_map/psum | solution.py:215
  59.5 13.8 collective-permute-start.3
  63.0 10.4 collective-permute-start.1
  66.4 8.5 collective-permute-start
  69.8 8.3 collective-permute-start.2
  114.7 16.7 collective-permute-start.7
  120.2 11.2 collective-permute-start.5
  124.5 6.9 collective-permute-start.4
  127.0 7.5 collective-permute-start.6
  171.7 21.1 collective-permute-start.11
  182.3 10.6 collective-permute-start.9
  187.1 7.2 collective-permute-start.8
  189.0 8.8 collective-permute-start.10
  245.1 13.3 collective-permute-start.15
  249.5 8.9 collective-permute-start.13
  253.9 7.3 collective-permute-start.12
  255.9 7.5 collective-permute-start.14
  310.6 12.9 collective-permute-start.19
  315.0 8.5 collective-permute-start.17
  318.1 6.7 collective-permute-start.16
  320.0 6.9 collective-permute-start.18
  374.2 14.2 collective-permute-start.23
  380.0 8.4 collective-permute-start.21
  438.7 16.7 collective-permute-start.27
  447.3 8.8 collective-permute-start.25
  598.3 126.8 %all-reduce.10.cloned.1.call-start = ((), (), s32[]{:S(2)}) async-start(), calls=%async_computation.12 | async-start | bytes 786432 | tf_op jit(solution)/shard_map/psum | solution.py:250
  693.5 2009.2 %reduce-scatter.34.cloned.1.call-start = ((), (), s32[]{:S(2)}) async-start(), calls=%async_computation.20 | async-start | bytes 491520
  695.7 2009.0 %reduce-scatter.28.cloned.1.call-start = ((), (), s32[]{:S(2)}) async-start(), calls=%async_computation.17 | async-start | bytes 442368 | tf_op jit(solution)/shard_map/reduce_scatter | solution.py:354
  740.1 1966.1 %reduce-scatter.26.cloned.1.call-start = ((), (), s32[]{:S(2)}) async-start(), calls=%async_computation.16 | async-start | bytes 442368 | tf_op jit(solution)/shard_map/reduce_scatter | solution.py:351
  950.0 6.5 collective-permute-start.31
  953.8 8.1 collective-permute-start.30
  955.1 8.6 collective-permute-start.28
  956.4 1757.1 %reduce-scatter.38.cloned.1.call-start = ((), (), s32[]{:S(2)}) async-start(), calls=%async_computation.22 | async-start | bytes 245760
  1183.9 6.4 collective-permute-start.35
  1185.2 7.0 collective-permute-start.33
  1186.6 9.4 collective-permute-start.34
  1187.9 9.5 collective-permute-start.32
  1417.6 6.4 collective-permute-start.39
  1418.9 7.0 collective-permute-start.37
  1420.3 9.4 collective-permute-start.38
  1421.6 9.5 collective-permute-start.36
  1651.3 6.4 collective-permute-start.43
  1652.6 7.0 collective-permute-start.41
  1654.0 9.3 collective-permute-start.42
  1655.2 9.5 collective-permute-start.40
  1885.0 6.4 collective-permute-start.47
  1886.3 7.0 collective-permute-start.45
  1887.6 9.4 collective-permute-start.46
  1888.9 9.5 collective-permute-start.44
  2118.7 6.4 collective-permute-start.51
  2120.0 7.0 collective-permute-start.49
  2121.3 9.4 collective-permute-start.50
  2122.6 9.5 collective-permute-start.48
  2353.7 7.0 collective-permute-start.53
  2355.0 9.3 collective-permute-start.54
  2356.3 9.5 collective-permute-start.52
  2681.4 89.6 %reduce-scatter.24.cloned.1.call-start = ((), (), s32[]{:S(2)}) async-start(), calls=%async_computation.15 | async-start | bytes 442368 | tf_op jit(solution)/shard_map/reduce_scatter | solution.py:348
  2683.5 151.4 %reduce-scatter.22.cloned.1.call-start = ((), (), s32[]{:S(2)}) async-start(), calls=%async_computation.14 | async-start | bytes 442368 | tf_op jit(solution)/shard_map/reduce_scatter | solution.py:345
  2684.7 214.2 %reduce-scatter.20.cloned.1.call-start = ((), (), s32[]{:S(2)}) async-start(), calls=%async_computation.13 | async-start | bytes 442368 | tf_op jit(solution)/shard_map/reduce_scatter | solution.py:342
  2686.7 277.2 %reduce-scatter.40.cloned.1.call-start = ((), (), s32[]{:S(2)}) async-start(), calls=%async_computation.23 | async-start | bytes 884736
  2690.5 338.1 %reduce-scatter.32.cloned.1.call-start = ((), (), s32[]{:S(2)}) async-start(), calls=%async_computation.19 | async-start | bytes 884736 | tf_op jit(solution)/shard_map/reduce_scatter | solution.py:360
  2692.8 400.8 %reduce-scatter.30.cloned.1.call-start = ((), (), s32[]{:S(2)}) async-start(), calls=%async_computation.18 | async-start | bytes 884736 | tf_op jit(solution)/shard_map/reduce_scatter | solution.py:357
  2701.6 414.4 %reduce-scatter.36.cloned.1.call-start = ((), (), s32[]{:S(2)}) async-start(), calls=%async_computation.21 | async-start | bytes 491520
  2710.3 481.0 %all-reduce.12.cloned.1.call-start = ((), (), s32[]{:S(2)}) async-start(), calls=%async_computation.24 | async-start | bytes 786432 | tf_op jit(solution)/shard_map/psum | solution.py:324
  (148 other events, 5128.0 us)
Sparse Core Ops, SparseCore 0:
  598.4 33.9 all-reduce.7
  693.6 31.4 all-reduce.9
  727.8 20.8 reduce-scatter.33
  752.1 61.5 reduce-scatter.27
  956.5 68.2 reduce-scatter.25
  2681.5 24.3 reduce-scatter.37
  2709.5 61.3 reduce-scatter.23
  2774.5 60.3 reduce-scatter.21
  2838.5 60.3 reduce-scatter.19
  2902.4 61.4 reduce-scatter.39
  2967.2 61.3 reduce-scatter.31
  3032.1 61.5 reduce-scatter.29
  3096.1 19.7 reduce-scatter.35
  3119.8 71.4 all-reduce.11
where the time goes:
time: 3240 us; the launch traced here: 3200 us
  matrix products  1300 us (40%)
  local copies, waits for them, and re-layouts  758 us (23%)
  waiting for transfers between devices  534 us (16%)
  other arithmetic  340 us (10%)
  starting transfers between devices  133 us (4%)
  blocking collectives  74 us (2%)
  loops' own time  45.2 us (1%)
    dot_general x3936, matrix products, mixing_contraction(): return jnp.einsum(form, left, right, precision=highest)  1240 us
    squeeze x512, local copies, waits for them, and re-layouts, run_block(): lax.scan(jax.checkpoint(advance), state_now, blocks)  418 us
    squeeze x384, local copies, waits for them, and re-layouts, run_states(): final_state, _ = lax.scan(advance, state_now, blocks)  179 us
    ppermute x56, starting transfers between devices, shifted(): return lax.ppermute(block, axis, route)  133 us
    unnamed x18, waiting for transfers between devices  84.5 us
    ppermute x56, waiting for transfers between devices, shifted(): return lax.ppermute(block, axis, route)  81.7 us
    psum x1, waiting for transfers between devices, local(): lax.psum((gain_one[0], gain_two, post_gain_term, post_bias_term, rate_wei...  72.4 us
    reduce_sum x416, other arithmetic, head_norm(): jnp.mean(centred * centred, axis=-1, keepdims=True) + eps_norm  67.2 us

commit v1 on v0

v1 whole, which is shorter than its diff:
```python
import functools

import jax
import jax.numpy as jnp
from jax import lax
from jax.experimental import pallas as pl
from jax.experimental.pallas import tpu as pltpu
from jax.sharding import PartitionSpec as P

MINI = 16
CHAIN = 8
FIRST = 2
AUG = 80
eps_norm = 1e-06
gelu_scale = 0.7978845608028654
f32 = jnp.float32
bf16 = jnp.bfloat16


def dot_nn(a, b):
    return lax.dot_general(a, b, (((1,), (0,)), ((), ())), preferred_element_type=f32)


def dot_nt(a, b):
    return lax.dot_general(a, b, (((1,), (1,)), ((), ())), preferred_element_type=f32)


def dot_tn(a, b):
    return lax.dot_general(a, b, (((0,), (0,)), ((), ())), preferred_element_type=f32)


def mean_row(x):
    return jnp.sum(x, axis=1, keepdims=True) * (1.0 / x.shape[1])


def gelu_first(z):
    sq = z * z
    th = jnp.tanh(gelu_scale * z * (1.0 + 0.044715 * sq))
    half = 0.5 * (1.0 + th)
    act = z * half
    der = half + (0.5 * gelu_scale) * z * (1.0 - th * th) * (1.0 + 0.134145 * sq)
    return act, der


def gelu_second(z):
    sq = z * z
    th = jnp.tanh(gelu_scale * z * (1.0 + 0.044715 * sq))
    half = 0.5 * (1.0 + th)
    act = z * half
    slope = gelu_scale * (1.0 + 0.134145 * sq)
    sech = 1.0 - th * th
    der = half + 0.5 * z * sech * slope
    curve = sech * (slope + z * (0.5 * gelu_scale * 0.26829 * z) - z * th * slope * slope)
    return act, der, curve


def tri_mask():
    rows = lax.broadcasted_iota(jnp.int32, (MINI, MINI), 0)
    cols = lax.broadcasted_iota(jnp.int32, (MINI, MINI), 1)
    return jnp.where(rows >= cols, 1.0, 0.0).astype(f32)


def inner_target_grad(z, base, gain_sq, rate):
    mz = mean_row(z)
    m_zz = mean_row(z * z)
    zg = z * gain_sq
    m_zg = mean_row(zg)
    m_zzg = mean_row(zg * z)
    m_zb = mean_row(z * base)
    m_b = mean_row(base)
    m_sq = mean_row(gain_sq)
    inv = lax.rsqrt(m_zz - mz * mz + eps_norm)
    c_zg = m_zg - mz * m_sq
    c_zzg = m_zzg - mz * (m_zg + c_zg)
    c_zb = m_zb - mz * m_b
    m_g = inv * c_zg + m_b
    m_gn = inv * (inv * c_zzg + c_zb)
    zc = z - mz
    n = zc * inv
    grad = inv * (n * (gain_sq - m_gn) + (base - m_g))
    return rate * grad, zc


def forward_step(state, z1, key_aug, key_next, query_aug, base, rate, gain, gain_sq, bias, tri):
    w1, w2t, b2 = state
    act, der = gelu_first(z1)
    act_h = act.astype(bf16)
    w1_h = w1.astype(bf16)
    w2_h = w2t.astype(bf16)
    s2, zc = inner_target_grad(dot_nt(act_h, w2_h) + b2, base, gain_sq, rate)
    s2_h = s2.astype(bf16)
    upd = dot_nn(s2_h, w2_h)
    s1_h = (upd * der).astype(bf16)
    both = jnp.concatenate([key_next, query_aug], axis=0)
    coef = dot_nt(both, key_aug)
    coef = jnp.concatenate([coef[:MINI], coef[MINI:] * tri], axis=0)
    zz = dot_nn(both, w1_h) - dot_nn(coef.astype(bf16), s1_h)
    z1_next = zz[:MINI]
    z1b = zz[MINI:]
    new_w1 = w1 - dot_tn(key_aug, s1_h)
    new_w2t = w2t - dot_tn(s2_h, act_h)
    new_b2 = b2 - jnp.sum(s2, axis=0, keepdims=True)
    actb, _ = gelu_first(z1b)
    actb_h = actb.astype(bf16)
    att = (dot_nt(actb_h, act_h) + 1.0) * tri
    z2b = dot_nt(actb_h, w2_h) + b2 - dot_nn(att.astype(bf16), s2_h)
    z2b = z2b - mean_row(z2b)
    invb = lax.rsqrt(mean_row(z2b * z2b) + eps_norm)
    out = z2b * invb * gain + bias
    return (new_w1, new_w2t, new_b2), z1_next, out, (w1_h, w2_h, upd, zc, s2, z1b, z2b)


def backward_step(carry, saved, d_out, key_aug, query_aug, target, rate, keep, gain, gain_sq, bias, tri):
    p1, p2t, p2 = carry
    w1_h, w2_h, z1, upd, zc, s2, z1b, z2b = saved
    act, der, curve = gelu_second(z1)
    act_h = act.astype(bf16)
    actb, derb = gelu_first(z1b)
    actb_h = actb.astype(bf16)
    s2_h = s2.astype(bf16)
    s1_h = (upd * der).astype(bf16)
    p1_h = p1.astype(bf16)
    p2_h = p2t.astype(bf16)
    invb = lax.rsqrt(mean_row(z2b * z2b) + eps_norm)
    nb = z2b * invb
    dn = d_out * gain
    d_z2b = invb * (dn - mean_row(dn) - nb * mean_row(dn * nb))
    d_z2b_h = d_z2b.astype(bf16)
    d_att2 = (-dot_nt(d_z2b_h, s2_h) * tri).astype(bf16)
    d_actb = dot_nn(d_z2b_h, w2_h) + dot_nn(d_att2, act_h)
    d_z1b_h = (d_actb * derb).astype(bf16)
    att2 = ((dot_nt(actb_h, act_h) + 1.0) * tri).astype(bf16)
    att1 = (dot_nt(query_aug, key_aug) * tri).astype(bf16)
    c2 = dot_tn(att2, d_z2b_h)
    c3 = dot_tn(d_att2, actb_h)
    c1 = dot_tn(att1, d_z1b_h)
    d_att1 = (-dot_nt(d_z1b_h, s1_h) * tri).astype(bf16)
    d_query = dot_nt(d_z1b_h, w1_h) + dot_nn(d_att1, key_aug)
    d_key = dot_tn(d_att1, query_aug)
    d_s1 = -c1 - dot_nn(key_aug, p1_h)
    d_upd = d_s1 * der
    d_upd_h = d_upd.astype(bf16)
    d_s2 = dot_nt(d_upd_h, w2_h) - c2 - dot_nt(act_h, p2_h) - p2
    h = rate * d_s2
    inv = lax.rsqrt(mean_row(zc * zc) + eps_norm)
    n = zc * inv
    base = (bias - target) * gain
    big_g = n * gain_sq + base
    m_g = mean_row(big_g)
    m_gn = mean_row(big_g * n)
    m_sq = mean_row(gain_sq)
    ng = n * gain_sq
    m_ng = mean_row(ng)
    m_nng = mean_row(n * ng)
    g = inv * (big_g - m_g - n * m_gn)
    a1 = mean_row(h)
    a2 = mean_row(h * n)
    a3 = mean_row(h * gain_sq)
    a4 = mean_row(h * ng)
    a5 = mean_row(h * g)
    proj = h - a1 - n * a2
    d_g = inv * proj
    dnn = inv * (proj * gain_sq - h * m_gn - big_g * a2)
    m_dn = inv * (a3 - a1 * (m_sq + m_gn) - a2 * (m_ng + m_g))
    m_dnn = inv * (a4 - a1 * m_ng - a2 * (m_nng + 2.0 * m_gn))
    d_zc = inv * (dnn - m_dn - n * (m_dnn + a5))
    d_zc_h = d_zc.astype(bf16)
    d_act = dot_nn(d_zc_h, w2_h) + c3 - dot_nn(s2_h, p2_h)
    d_z1 = d_act * der + d_s1 * upd * curve
    d_z1_h = d_z1.astype(bf16)
    d_gg = d_g * gain
    d_key = d_key + dot_nt(d_z1_h, w1_h) - dot_nt(s1_h, p1_h)
    d_key = d_key[:, : gain.shape[1]] + d_gg
    d_query = d_query[:, : gain.shape[1]] + d_out
    d_value = -d_gg
    d_logit = keep * jnp.sum(d_s2 * s2, axis=1, keepdims=True)
    new_p1 = p1 + dot_tn(
        jnp.concatenate([key_aug, query_aug], axis=0), jnp.concatenate([d_z1_h, d_z1b_h], axis=0)
    )
    new_p2t = p2t + dot_tn(
        jnp.concatenate([s2_h, d_zc_h, d_z2b_h], axis=0),
        jnp.concatenate([d_upd_h, act_h, actb_h], axis=0),
    )
    new_p2 = p2 + jnp.sum(d_zc + d_z2b, axis=0, keepdims=True)
    d_bias = jnp.sum(d_out + d_gg, axis=0, keepdims=True)
    d_gain = jnp.sum(d_out * nb + d_g * (2.0 * n * gain + bias - target), axis=0, keepdims=True)
    return (new_p1, new_p2t, new_p2), (d_query, d_key, d_value, d_logit), d_gain, d_bias


def fwd_kernel(block, unroll, q_ref, k_ref, base_ref, rate_ref, w1_in, w2t_in, b2_in, gain_ref, bias_ref,
               out_ref, w1s_ref, w2s_ref, z1s_ref, upd_ref, zc_ref, s2_ref, z1b_ref, z2b_ref,
               w1, w2t, b2, z1):
    blk = pl.program_id(0)
    gain = gain_ref[...]
    bias = bias_ref[...]
    gain_sq = gain * gain
    tri = tri_mask()
    width = gain.shape[1]

    @pl.when(blk == 0)
    def _():
        w1[...] = w1_in[...]
        w2t[...] = w2t_in[...]
        b2[...] = b2_in[...]
        z1[...] = dot_nn(k_ref[0:MINI, :], w1_in[...].astype(bf16))

    def group(it, _):
        for u in range(unroll):
            loc = it * unroll + u
            row = pl.multiple_of(blk * block + loc * MINI, MINI)
            lrow = pl.multiple_of(loc * MINI, MINI)
            rows = pl.ds(row, MINI)
            lrows = pl.ds(lrow, MINI)
            q_aug = q_ref[rows, :]
            z1_now = z1[...]
            state, z1_next, out, saved = forward_step(
                (w1[...], w2t[...], b2[...]), z1_now, k_ref[rows, :], k_ref[pl.ds(row + MINI, MINI), :], q_aug,
                base_ref[rows, :], rate_ref[rows, :], gain, gain_sq, bias, tri)
            w1[...], w2t[...], b2[...] = state
            z1[...] = z1_next
            out_ref[lrows, :] = out + q_aug[:, :width].astype(f32)
            w1_h, w2_h, upd, zc, s2, z1b, z2b = saved
            w1s_ref[loc] = w1_h
            w2s_ref[loc] = w2_h
            z1s_ref[lrows, :] = z1_now
            upd_ref[lrows, :] = upd
            zc_ref[lrows, :] = zc
            s2_ref[lrows, :] = s2
            z1b_ref[lrows, :] = z1b
            z2b_ref[lrows, :] = z2b
        return 0

    lax.fori_loop(0, block // MINI // unroll, group, 0)


def chain_forward(q_aug, k_aug, base, rate, w1, w2t, b2, gain, bias, block=128, unroll=8):
    tokens = q_aug.shape[0]
    hidden = w1.shape[1]
    width = gain.shape[1]
    steps = tokens // MINI
    whole = lambda a: pl.BlockSpec(a.shape, lambda i: (0,) * a.ndim, pipeline_mode=pl.Buffered(1))
    rowblk = lambda w: pl.BlockSpec((block, w), lambda i: (i, 0))
    nb = block // MINI
    ins = (q_aug, k_aug, base, rate, w1, w2t, b2, gain, bias)
    return pl.pallas_call(
        functools.partial(fwd_kernel, block, unroll),
        grid=(tokens // block,),
        in_specs=[whole(a) for a in ins],
        out_specs=[rowblk(width),
                   pl.BlockSpec((nb, AUG, hidden), lambda i: (i, 0, 0)),
                   pl.BlockSpec((nb, width, hidden), lambda i: (i, 0, 0)),
                   rowblk(hidden), rowblk(hidden), rowblk(width), rowblk(width), rowblk(hidden), rowblk(width)],
        out_shape=[jax.ShapeDtypeStruct((tokens, width), f32),
                   jax.ShapeDtypeStruct((steps, AUG, hidden), bf16),
                   jax.ShapeDtypeStruct((steps, width, hidden), bf16),
                   jax.ShapeDtypeStruct((tokens, hidden), f32),
                   jax.ShapeDtypeStruct((tokens, hidden), f32),
                   jax.ShapeDtypeStruct((tokens, width), f32),
                   jax.ShapeDtypeStruct((tokens, width), f32),
                   jax.ShapeDtypeStruct((tokens, hidden), f32),
                   jax.ShapeDtypeStruct((tokens, width), f32)],
        scratch_shapes=[pltpu.VMEM((AUG, hidden), f32), pltpu.VMEM((width, hidden), f32),
                        pltpu.VMEM((1, width), f32), pltpu.VMEM((MINI, hidden), f32)],
        name="inner_forward",
    )(*ins)


def bwd_kernel(block, unroll, dout_ref, q_ref, k_ref, target_ref, rate_ref, keep_ref, gain_ref, bias_ref,
               w1s_ref, w2s_ref, z1s_ref, upd_ref, zc_ref, s2_ref, z1b_ref, z2b_ref,
               dq_ref, dk_ref, dv_ref, dl_ref, p1_out, p2t_out, p2_out, dg_out, db_out,
               p1, p2t, p2, dg, db):
    pid = pl.program_id(0)
    blk = pl.num_programs(0) - 1 - pid
    gain = gain_ref[...]
    bias = bias_ref[...]
    gain_sq = gain * gain
    tri = tri_mask()

    @pl.when(pid == 0)
    def _():
        for r in (p1, p2t, p2, dg, db):
            r[...] = jnp.zeros_like(r)

    count = block // MINI

    def group(it, _):
        for u in range(unroll):
            loc = count - 1 - (it * unroll + u)
            row = pl.multiple_of(blk * block + loc * MINI, MINI)
            lrow = pl.multiple_of(loc * MINI, MINI)
            rows = pl.ds(row, MINI)
            lr = pl.ds(lrow, MINI)
            saved = (w1s_ref[loc], w2s_ref[loc], z1s_ref[lr, :], upd_ref[lr, :], zc_ref[lr, :], s2_ref[lr, :],
                     z1b_ref[lr, :], z2b_ref[lr, :])
            carry, outs, dgn, dbn = backward_step(
                (p1[...], p2t[...], p2[...]), saved, dout_ref[rows, :].astype(f32), k_ref[rows, :], q_ref[rows, :],
                target_ref[rows, :], rate_ref[rows, :], keep_ref[rows, :], gain, gain_sq, bias, tri)
            p1[...], p2t[...], p2[...] = carry
            dg[...] += dgn
            db[...] += dbn
            dq_ref[lr, :], dk_ref[lr, :], dv_ref[lr, :] = (o.astype(bf16) for o in outs[:3])
            dl_ref[lr, :] = outs[3]
        return 0

    lax.fori_loop(0, count // unroll, group, 0)

    @pl.when(pid == pl.num_programs(0) - 1)
    def _():
        for o, r in zip((p1_out, p2t_out, p2_out, dg_out, db_out), (p1, p2t, p2, dg, db)):
            o[...] = r[...]


def chain_backward(dout, q_aug, k_aug, target, rate, keep, gain, bias, saved, block=128, unroll=4):
    tokens = q_aug.shape[0]
    width = gain.shape[1]
    hidden = saved[2].shape[1]
    steps = tokens // MINI
    nblk = tokens // block
    whole = lambda a: pl.BlockSpec(a.shape, lambda i: (0,) * a.ndim, pipeline_mode=pl.Buffered(1))
    rowblk = lambda w: pl.BlockSpec((block, w), lambda i: (nblk - 1 - i, 0))
    nb = block // MINI
    ins = (dout, q_aug, k_aug, target, rate, keep, gain, bias)
    acc = [(AUG, hidden), (width, hidden), (1, width), (1, width), (1, width)]
    return pl.pallas_call(
        functools.partial(bwd_kernel, block, unroll),
        grid=(nblk,),
        in_specs=[whole(a) for a in ins]
        + [pl.BlockSpec((nb, AUG, hidden), lambda i: (nblk - 1 - i, 0, 0)),
           pl.BlockSpec((nb, width, hidden), lambda i: (nblk - 1 - i, 0, 0)),
           rowblk(hidden), rowblk(hidden), rowblk(width), rowblk(width), rowblk(hidden), rowblk(width)],
        out_specs=[rowblk(width), rowblk(width), rowblk(width), rowblk(1)]
        + [pl.BlockSpec(s, lambda i: (0, 0)) for s in acc],
        out_shape=[jax.ShapeDtypeStruct((tokens, width), bf16)] * 3 + [jax.ShapeDtypeStruct((tokens, 1), f32)]
        + [jax.ShapeDtypeStruct(s, f32) for s in acc],
        scratch_shapes=[pltpu.VMEM(s, f32) for s in acc],
        name="inner_backward",
    )(*ins, *saved)


def groups_of(axis):
    count = lax.axis_size(axis)
    if count == CHAIN:
        return None
    return [list(range(start, start + CHAIN)) for start in range(0, count, CHAIN)]


def gelu_tanh(arg_value):
    cubic = arg_value + 0.044715 * arg_value * arg_value * arg_value
    return 0.5 * arg_value * (1.0 + jnp.tanh(gelu_scale * cubic))


def gelu_derivative(arg_value):
    tangent = jnp.tanh(gelu_scale * (arg_value + 0.044715 * arg_value * arg_value * arg_value))
    return 0.5 * (1.0 + tangent) + 0.5 * arg_value * (1.0 - tangent * tangent) * gelu_scale * (
        1.0 + 0.134145 * arg_value * arg_value
    )


def bf_product(form, left, right):
    return jnp.einsum(form, left, right, preferred_element_type=f32)


def to_owners(parts):
    heads, rows, width = parts.shape
    padded = jnp.pad(parts, ((FIRST, CHAIN - FIRST - heads), (0, 0), (0, 0)))
    got = lax.all_to_all(padded, "seq", 0, 0, axis_index_groups=groups_of("seq"), tiled=True)
    return got.reshape(CHAIN * rows, width)


def from_owners(rows_of_head, heads):
    total, width = rows_of_head.shape
    got = lax.all_to_all(
        rows_of_head.reshape(CHAIN, total // CHAIN, width), "seq", 0, 0,
        axis_index_groups=groups_of("seq"), tiled=True)
    return got[FIRST : FIRST + heads]


def local(
    inputs,
    pre_gain,
    w_query,
    w_key,
    w_value,
    mix_gate,
    w_rate,
    rate_bias,
    inner_gain,
    inner_bias,
    init_w_one,
    init_b_one,
    init_w_two,
    init_b_two,
    post_gain,
    post_bias,
    w_out,
    ffn_gain,
    w_gate,
    w_up,
    w_down,
    cotangent,
):
    full_width = pre_gain.shape[0]
    rows, local_cols = inputs.shape
    heads, head_dim = inner_gain.shape
    head_index = lax.axis_index("head")
    position = lax.axis_index("seq") % CHAIN
    mine = jnp.clip(position - FIRST, 0, heads - 1)
    is_owner = (position >= FIRST) & (position < FIRST + heads)
    whole_in = lax.all_gather(inputs, "head", axis=1, tiled=True).astype(f32)
    grad_whole = lax.all_gather(cotangent, "head", axis=1, tiled=True)
    rms_one = lax.rsqrt(jnp.mean(whole_in * whole_in, axis=1, keepdims=True) + eps_norm)
    normed_one = (whole_in * rms_one * pre_gain).astype(bf16)
    queries = bf_product("rd,dc->rc", normed_one, w_query).astype(bf16)
    keys_in = bf_product("rd,dc->rc", normed_one, w_key).astype(bf16)
    values_in = bf_product("rd,dc->rc", normed_one, w_value).astype(bf16)
    gate_pre = bf_product("rd,dc->rc", normed_one, mix_gate)
    logits = bf_product("rd,dc->rc", normed_one, w_rate) + rate_bias

    def split_heads(block):
        return block.reshape(rows, heads, -1).transpose(1, 0, 2)

    logit_high = lax.reduce_precision(logits, 8, 7)
    logit_low = (logits - logit_high).astype(bf16)
    payload = jnp.concatenate(
        [split_heads(block) for block in (queries, keys_in, values_in)]
        + [split_heads(logit_high.astype(bf16)), split_heads(logit_low)], axis=2)
    got = to_owners(payload)
    query_h = got[:, :head_dim]
    key_h = got[:, head_dim : 2 * head_dim]
    value_h = got[:, 2 * head_dim : 3 * head_dim]
    logit_h = got[:, 3 * head_dim : 3 * head_dim + 1].astype(f32) + got[:, 3 * head_dim + 1 :].astype(f32)
    total = query_h.shape[0]

    def augment(block):
        lane = lax.broadcasted_iota(jnp.int32, (block.shape[0], AUG), 1)
        wide = jnp.pad(block, ((0, 0), (0, AUG - head_dim)))
        return jnp.where(lane == head_dim, jnp.ones_like(wide), wide)

    query_aug = augment(query_h)
    key_aug = augment(jnp.pad(key_h, ((0, MINI), (0, 0))))
    gain_h = lax.dynamic_slice_in_dim(inner_gain, mine, 1, 0)
    bias_h = lax.dynamic_slice_in_dim(inner_bias, mine, 1, 0)
    target = value_h.astype(f32) - key_h.astype(f32)
    base = (bias_h - target) * gain_h
    sig = jax.nn.sigmoid(logit_h)
    rate = sig / head_dim
    keep = 1.0 - sig
    start_one = jnp.pad(
        jnp.concatenate(
            [lax.dynamic_index_in_dim(init_w_one, mine, 0, False), lax.dynamic_slice_in_dim(init_b_one, mine, 1, 0)], 0),
        ((0, AUG - head_dim - 1), (0, 0)))
    start_two = lax.dynamic_index_in_dim(init_w_two, mine, 0, False).T
    start_two = start_two - jnp.mean(start_two, axis=0, keepdims=True)
    start_b_two = lax.dynamic_slice_in_dim(init_b_two, mine, 1, 0)
    start_b_two = start_b_two - jnp.mean(start_b_two)
    mixed_h, *saved = chain_forward(
        query_aug, key_aug, base, rate, start_one, start_two, start_b_two, gain_h, bias_h)
    mixed = from_owners(mixed_h, heads).transpose(1, 0, 2).reshape(rows, local_cols).astype(f32)
    totals = lax.psum((jnp.sum(mixed, axis=1), jnp.sum(mixed * mixed, axis=1)), "head")
    mean_z = totals[0][:, None] / full_width
    var_z = totals[1][:, None] / full_width - mean_z * mean_z
    inv_z = lax.rsqrt(var_z + eps_norm)
    z_hat = (mixed - mean_z) * inv_z
    post_out = z_hat * post_gain + post_bias
    gate_act = gelu_tanh(gate_pre)
    gated_low = (post_out * gate_act).astype(bf16)
    out_whole = lax.psum(bf_product("rc,cd->rd", gated_low, w_out), "head")
    resid = whole_in + out_whole
    rms_two = lax.rsqrt(jnp.mean(resid * resid, axis=1, keepdims=True) + eps_norm)
    normed_two = (resid * rms_two * ffn_gain).astype(bf16)
    gate_val = bf_product("rd,df->rf", normed_two, w_gate)
    up_val = bf_product("rd,df->rf", normed_two, w_up)
    silu_gate = jax.nn.silu(gate_val)
    hidden_ffn = (silu_gate * up_val).astype(bf16)
    down_local = lax.psum_scatter(
        bf_product("rf,fd->rd", hidden_ffn, w_down).astype(bf16), "head", scatter_dimension=1, tiled=True
    ).astype(f32)
    resid_local = lax.dynamic_slice_in_dim(resid, head_index * local_cols, local_cols, 1)
    outputs = resid_local + down_local
    grad_down_t = bf_product("rd,rf->df", grad_whole, hidden_ffn)
    grad_hidden = bf_product("rd,fd->rf", grad_whole, w_down)
    sig_gate = jax.nn.sigmoid(gate_val)
    grad_gate_val = (grad_hidden * up_val * sig_gate * (1.0 + gate_val * (1.0 - sig_gate))).astype(bf16)
    grad_up_val = (grad_hidden * silu_gate).astype(bf16)
    gate_term = bf_product("rd,rf->df", normed_two, grad_gate_val)
    up_term = bf_product("rd,rf->df", normed_two, grad_up_val)
    grad_normed_two = bf_product("rf,df->rd", grad_gate_val, w_gate) + bf_product(
        "rf,df->rd", grad_up_val, w_up
    )
    scaled_two = grad_normed_two * ffn_gain
    resid_back = rms_two * (
        scaled_two - resid * rms_two * rms_two * jnp.mean(scaled_two * resid, axis=1, keepdims=True)
    )
    gain_two_term = jnp.sum(grad_normed_two * resid * rms_two, axis=0)
    resid_sum = lax.psum(resid_back.astype(bf16), "head").astype(f32)
    grad_resid = grad_whole.astype(f32) + resid_sum
    grad_out_val = grad_resid.astype(bf16)
    grad_out_t = bf_product("rd,rc->dc", grad_out_val, gated_low)
    grad_gated = bf_product("rd,cd->rc", grad_out_val, w_out)
    grad_post = grad_gated * gate_act
    grad_gate_pre = (grad_gated * post_out * gelu_derivative(gate_pre)).astype(bf16)
    post_gain_term = jnp.sum(grad_post * z_hat, axis=0)
    post_bias_term = jnp.sum(grad_post, axis=0)
    grad_zhat = grad_post * post_gain
    sums_back = lax.psum((jnp.sum(grad_zhat, axis=1), jnp.sum(grad_zhat * z_hat, axis=1)), "head")
    grad_mixed = inv_z * (
        grad_zhat - sums_back[0][:, None] / full_width - z_hat * sums_back[1][:, None] / full_width
    )
    mixgate_term = bf_product("rd,rc->dc", normed_one, grad_gate_pre)
    early = jnp.concatenate(
        [block.astype(bf16) for block in (mixgate_term, grad_out_t, gate_term, up_term, grad_down_t)], axis=1)
    early_sum = lax.psum_scatter(early, "seq", scatter_dimension=0, tiled=True).astype(f32)
    grad_mixed_h = to_owners(split_heads(grad_mixed.astype(bf16)))
    dq_h, dk_h, dv_h, dl_h, end_one, end_two, end_b_two, end_gain, end_bias = chain_backward(
        grad_mixed_h, query_aug, key_aug, target, rate, keep, gain_h, bias_h, saved)
    dl_high = lax.reduce_precision(dl_h, 8, 7)
    back = from_owners(
        jnp.concatenate([dq_h, dk_h, dv_h, dl_high.astype(bf16), (dl_h - dl_high).astype(bf16)], axis=1), heads)

    def join_heads(lo, hi):
        return back[:, :, lo:hi].transpose(1, 0, 2).reshape(rows, -1)

    grad_q_low = join_heads(0, head_dim)
    grad_k_low = join_heads(head_dim, 2 * head_dim)
    grad_v_low = join_heads(2 * head_dim, 3 * head_dim)
    grad_logits = join_heads(3 * head_dim, 3 * head_dim + 1).astype(f32) + join_heads(
        3 * head_dim + 1, 3 * head_dim + 2).astype(f32)
    rate_bias_term = jnp.sum(grad_logits, axis=0)
    grad_logit_low = grad_logits.astype(bf16)
    query_term = bf_product("rd,rc->dc", normed_one, grad_q_low)
    key_term = bf_product("rd,rc->dc", normed_one, grad_k_low)
    value_term = bf_product("rd,rc->dc", normed_one, grad_v_low)
    rate_weight_term = bf_product("rd,rc->dc", normed_one, grad_logit_low)
    grad_normed_one = (
        bf_product("rc,dc->rd", grad_q_low, w_query)
        + bf_product("rc,dc->rd", grad_k_low, w_key)
        + bf_product("rc,dc->rd", grad_v_low, w_value)
        + bf_product("rc,dc->rd", grad_gate_pre, mix_gate)
        + bf_product("rc,dc->rd", grad_logit_low, w_rate)
    )
    scaled_one = grad_normed_one * pre_gain
    input_back = rms_one * (
        scaled_one
        - whole_in * rms_one * rms_one * jnp.mean(scaled_one * whole_in, axis=1, keepdims=True)
    )
    gain_one_term = jnp.sum(grad_normed_one * whole_in * rms_one, axis=0)
    input_local = lax.psum_scatter(
        input_back.astype(bf16), "head", scatter_dimension=1, tiled=True).astype(f32)
    grad_inputs = (
        lax.dynamic_slice_in_dim(grad_resid, head_index * local_cols, local_cols, 1) + input_local
    )
    late = jnp.concatenate([block.astype(bf16) for block in (query_term, key_term, value_term)], axis=1)
    late_sum = lax.psum_scatter(late, "seq", scatter_dimension=0, tiled=True).astype(f32)

    def place(part):
        slot = lax.broadcasted_iota(jnp.int32, (heads,) + part.shape, 0)
        return jnp.where((slot == mine) & is_owner, part[None], 0.0)

    end_one_w = place(end_one[:head_dim])
    end_two_w = place((end_two - jnp.mean(end_two, axis=0, keepdims=True)).T)
    hidden = end_one.shape[1]
    flat = jnp.concatenate(
        [end_one_w.reshape(-1), end_two_w.reshape(-1), place(end_one[head_dim]).reshape(-1),
         place(end_b_two[0] - jnp.mean(end_b_two)).reshape(-1), place(end_gain[0]).reshape(-1),
         place(end_bias[0]).reshape(-1), post_gain_term, post_bias_term, rate_weight_term.reshape(-1),
         rate_bias_term])
    flat = lax.psum(flat, "seq")
    at = 0

    def take(shape):
        nonlocal at
        size = 1
        for extent in shape:
            size *= extent
        at += size
        return flat[at - size : at].reshape(shape)

    grad_one = take((heads, head_dim, hidden))
    grad_two = take((heads, hidden, head_dim))
    grad_b_one = take((heads, hidden))
    grad_b_two = take((heads, head_dim))
    grad_gain = take((heads, head_dim))
    grad_bias = take((heads, head_dim))
    grad_post_gain = take((local_cols,))
    grad_post_bias = take((local_cols,))
    grad_rate_w = take((full_width, heads))
    grad_rate_b = take((heads,))
    gain_both = lax.psum(jnp.concatenate([gain_one_term, gain_two_term]), ("seq", "head"))
    gain_one = lax.dynamic_slice_in_dim(gain_both, head_index * local_cols, local_cols, 0)
    gain_two = gain_both[full_width:]
    ffn = gate_term.shape[1]
    return (
        outputs,
        grad_inputs,
        gain_one,
        late_sum[:, :local_cols],
        late_sum[:, local_cols : 2 * local_cols],
        late_sum[:, 2 * local_cols :],
        early_sum[:, :local_cols],
        grad_rate_w,
        grad_rate_b,
        grad_gain,
        grad_bias,
        grad_one,
        grad_b_one,
        grad_two,
        grad_b_two,
        grad_post_gain,
        grad_post_bias,
        early_sum[:, local_cols : 2 * local_cols].T,
        gain_two,
        early_sum[:, 2 * local_cols : 2 * local_cols + ffn],
        early_sum[:, 2 * local_cols + ffn : 2 * local_cols + 2 * ffn],
        early_sum[:, 2 * local_cols + 2 * ffn :].T,
    )


def solution(mesh):
    in_specs = (
        P("seq", "head"),
        P(),
        P(None, "head"),
        P(None, "head"),
        P(None, "head"),
        P(None, "head"),
        P(None, "head"),
        P("head"),
        P("head", None),
        P("head", None),
        P("head", None, None),
        P("head", None),
        P("head", None, None),
        P("head", None),
        P("head"),
        P("head"),
        P("head", None),
        P(),
        P(None, "head"),
        P(None, "head"),
        P("head", None),
        P("seq", "head"),
    )
    out_specs = (
        P("seq", "head"),
        P("seq", "head"),
        P("head"),
        P("seq", "head"),
        P("seq", "head"),
        P("seq", "head"),
        P("seq", "head"),
        P(None, "head"),
        P("head"),
        P("head", None),
        P("head", None),
        P("head", None, None),
        P("head", None),
        P("head", None, None),
        P("head", None),
        P("head"),
        P("head"),
        P("head", "seq"),
        P(),
        P("seq", "head"),
        P("seq", "head"),
        P("head", "seq"),
    )
    return jax.shard_map(local, mesh=mesh, in_specs=in_specs, out_specs=out_specs, check_vma=False)
```

time: 3240 us -> 673 us (0.21); the launches traced: 3200 us -> 671 us
  matrix products: 1300 us -> 28.6 us
  local copies, waits for them, and re-layouts: 758 us -> 55.6 us
  other arithmetic: 340 us -> 15.4 us
  waiting for transfers between devices: 534 us -> 261 us
  Pallas kernels: 0 us -> 197 us
  starting transfers between devices: 133 us -> 15.5 us
  loops' own time: 45.2 us -> 0 us
    dot_general x4139 -> x27, matrix products: 1300 us -> 28.6 us  [bf_product(): return jnp.einsum(form, left, right, preferred_element_type=f32)]
    squeeze x896 -> x1, local copies, waits for them, and re-layouts: 597 us -> 0.85 us  [local(): lax.dynamic_index_in_dim(init_w_one, mine, 0, False)]
    reduce_scatter x7 -> x0, waiting for transfers between devices: 266 us -> none  [the longest x1 63.5 us: local(): lax.psum_scatter(gate_term.astype(jnp.bfloat16), 'seq', scatter_dimension...]
    reduce_sum x1489 -> x5, other arithmetic: 231 us -> 1.31 us  [the longest x1 0.6 us: local(): start_b_two = start_b_two - jnp.mean(start_b_two)]
    pallas_call x0 -> x2, Pallas kernels: none -> 197 us  [the longest x1 124 us: chain_backward(): pl.pallas_call(functools.partial(bwd_kernel, block, unroll), grid=(nblk,)...]
    ppermute x56 -> x0, starting transfers between devices: 133 us -> none  [shifted(): return lax.ppermute(block, axis, route)]
    ppermute x56 -> x0, waiting for transfers between devices: 81.7 us -> none  [shifted(): return lax.ppermute(block, axis, route)]
    mul x145 -> x0, local copies, waits for them, and re-layouts: 67.3 us -> none  [the longest x144 66.3 us: inner_update(): first_update_step = rate_mb[:, :, None] * first_gradient]
where the time goes in v1:
time: 673 us; the launch traced here: 671 us
  waiting for transfers between devices  261 us (39%)
  Pallas kernels  197 us (29%)
  blocking collectives  81.9 us (12%)
  local copies, waits for them, and re-layouts  55.6 us (8%)
  matrix products  28.6 us (4%)
  between operations  16.3 us (2%)
  starting transfers between devices  15.5 us (2%)
  other arithmetic  15.4 us (2%)
    unnamed x11, waiting for transfers between devices  149 us
    pallas_call x1, Pallas kernels, chain_backward(): pl.pallas_call(functools.partial(bwd_kernel, block, unroll), grid=(nblk,)...  124 us
    pallas_call x1, Pallas kernels, chain_forward(): pl.pallas_call(functools.partial(fwd_kernel, block, unroll), grid=(tokens...  73 us
    psum x1, blocking collectives, local(): lax.psum(jnp.concatenate([gain_one_term, gain_two_term]), ('seq', 'head'))  37.9 us
    psum x1, waiting for transfers between devices, local(): resid_sum = lax.psum(resid_back.astype(bf16), 'head').astype(f32)  32.6 us
    dot_general x27, matrix products, bf_product(): return jnp.einsum(form, left, right, preferred_element_type=f32)  28.6 us
    psum x1, waiting for transfers between devices, local(): out_whole = lax.psum(bf_product('rc,cd->rd', gated_low, w_out), 'head')  27.3 us
    all_to_all x2, waiting for transfers between devices, to_owners(): lax.all_to_all(padded, 'seq', 0, 0, axis_index_groups=groups_of('seq'), t...  23.3 us
  transfers between devices with their start and end apart: 10, of which 9 were waited for; matrix products, arithmetic and copies ran while one was open for 10% of the time, Pallas kernels for 18%

profile of v1, /device:TPU:0, one launch (start us, length us, event | category | flops | bytes accessed | tf_op | source)
XLA Modules:
  0.0 671.0 jit_solution(11515902922506826850)
XLA Ops:
  7.2 8.2 %all_gather.6 = bf16[256,768]{0,1:T(8,128)(2,1)S(1)} all-gather(bf16[256,192]{0,1:T(8,128)(2,1)} %param.22), channel_id=1, replica_groups=mesh['seq'=8,'head'=4] {'head'}, dimensions={1}, use_global_device_ids=true | all-gather | bytes 491520 | tf_op jit(solution)/shard_map/all_gather | solution.py:409
  15.8 1.0 fusion.37
  16.9 1.3 convolution_convert_fusion.10
  19.1 1.0 pad.24
  20.1 5.8 all-to-all-start
  29.2 0.8 dynamic-slice_bitcast_fusion
  31.3 15.9 %all-to-all-done = bf16[8,256,194]{1,2,0:T(8,128)(2,1)S(1)} async-done(((bf16[8,256,194]{1,2,0:T(8,128)(2,1)}), bf16[8,256,194]{1,2,0:T(8,128)(2,1)S(1)}, u32[]{:S(2)}, u32[]{:S(2)}) %all-to-all-start) | async-done | bytes 794656 | tf_op jit(solution)/shard_map/all_to_all | solution.py:366
  48.0 1.7 broadcast_subtract_fusion
  49.7 0.9 fusion.19.q_ref
  50.7 0.9 pad_select_fusion.k_ref
  51.6 1.6 convert_subtract_fusion
  53.2 73.0 %inner_forward.1 = (f32[2048,64]{1,0:T(8,128)}, bf16[128,80,256]{2,1,0:T(8,128)(2,1)}, bf16[128,64,256]{2,1,0:T(8,128)(2,1)}, f32[2048,256]{1,0:T(8,128)}, f32[2...) custom-call(bf16[2048,80]{1,0:T(8,128)(2,1)} %fusion.19.q_ref, ...), custom_call_target="tpu_custom_call" | custom-call | tf_op jit(solution)/shard_map/inner_forward/pallas_call | solution.py:245
  126.2 1.6 copy.116
  127.8 18.2 %all_to_all.20 = f32[8,256,64]{1,2,0:T(8,128)S(1)} all-to-all(f32[8,256,64]{1,2,0:T(8,128)S(1)} %copy.116), channel_id=1, replica_groups=mesh['seq'=8,'head'=4] {'seq'}, dimensions={0} | all-to-all | bytes 1048576 | tf_op jit(solution)/shard_map/all_to_all | solution.py:372
  146.2 5.7 all-reduce.6
  151.9 1.1 multiply_convert_fusion.6
  153.0 1.2 fusion.68
  154.3 6.2 all_gather.7
  160.4 27.3 %all-reduce.11.cloned.1.call-done = f32[256,768]{1,0:T(8,128)} async-done(((f32[256,768]{1,0:T(8,128)}), f32[256,768]{1,0:T(8,128)}) %all-reduce.11.cloned.1.call-update) | async-done | bytes 786448 | tf_op jit(solution)/shard_map/psum | solution.py:467
  187.8 1.3 multiply_reduce_fusion.2
  189.2 1.5 fusion.70
  190.8 1.6 fusion.69
  194.1 1.0 multiply_convert_fusion
  195.3 32.6 %all-reduce.13.cloned.1.call-done = bf16[256,768]{1,0:T(8,128)(2,1)} async-done(((bf16[256,768]{1,0:T(8,128)(2,1)}), bf16[256,768]{1,0:T(8,128)(2,1)}) %all-reduce.13.cloned.1.call-update) | async-done | bytes 393232 | tf_op jit(solution)/shard_map/psum | solution.py:495
  227.9 2.3 multiply_reduce_fusion.3
  230.2 5.7 all-reduce.5
  235.9 1.0 multiply_convert_fusion.5
  237.7 5.6 all-to-all-start.2
  243.4 1.2 fusion.6
  244.7 7.4 %all-to-all-done.2 = bf16[8,256,64]{1,2,0:T(8,128)(2,1)S(1)} async-done(((bf16[8,256,64]{1,2,0:T(8,128)(2,1)}), bf16[8,256,64]{1,2,0:T(8,128)(2,1)S(1)}, u32[]{:S(2)}, u32[]{:S(2)}) %all-to-all-start.2) | async-done | bytes 262176 | tf_op jit(solution)/shard_map/all_to_all | solution.py:366
  252.1 1.1 copy.119
  253.1 123.8 %inner_backward.1 = (bf16[2048,64]{1,0:T(8,128)(2,1)}, bf16[2048,64]{1,0:T(8,128)(2,1)}, bf16[2048,64]{1,0:T(8,128)(2,1)}, f32[2048,1]{1,0:T(8,128)}, f32[80,256...) custom-call(bf16[2048,64]{1,0:T(8,128)(2,1)} %bitcast.132, ...), custom_call_target="tpu_custom_call" | custom-call | tf_op jit(solution)/shard_map/inner_backward/pallas_call | solution.py:324
  377.6 2.2 fusion.7
  379.8 3.0 concatenate.23
  382.8 1.3 copy.121
  384.1 3.7 all-to-all-start.3
  390.8 17.6 %all-to-all-done.3 = bf16[8,256,194]{1,2,0:T(8,128)(2,1)S(1)} async-done(((bf16[8,256,194]{1,2,0:T(8,128)(2,1)}), bf16[8,256,194]{1,2,0:T(8,128)(2,1)S(1)}, u32[]{:S(2)}, u32[]{:S(2)}) %all-to-all-start.3) | async-done | bytes 794656 | tf_op jit(solution)/shard_map/all_to_all | solution.py:372
  409.8 1.3 fusion.72
  411.1 1.3 convolution_add_fusion.3
  412.4 8.8 %concatenate.27 = f32[102339]{0:T(1024)} concatenate(f32[49152]{0:T(1024)S(1)} %bitcast.136, f32[49152]{0:T(1024)} %select_n.84, f32[768]{0:T(1024)S(1)} %select_n.86, f32[192]{0:T(256)S(1)} %select_n.88, f32[192]{0:T(256)S(1)} %select_n.90, f32[192]{0:T(256)S(1)} %select_n.92, f32[192]{0:T(256)S(1)} %get-tuple-element.150, f32[192]{0:T(256)S(1)} %get-tuple-element.153, ...), dimensions={0} | concatenate | bytes 818712 | tf_op jit(solution)/shard_map/concatenate | solution.py:562
  421.2 1.3 convolution_add_fusion.2
  422.5 1.3 convolution_add_fusion.1
  424.8 0.9 copy.138
  426.9 1.3 copy.140
  428.3 2.0 fusion.5
  430.4 2.0 fusion.4
  432.4 1.3 fusion.1
  433.7 1.3 fusion
  435.0 1.3 fusion.3
  436.4 4.7 copy.142
  441.1 1.0 copy-done.8
  442.2 1.0 copy.137
  444.1 37.9 %psum.62 = f32[1536]{0:T(1024)S(1)} all-reduce(f32[1536]{0:T(1024)S(1)} %pad_maximum_fusion.1), channel_id=1, replica_groups=mesh['seq'=8,'head'=4] {'seq','head'}, use_global_device_ids=true, to_apply=%region_20.21 | all-reduce | flops 1536 | bytes 12288 | tf_op jit(solution)/shard_map/psum | solution.py:588
  483.2 10.9 %all-reduce.15.cloned.1.call-done = f32[102339]{0:T(1024)} async-done(((f32[102339]{0:T(1024)}), f32[102339]{0:T(1024)}) %all-reduce.15.cloned.1.call-update) | async-done | bytes 409372 | tf_op jit(solution)/shard_map/psum | solution.py:567
  495.5 1.5 fusion.63
  498.9 1.0 fusion.64
  500.1 0.8 copy.131
  503.5 1.3 slice.159
  504.8 12.0 %reduce-scatter.15.cloned.1.call-done = bf16[192,256]{1,0:T(8,128)(2,1)} async-done(((bf16[768,256]{1,0:T(8,128)(2,1)}), bf16[192,256]{1,0:T(8,128)(2,1)}) %reduce-scatter.15.cloned.1.call-update) | async-done | bytes 98320
  516.8 1.0 copy.139
  518.7 64.6 %reduce-scatter.17.cloned.1.call-done = bf16[96,576]{1,0:T(8,128)(2,1)} async-done(((bf16[768,576]{1,0:T(8,128)(2,1)}), bf16[96,576]{1,0:T(8,128)(2,1)}) %reduce-scatter.17.cloned.1.call-update) | async-done | bytes 110608
  583.4 1.0 copy.141
  586.6 72.3 %reduce-scatter.19.cloned.1.call-done = bf16[96,1920]{1,0:T(8,128)(2,1)} async-done(((bf16[768,1920]{1,0:T(8,128)(2,1)}), bf16[96,1920]{1,0:T(8,128)(2,1)}) %reduce-scatter.19.cloned.1.call-update) | async-done | bytes 368656
  659.0 1.3 copy.143
  (184 shorter events, 30.6 us)
Async XLA Ops:
  7.2 185.1 %copy-start = (bf16[512,768]{1,0:T(8,128)(2,1)S(1)}, bf16[512,768]{1,0:T(8,128)(2,1)}, u32[]{:S(2)}) copy-start(bf16[512,768]{1,0:T(8,128)(2,1)} %param.42) | copy-start | bytes 2359300
  7.2 11.1 %copy-start.28 = (f32[768]{0:T(1024)S(1)}, f32[768]{0:T(1024)}, u32[]{:S(2)}) copy-start(f32[768]{0:T(1024)} %param.23) | copy-start | bytes 9220
  7.2 11.1 %copy-start.21 = (bf16[768,192]{0,1:T(8,128)(2,1)S(1)}, bf16[768,192]{0,1:T(8,128)(2,1)}, u32[]{:S(2)}) copy-start(bf16[768,192]{0,1:T(8,128)(2,1)} %param.26) | copy-start | bytes 884740
  7.2 11.4 %copy-start.20 = (bf16[768,192]{0,1:T(8,128)(2,1)S(1)}, bf16[768,192]{0,1:T(8,128)(2,1)}, u32[]{:S(2)}) copy-start(bf16[768,192]{0,1:T(8,128)(2,1)} %param.24) | copy-start | bytes 884740
  18.3 7.7 %copy-start.36 = (f32[3,64]{1,0:T(4,128)S(1)}, f32[3,64]{1,0:T(4,128)}, u32[]{:S(2)}) copy-start(f32[3,64]{1,0:T(4,128)} %param.35) | copy-start | bytes 2308
  18.3 8.9 %copy-start.25 = (f32[3,256,64]{1,2,0:T(8,128)S(1)}, f32[3,256,64]{1,2,0:T(8,128)}, u32[]{:S(2)}) copy-start(f32[3,256,64]{1,2,0:T(8,128)} %param.34) | copy-start | bytes 589828
  20.1 27.2 %all-to-all-start = ((bf16[8,256,194]{1,2,0:T(8,128)(2,1)}), bf16[8,256,194]{1,2,0:T(8,128)(2,1)S(1)}, u32[]{:S(2)}, u32[]{:S(2)}) async-start(bf16[8,256,194]{1,2,0:T(8,128)(2,1)} %pad.24), calls=%async_computation | async-start | bytes 1638400 | tf_op jit(solution)/shard_map/all_to_all | solution.py:366
  25.9 161.9 %all-reduce.11.cloned.1.call-start = ((), (), s32[]{:S(2)}) async-start(), calls=%async_computation.8 | async-start | bytes 1572864 | tf_op jit(solution)/shard_map/psum | solution.py:467
  29.2 22.4 %copy-start.29 = (f32[1,64]{1,0:T(1,128)}, f32[1,64]{1,0:T(1,128)S(1)}, u32[]{:S(2)}) copy-start(f32[1,64]{1,0:T(1,128)S(1)} %get-tuple-element.202.gain_ref) | copy-start | bytes 772
  29.2 22.4 %copy-start.30 = (f32[1,64]{1,0:T(1,128)}, f32[1,64]{1,0:T(1,128)S(1)}, u32[]{:S(2)}) copy-start(f32[1,64]{1,0:T(1,128)S(1)} %get-tuple-element.203.bias_ref) | copy-start | bytes 772
  31.3 18.4 %copy-start.33 = (pred[80]{0:T(512)(128)(4,1)S(1)}, pred[80]{0:T(512)(128)(4,1)}, u32[]{:S(2)}) copy-start(pred[80]{0:T(512)(128)(4,1)} %constant.41.clone.1) | copy-start | bytes 244
  53.2 98.7 %copy-start.22 = (bf16[768,192]{0,1:T(8,128)(2,1)S(1)}, bf16[768,192]{0,1:T(8,128)(2,1)}, u32[]{:S(2)}) copy-start(bf16[768,192]{0,1:T(8,128)(2,1)} %param.27) | copy-start | bytes 884740
  53.2 98.7 %copy-start.32 = (f32[192]{0:T(256)S(1)}, f32[192]{0:T(256)}, u32[]{:S(2)}) copy-start(f32[192]{0:T(256)} %param.36) | copy-start | bytes 2308
  53.2 98.7 %copy-start.37 = (f32[192]{0:T(256)S(1)}, f32[192]{0:T(256)}, u32[]{:S(2)}) copy-start(f32[192]{0:T(256)} %param.37) | copy-start | bytes 2308
  126.2 26.8 %copy-start.19 = (bf16[192,768]{1,0:T(8,128)(2,1)S(1)}, bf16[192,768]{1,0:T(8,128)(2,1)}, u32[]{:S(2)}) copy-start(bf16[192,768]{1,0:T(8,128)(2,1)} %param.38) | copy-start | bytes 884740
  127.8 26.4 %copy-start.24 = (bf16[256,192]{0,1:T(8,128)(2,1)S(1)}, bf16[256,192]{0,1:T(8,128)(2,1)}, u32[]{:S(2)}) copy-start(bf16[256,192]{0,1:T(8,128)(2,1)} %param.43) | copy-start | bytes 294916
  151.9 37.2 %copy-start.27 = (f32[768]{0:T(1024)S(1)}, f32[768]{0:T(1024)}, u32[]{:S(2)}) copy-start(f32[768]{0:T(1024)} %param.39) | copy-start | bytes 9220
  153.0 7.4 %copy-start.15 = (bf16[256,192]{0,1:T(8,128)(2,1)}, bf16[256,192]{0,1:T(8,128)(2,1)S(1)}, u32[]{:S(2)}) copy-start(bf16[256,192]{0,1:T(8,128)(2,1)S(1)} %get-tuple-element.163) | copy-start | bytes 294916
  154.2 73.7 %all-reduce.13.cloned.1.call-start = ((), (), s32[]{:S(2)}) async-start(), calls=%async_computation.9 | async-start | bytes 786432 | tf_op jit(solution)/shard_map/psum | solution.py:495
  160.4 34.7 %copy-start.2 = (bf16[256,768]{0,1:T(8,128)(2,1)}, bf16[256,768]{0,1:T(8,128)(2,1)S(1)}, u32[]{:S(2)}) copy-start(bf16[256,768]{0,1:T(8,128)(2,1)S(1)} %all_gather.7) | copy-start | bytes 1179652
  190.7 2.2 copy-start.6
  192.3 1.1 copy-start.7
  192.9 1.1 copy-start.9
  192.9 1.1 copy-start.11
  192.9 50.5 %copy-start.13 = (bf16[256,512]{1,0:T(8,128)(2,1)}, bf16[256,512]{1,0:T(8,128)(2,1)S(1)}, u32[]{:S(2)}) copy-start(bf16[256,512]{1,0:T(8,128)(2,1)S(1)} %get-tuple-element.173) | copy-start | bytes 786436
  195.3 57.8 %copy-start.4 = (bf16[256,768]{1,0:T(8,128)(2,1)}, bf16[256,768]{1,0:T(8,128)(2,1)S(1)}, u32[]{:S(2)}) copy-start(bf16[256,768]{1,0:T(8,128)(2,1)S(1)} %copy.118) | copy-start | bytes 1179652
  237.7 14.4 %all-to-all-start.2 = ((bf16[8,256,64]{1,2,0:T(8,128)(2,1)}), bf16[8,256,64]{1,2,0:T(8,128)(2,1)S(1)}, u32[]{:S(2)}, u32[]{:S(2)}) async-start(bf16[8,256,64]{1,2,0:T(8,128)(2,1)} %pad.29), calls=%async_computation.2 | async-start | bytes 524288 | tf_op jit(solution)/shard_map/all_to_all | solution.py:366
  243.3 198.8 %reduce-scatter.13.cloned.1.call-start = ((), (), s32[]{:S(2)}) async-start(), calls=%async_computation.11 | async-start | bytes 491520
  379.8 8.1 %copy-start.26 = (f32[80,256]{1,0:T(8,128)S(1)}, f32[80,256]{1,0:T(8,128)}, u32[]{:S(2)}) copy-start(f32[80,256]{1,0:T(8,128)} %get-tuple-element.53) | copy-start | bytes 245764
  379.8 8.1 %copy-start.38 = (f32[1,64]{1,0:T(1,128)S(1)}, f32[1,64]{1,0:T(1,128)}, u32[]{:S(2)}) copy-start(f32[1,64]{1,0:T(1,128)} %get-tuple-element.55) | copy-start | bytes 772
  379.8 9.4 %copy-start.23 = (f32[64,256]{1,0:T(8,128)S(1)}, f32[64,256]{1,0:T(8,128)}, u32[]{:S(2)}) copy-start(f32[64,256]{1,0:T(8,128)} %get-tuple-element.54) | copy-start | bytes 196612
  379.8 9.5 %copy-start.34 = (f32[1,64]{1,0:T(1,128)S(1)}, f32[1,64]{1,0:T(1,128)}, u32[]{:S(2)}) copy-start(f32[1,64]{1,0:T(1,128)} %get-tuple-element.56) | copy-start | bytes 772
  379.8 9.5 %copy-start.35 = (f32[1,64]{1,0:T(1,128)S(1)}, f32[1,64]{1,0:T(1,128)}, u32[]{:S(2)}) copy-start(f32[1,64]{1,0:T(1,128)} %get-tuple-element.57) | copy-start | bytes 772
  384.1 24.3 %all-to-all-start.3 = ((bf16[8,256,194]{1,2,0:T(8,128)(2,1)}), bf16[8,256,194]{1,2,0:T(8,128)(2,1)S(1)}, u32[]{:S(2)}, u32[]{:S(2)}) async-start(bf16[8,256,194]{1,2,0:T(8,128)(2,1)} %copy.121), calls=%async_computation.3 | async-start | bytes 1638400 | tf_op jit(solution)/shard_map/all_to_all | solution.py:372
  387.8 106.4 %all-reduce.15.cloned.1.call-start = ((), (), s32[]{:S(2)}) async-start(), calls=%async_computation.10 | async-start | bytes 819200 | tf_op jit(solution)/shard_map/psum | solution.py:567
  409.8 2.6 copy-start.17
  411.1 12.8 %copy-start.31 = (bf16[768,3]{0,1:T(4,128)(2,1)S(1)}, bf16[768,3]{0,1:T(4,128)(2,1)}, u32[]{:S(2)}) copy-start(bf16[768,3]{0,1:T(4,128)(2,1)} %param.28) | copy-start | bytes 13828
  423.9 1.9 copy-start.18
  423.9 2.2 copy-start.16
  424.5 92.3 %reduce-scatter.15.cloned.1.call-start = ((), (), s32[]{:S(2)}) async-start(), calls=%async_computation.12 | async-start | bytes 491520
  425.7 157.6 %reduce-scatter.17.cloned.1.call-start = ((), (), s32[]{:S(2)}) async-start(), calls=%async_computation.13 | async-start | bytes 1105920
  426.8 3.5 copy-start.5
  426.9 6.8 %copy-start.10 = (bf16[256,512]{1,0:T(8,128)(2,1)S(1)}, bf16[256,512]{1,0:T(8,128)(2,1)}, u32[]{:S(2)}) copy-start(bf16[256,512]{1,0:T(8,128)(2,1)} %copy-done.9) | copy-start | bytes 786436
  428.3 4.2 copy-start.12
  428.3 6.8 %copy-start.3 = (bf16[256,768]{0,1:T(8,128)(2,1)S(1)}, bf16[256,768]{0,1:T(8,128)(2,1)}, u32[]{:S(2)}) copy-start(bf16[256,768]{0,1:T(8,128)(2,1)} %copy-done.2) | copy-start | bytes 1179652
  428.3 6.8 %copy-start.14 = (bf16[256,512]{1,0:T(8,128)(2,1)S(1)}, bf16[256,512]{1,0:T(8,128)(2,1)}, u32[]{:S(2)}) copy-start(bf16[256,512]{1,0:T(8,128)(2,1)} %copy-done.13) | copy-start | bytes 786436
  428.3 230.7 %reduce-scatter.19.cloned.1.call-start = ((), (), s32[]{:S(2)}) async-start(), calls=%async_computation.14 | async-start | bytes 3317760
  441.1 1.0 copy-start.8
  585.9 78.3 %copy-start.1 = (bf16[512,768]{1,0:T(8,128)(2,1)S(1)}, bf16[512,768]{1,0:T(8,128)(2,1)}, u32[]{:S(2)}) copy-start(bf16[512,768]{1,0:T(8,128)(2,1)} %param.42) | copy-start | bytes 2359300
Sparse Core Ops, SparseCore 0:
  154.3 33.3 all-reduce.10
  195.2 32.6 all-reduce.12
  246.8 21.4 reduce-scatter.12
  424.6 69.5 all-reduce.14
  496.5 20.2 reduce-scatter.14
  520.0 63.3 reduce-scatter.16
  587.4 71.5 reduce-scatter.18

commit v2 on v1

v2 whole, which is shorter than its diff:
```python
import functools

import jax
import jax.numpy as jnp
from jax import lax
from jax.experimental import pallas as pl
from jax.experimental.pallas import tpu as pltpu
from jax.sharding import PartitionSpec as P

MINI = 16
CHAIN = 8
FIRST = 2
AUG = 80
eps_norm = 1e-06
gelu_scale = 0.7978845608028654
f32 = jnp.float32
bf16 = jnp.bfloat16


def dot_nn(a, b):
    return lax.dot_general(a, b, (((1,), (0,)), ((), ())), preferred_element_type=f32)


def dot_nt(a, b):
    return lax.dot_general(a, b, (((1,), (1,)), ((), ())), preferred_element_type=f32)


def dot_tn(a, b):
    return lax.dot_general(a, b, (((0,), (0,)), ((), ())), preferred_element_type=f32)


def mean_row(x):
    return jnp.sum(x, axis=1, keepdims=True) * (1.0 / x.shape[1])


def gelu_first(z):
    sq = z * z
    th = jnp.tanh(gelu_scale * z * (1.0 + 0.044715 * sq))
    half = 0.5 * (1.0 + th)
    act = z * half
    der = half + (0.5 * gelu_scale) * z * (1.0 - th * th) * (1.0 + 0.134145 * sq)
    return act, der


def gelu_second(z):
    sq = z * z
    th = jnp.tanh(gelu_scale * z * (1.0 + 0.044715 * sq))
    half = 0.5 * (1.0 + th)
    act = z * half
    slope = gelu_scale * (1.0 + 0.134145 * sq)
    sech = 1.0 - th * th
    der = half + 0.5 * z * sech * slope
    curve = sech * (slope + z * (0.5 * gelu_scale * 0.26829 * z) - z * th * slope * slope)
    return act, der, curve


def tri_mask():
    rows = lax.broadcasted_iota(jnp.int32, (MINI, MINI), 0)
    cols = lax.broadcasted_iota(jnp.int32, (MINI, MINI), 1)
    return jnp.where(rows >= cols, 1.0, 0.0).astype(f32)


def inner_target_grad(z, base, gain_sq, rate):
    mz = mean_row(z)
    m_zz = mean_row(z * z)
    zg = z * gain_sq
    m_zg = mean_row(zg)
    m_zzg = mean_row(zg * z)
    m_zb = mean_row(z * base)
    m_b = mean_row(base)
    m_sq = mean_row(gain_sq)
    inv = lax.rsqrt(m_zz - mz * mz + eps_norm)
    c_zg = m_zg - mz * m_sq
    c_zzg = m_zzg - mz * (m_zg + c_zg)
    c_zb = m_zb - mz * m_b
    m_g = inv * c_zg + m_b
    m_gn = inv * (inv * c_zzg + c_zb)
    zc = z - mz
    n = zc * inv
    grad = inv * (n * (gain_sq - m_gn) + (base - m_g))
    return rate * grad, zc


def forward_step(state, z1, key_aug, key_next, query_aug, base, rate, gain, gain_sq, bias, tri):
    w1, w2t, b2 = state
    act, der = gelu_first(z1)
    act_h = act.astype(bf16)
    w1_h = w1.astype(bf16)
    w2_h = w2t.astype(bf16)
    s2, zc = inner_target_grad(dot_nt(act_h, w2_h) + b2, base, gain_sq, rate)
    s2_h = s2.astype(bf16)
    upd = dot_nn(s2_h, w2_h)
    s1_h = (upd * der).astype(bf16)
    both = jnp.concatenate([key_next, query_aug], axis=0)
    coef = dot_nt(both, key_aug)
    coef = jnp.concatenate([coef[:MINI], coef[MINI:] * tri], axis=0)
    zz = dot_nn(both, w1_h) - dot_nn(coef.astype(bf16), s1_h)
    z1_next = zz[:MINI]
    z1b = zz[MINI:]
    new_w1 = w1 - dot_tn(key_aug, s1_h)
    new_w2t = w2t - dot_tn(s2_h, act_h)
    new_b2 = b2 - jnp.sum(s2, axis=0, keepdims=True)
    actb, _ = gelu_first(z1b)
    actb_h = actb.astype(bf16)
    att = (dot_nt(actb_h, act_h) + 1.0) * tri
    z2b = dot_nt(actb_h, w2_h) + b2 - dot_nn(att.astype(bf16), s2_h)
    z2b = z2b - mean_row(z2b)
    invb = lax.rsqrt(mean_row(z2b * z2b) + eps_norm)
    out = z2b * invb * gain + bias
    return (new_w1, new_w2t, new_b2), z1_next, out, (w1_h, w2_h, upd, zc, s2, z1b, z2b)


def backward_step(carry, saved, d_out, key_aug, query_aug, target, rate, keep, gain, gain_sq, bias, tri):
    p1, p2t, p2 = carry
    w1_h, w2_h, z1, upd, zc, s2, z1b, z2b = saved
    act, der, curve = gelu_second(z1)
    act_h = act.astype(bf16)
    actb, derb = gelu_first(z1b)
    actb_h = actb.astype(bf16)
    s2_h = s2.astype(bf16)
    s1_h = (upd * der).astype(bf16)
    p1_h = p1.astype(bf16)
    p2_h = p2t.astype(bf16)
    invb = lax.rsqrt(mean_row(z2b * z2b) + eps_norm)
    nb = z2b * invb
    dn = d_out * gain
    d_z2b = invb * (dn - mean_row(dn) - nb * mean_row(dn * nb))
    d_z2b_h = d_z2b.astype(bf16)
    d_att2 = (-dot_nt(d_z2b_h, s2_h) * tri).astype(bf16)
    d_actb = dot_nn(d_z2b_h, w2_h) + dot_nn(d_att2, act_h)
    d_z1b_h = (d_actb * derb).astype(bf16)
    att2 = ((dot_nt(actb_h, act_h) + 1.0) * tri).astype(bf16)
    att1 = (dot_nt(query_aug, key_aug) * tri).astype(bf16)
    c2 = dot_tn(att2, d_z2b_h)
    c3 = dot_tn(d_att2, actb_h)
    c1 = dot_tn(att1, d_z1b_h)
    d_att1 = (-dot_nt(d_z1b_h, s1_h) * tri).astype(bf16)
    d_query = dot_nt(d_z1b_h, w1_h) + dot_nn(d_att1, key_aug)
    d_key = dot_tn(d_att1, query_aug)
    d_s1 = -c1 - dot_nn(key_aug, p1_h)
    d_upd = d_s1 * der
    d_upd_h = d_upd.astype(bf16)
    d_s2 = dot_nt(d_upd_h, w2_h) - c2 - dot_nt(act_h, p2_h) - p2
    h = rate * d_s2
    inv = lax.rsqrt(mean_row(zc * zc) + eps_norm)
    n = zc * inv
    base = (bias - target) * gain
    big_g = n * gain_sq + base
    m_g = mean_row(big_g)
    m_gn = mean_row(big_g * n)
    m_sq = mean_row(gain_sq)
    ng = n * gain_sq
    m_ng = mean_row(ng)
    m_nng = mean_row(n * ng)
    g = inv * (big_g - m_g - n * m_gn)
    a1 = mean_row(h)
    a2 = mean_row(h * n)
    a3 = mean_row(h * gain_sq)
    a4 = mean_row(h * ng)
    a5 = mean_row(h * g)
    proj = h - a1 - n * a2
    d_g = inv * proj
    dnn = inv * (proj * gain_sq - h * m_gn - big_g * a2)
    m_dn = inv * (a3 - a1 * (m_sq + m_gn) - a2 * (m_ng + m_g))
    m_dnn = inv * (a4 - a1 * m_ng - a2 * (m_nng + 2.0 * m_gn))
    d_zc = inv * (dnn - m_dn - n * (m_dnn + a5))
    d_zc_h = d_zc.astype(bf16)
    d_act = dot_nn(d_zc_h, w2_h) + c3 - dot_nn(s2_h, p2_h)
    d_z1 = d_act * der + d_s1 * upd * curve
    d_z1_h = d_z1.astype(bf16)
    d_gg = d_g * gain
    d_key = d_key + dot_nt(d_z1_h, w1_h) - dot_nt(s1_h, p1_h)
    d_key = d_key[:, : gain.shape[1]] + d_gg
    d_query = d_query[:, : gain.shape[1]] + d_out
    d_value = -d_gg
    d_logit = keep * jnp.sum(d_s2 * s2, axis=1, keepdims=True)
    new_p1 = p1 + dot_tn(
        jnp.concatenate([key_aug, query_aug], axis=0), jnp.concatenate([d_z1_h, d_z1b_h], axis=0)
    )
    new_p2t = p2t + dot_tn(
        jnp.concatenate([s2_h, d_zc_h, d_z2b_h], axis=0),
        jnp.concatenate([d_upd_h, act_h, actb_h], axis=0),
    )
    new_p2 = p2 + jnp.sum(d_zc + d_z2b, axis=0, keepdims=True)
    d_bias = jnp.sum(d_out + d_gg, axis=0, keepdims=True)
    d_gain = jnp.sum(d_out * nb + d_g * (2.0 * n * gain + bias - target), axis=0, keepdims=True)
    return (new_p1, new_p2t, new_p2), (d_query, d_key, d_value, d_logit), d_gain, d_bias


MESH = pl.DeviceIdType.MESH
PACK = 256
ENDS = 160


def seq_place():
    index = lax.axis_index("seq")
    pos = lax.rem(index, CHAIN)
    return pos, index - pos


def meet_group(pos, base):
    barrier = pltpu.get_barrier_semaphore()
    for d in range(1, CHAIN):
        pl.semaphore_signal(
            barrier, inc=1, device_id={"seq": base + lax.rem(pos + d, CHAIN)}, device_id_type=MESH)
    pl.semaphore_wait(barrier, CHAIN - 1)


def push(src, dst, send_sem, recv_sem, target):
    return pltpu.make_async_remote_copy(
        src_ref=src, dst_ref=dst, send_sem=send_sem, recv_sem=recv_sem,
        device_id={"seq": target}, device_id_type=MESH)


def await_bytes(ref, sem):
    pltpu.make_async_copy(ref, ref, sem).wait()


def swap_start(src, dst, send, recv, local_sem, pos, base):
    for d in range(1, CHAIN):
        peer = lax.rem(pos + d, CHAIN)
        push(src.at[peer], dst.at[pos], send.at[d - 1], recv.at[d - 1], base + peer).start()
    pltpu.make_async_copy(src.at[pos], dst.at[pos], local_sem).start()


def swap_wait(src, dst, send, recv, local_sem, pos, base):
    for d in range(1, CHAIN):
        peer = lax.rem(pos + d, CHAIN)
        origin = lax.rem(pos + CHAIN - d, CHAIN)
        push(src.at[peer], dst.at[pos], send.at[d - 1], recv.at[d - 1], base + peer).wait_send()
        await_bytes(dst.at[origin], recv.at[d - 1])
    await_bytes(dst.at[pos], local_sem)


def fwd_kernel(block, unroll, heads, pay_ref, w1_in, b1_in, w2_in, b2_in, gain_in, bias_in,
               mixed_ref, k_out, q_out, aux_out, w1s_ref, w2s_ref, z1s_ref, upd_ref, zc_ref, s2_ref, z1b_ref, z2b_ref,
               got, k_all, q_all, base_all, aux_all, mixed_all, w1, w2t, b2, z1,
               pay_send, pay_recv, mix_send, mix_recv):
    blk = pl.program_id(0)
    last = pl.num_programs(0) - 1
    pos, base = seq_place()
    width = gain_in.shape[1]
    hidden = w1.shape[1]
    rows_each = pay_ref.shape[0]
    per = rows_each // block
    owner = (pos >= FIRST) & (pos < FIRST + heads)
    mine = jnp.clip(pos - FIRST, 0, heads - 1)
    gain = gain_in[pl.ds(mine, 1), :]
    bias = bias_in[pl.ds(mine, 1), :]
    gain_sq = gain * gain
    tri = tri_mask()

    @pl.when(blk == 0)
    def _():
        meet_group(pos, base)
        for j in range(heads):
            src = pay_ref.at[:, pl.ds(j * PACK, PACK)]
            dst = got.at[pos]

            @pl.when(pos != FIRST + j)
            def _():
                push(src, dst, pay_send.at[j], pay_recv.at[pos], base + FIRST + j).start()

            @pl.when(pos == FIRST + j)
            def _():
                pltpu.make_async_copy(src, dst, pay_recv.at[pos]).start()

    def take_in(p):
        await_bytes(got.at[p], pay_recv.at[p])
        part = got[p]
        rows = pl.ds(pl.multiple_of(p * rows_each, rows_each), rows_each)
        lane = lax.broadcasted_iota(jnp.int32, (rows_each, AUG), 1)
        one = jnp.ones((), bf16)
        zero = jnp.zeros((), bf16)
        tail = jnp.where(lane == width, one, zero)
        query = part[:, :AUG]
        key = part[:, width : width + AUG]
        q_all[rows, :] = jnp.where(lane < width, query, tail)
        k_all[rows, :] = jnp.where(lane < width, key, tail)
        key_f = part[:, width : 2 * width].astype(f32)
        target = part[:, 2 * width : 3 * width].astype(f32) - key_f
        logit = part[:, 3 * width : 3 * width + 1].astype(f32) + part[:, 3 * width + 1 : 3 * width + 2].astype(f32)
        sig = 1.0 / (1.0 + jnp.exp(-logit))
        base_all[rows, :] = (bias - target) * gain
        spot = lax.broadcasted_iota(jnp.int32, (rows_each, 2 * width), 1)
        wide = jnp.concatenate([target, target], axis=1)
        aux_all[rows, :] = jnp.where(
            spot < width, wide, jnp.where(spot == width, sig * (1.0 / width), 1.0 - sig))

    def send_mixed(b):
        p = lax.div(b, per)
        src = mixed_all.at[pl.ds(pl.multiple_of(b * block, block), block), :]
        dst = mixed_ref.at[mine, pl.ds(pl.multiple_of(lax.rem(b, per) * block, block), block), :]

        @pl.when(p != pos)
        def _():
            push(src, dst, mix_send, mix_recv.at[mine], base + p).start()

        @pl.when(p == pos)
        def _():
            pltpu.make_async_copy(src, dst, mix_recv.at[mine]).start()

    @pl.when(owner)
    def _():
        @pl.when(blk == 0)
        def _():
            row = lax.broadcasted_iota(jnp.int32, (AUG - width, hidden), 0)
            w1[pl.ds(0, width), :] = w1_in[mine]
            w1[pl.ds(width, AUG - width), :] = jnp.where(row == 0, b1_in[pl.ds(mine, 1), :], 0.0)
            turned = w2_in[mine].T
            w2t[...] = turned - jnp.mean(turned, axis=0, keepdims=True)
            start = b2_in[pl.ds(mine, 1), :]
            b2[...] = start - mean_row(start)
            k_all[pl.ds(CHAIN * rows_each, MINI), :] = jnp.zeros((MINI, AUG), bf16)
            take_in(0)
            z1[...] = dot_nn(k_all[0:MINI, :], w1[...].astype(bf16))

        @pl.when((lax.rem(blk, per) == 0) & (blk < last + 1 - per))
        def _():
            take_in(lax.div(blk, per) + 1)

        @pl.when(blk > 0)
        def _():
            send_mixed(blk - 1)

        brows = pl.ds(pl.multiple_of(blk * block, block), block)
        k_out[...] = k_all[brows, :]
        q_out[...] = q_all[brows, :]
        aux_out[...] = aux_all[brows, :]

        def group(it, _):
            for u in range(unroll):
                loc = it * unroll + u
                row = pl.multiple_of(blk * block + loc * MINI, MINI)
                rows = pl.ds(row, MINI)
                lrows = pl.ds(pl.multiple_of(loc * MINI, MINI), MINI)
                q_aug = q_all[rows, :]
                z1_now = z1[...]
                state, z1_next, out, saved = forward_step(
                    (w1[...], w2t[...], b2[...]), z1_now, k_all[rows, :], k_all[pl.ds(row + MINI, MINI), :], q_aug,
                    base_all[rows, :], aux_all[rows, width : width + 1], gain, gain_sq, bias, tri)
                w1[...], w2t[...], b2[...] = state
                z1[...] = z1_next
                mixed_all[rows, :] = (out + q_aug[:, :width].astype(f32)).astype(bf16)
                w1s_ref[loc], w2s_ref[loc], upd, zc, s2, z1b, z2b = saved
                z1s_ref[lrows, :] = z1_now
                upd_ref[lrows, :] = upd
                zc_ref[lrows, :] = zc
                s2_ref[lrows, :] = s2
                z1b_ref[lrows, :] = z1b
                z2b_ref[lrows, :] = z2b
            return 0

        lax.fori_loop(0, block // MINI // unroll, group, 0)

    @pl.when(blk == last)
    def _():
        @pl.when(owner)
        def _():
            send_mixed(last)
            others = mixed_all.at[pl.ds(0, (CHAIN - 1) * rows_each), :]
            await_bytes(others, mix_send)

        for j in range(heads):
            @pl.when(pos != FIRST + j)
            def _():
                await_bytes(got.at[pos], pay_send.at[j])

            await_bytes(mixed_ref.at[j], mix_recv.at[j])


def chain_forward(payload, w1, b1, w2, b2, gain, bias, block=128, unroll=8):
    rows = payload.shape[0]
    heads, width, hidden = w1.shape
    tokens = rows * CHAIN
    steps = tokens // MINI
    nb = block // MINI
    whole = lambda a: pl.BlockSpec(a.shape, lambda i: (0,) * a.ndim)
    rowblk = lambda w: pl.BlockSpec((block, w), lambda i: (i, 0))
    stepblk = lambda r: pl.BlockSpec((nb, r, hidden), lambda i: (i, 0, 0))
    anywhere = pl.BlockSpec(memory_space=pl.ANY)
    small = (w1, b1, w2, b2, gain, bias)
    dma = pltpu.SemaphoreType.DMA
    wide = jax.ShapeDtypeStruct((tokens, hidden), f32)
    narrow = jax.ShapeDtypeStruct((tokens, width), f32)
    return pl.pallas_call(
        functools.partial(fwd_kernel, block, unroll, heads),
        grid=(tokens // block,),
        in_specs=[anywhere] + [whole(a) for a in small],
        out_specs=[anywhere, rowblk(AUG), rowblk(AUG), rowblk(2 * width), stepblk(AUG), stepblk(width),
                   rowblk(hidden), rowblk(hidden), rowblk(width), rowblk(width), rowblk(hidden), rowblk(width)],
        out_shape=[jax.ShapeDtypeStruct((heads, rows, width), bf16),
                   jax.ShapeDtypeStruct((tokens, AUG), bf16),
                   jax.ShapeDtypeStruct((tokens, AUG), bf16),
                   jax.ShapeDtypeStruct((tokens, 2 * width), f32),
                   jax.ShapeDtypeStruct((steps, AUG, hidden), bf16),
                   jax.ShapeDtypeStruct((steps, width, hidden), bf16),
                   wide, wide, narrow, narrow, wide, narrow],
        scratch_shapes=[pltpu.VMEM((CHAIN, rows, PACK), bf16),
                        pltpu.VMEM((tokens + MINI, AUG), bf16), pltpu.VMEM((tokens, AUG), bf16),
                        pltpu.VMEM((tokens, width), f32), pltpu.VMEM((tokens, 2 * width), f32),
                        pltpu.VMEM((tokens, width), bf16),
                        pltpu.VMEM((AUG, hidden), f32), pltpu.VMEM((width, hidden), f32),
                        pltpu.VMEM((1, width), f32), pltpu.VMEM((MINI, hidden), f32),
                        dma((heads,)), dma((CHAIN,)), dma, dma((heads,))],
        compiler_params=pltpu.CompilerParams(collective_id=0, has_side_effects=True),
        name="inner_forward",
    )(payload, *small)


def bwd_kernel(block, unroll, heads, gm_ref, early_ref, norm_ref, gain_in, bias_in,
               k_ref, q_ref, aux_ref, w1s_ref, w2s_ref, z1s_ref, upd_ref, zc_ref, s2_ref, z1b_ref, z2b_ref,
               grads_ref, ends_ref, early_out, norm_out,
               dout, early_got, packed, ends, p1, p2t, p2, dg, db,
               gm_send, gm_recv, ea_send, ea_recv, ea_loc, no_send, no_recv, no_loc, bc_send, bc_recv, en_send, en_recv):
    pid = pl.program_id(0)
    last = pl.num_programs(0) - 1
    blk = last - pid
    pos, base = seq_place()
    width = gain_in.shape[1]
    rows_each = gm_ref.shape[1]
    per = rows_each // block
    owner = (pos >= FIRST) & (pos < FIRST + heads)
    mine = jnp.clip(pos - FIRST, 0, heads - 1)
    gain = gain_in[pl.ds(mine, 1), :]
    bias = bias_in[pl.ds(mine, 1), :]
    gain_sq = gain * gain
    tri = tri_mask()
    count = block // MINI

    @pl.when(pid == 0)
    def _():
        meet_group(pos, base)
        for j in range(heads):
            @pl.when(pos != FIRST + j)
            def _():
                push(gm_ref.at[j], dout.at[pos], gm_send.at[j], gm_recv.at[pos], base + FIRST + j).start()

            @pl.when(pos == FIRST + j)
            def _():
                pltpu.make_async_copy(gm_ref.at[j], dout.at[pos], gm_recv.at[pos]).start()

        swap_start(early_ref, early_got, ea_send, ea_recv, ea_loc, pos, base)
        swap_start(norm_ref, norm_out, no_send, no_recv, no_loc, pos, base)

    def share_block(b):
        rows = pl.ds(pl.multiple_of(b * block, block), block)
        for d in range(1, CHAIN):
            push(packed.at[rows, :], grads_ref.at[mine, rows, :], bc_send.at[d - 1], bc_recv.at[mine],
                 base + lax.rem(pos + d, CHAIN)).start()
        pltpu.make_async_copy(packed.at[rows, :], grads_ref.at[mine, rows, :], bc_recv.at[mine]).start()

    @pl.when(owner)
    def _():
        @pl.when(pid == 0)
        def _():
            for r in (p1, p2t, p2, dg, db):
                r[...] = jnp.zeros_like(r)

        @pl.when(lax.rem(pid, per) == 0)
        def _():
            p = lax.div(blk, per)
            await_bytes(dout.at[p], gm_recv.at[p])

        @pl.when(pid > 0)
        def _():
            share_block(blk + 1)

        def group(it, _):
            for u in range(unroll):
                loc = count - 1 - (it * unroll + u)
                row = pl.multiple_of(blk * block + loc * MINI, MINI)
                lr = pl.ds(pl.multiple_of(loc * MINI, MINI), MINI)
                inner = pl.ds(pl.multiple_of(lax.rem(blk, per) * block + loc * MINI, MINI), MINI)
                saved = (w1s_ref[loc], w2s_ref[loc], z1s_ref[lr, :], upd_ref[lr, :], zc_ref[lr, :], s2_ref[lr, :],
                         z1b_ref[lr, :], z2b_ref[lr, :])
                aux = aux_ref[lr, :]
                carry, outs, dgn, dbn = backward_step(
                    (p1[...], p2t[...], p2[...]), saved, dout[lax.div(blk, per), inner, :].astype(f32), k_ref[lr, :],
                    q_ref[lr, :], aux[:, :width], aux[:, width : width + 1], aux[:, width + 1 : width + 2],
                    gain, gain_sq, bias, tri)
                p1[...], p2t[...], p2[...] = carry
                dg[...] += dgn
                db[...] += dbn
                d_query, d_key, d_value, d_logit = outs
                high = d_logit.astype(bf16).astype(f32)
                lane = lax.broadcasted_iota(jnp.int32, (MINI, width), 1)
                extra = jnp.where(lane == 0, high, jnp.where(lane == 1, d_logit - high, 0.0))
                packed[pl.ds(row, MINI), :] = jnp.concatenate([d_query, d_key, d_value, extra], axis=1).astype(bf16)
            return 0

        lax.fori_loop(0, count // unroll, group, 0)

        @pl.when(pid == last)
        def _():
            ends[pl.ds(0, AUG), :] = p1[...].astype(bf16)
            ends[pl.ds(AUG, width), :] = p2t[...].astype(bf16)
            rest = ENDS - AUG - width
            row = lax.broadcasted_iota(jnp.int32, (rest, width), 0)
            tailing = jnp.where(row == 0, p2[...], jnp.where(row == 1, dg[...], jnp.where(row == 2, db[...], 0.0)))
            ends[pl.ds(AUG + width, rest), :] = jnp.concatenate([tailing] * 4, axis=1).astype(bf16)
            share_block(0)
            for d in range(1, CHAIN):
                push(ends, ends_ref.at[mine], en_send.at[d - 1], en_recv.at[mine],
                     base + lax.rem(pos + d, CHAIN)).start()
            pltpu.make_async_copy(ends, ends_ref.at[mine], en_recv.at[mine]).start()

    @pl.when(pid == last)
    def _():
        swap_wait(early_ref, early_got, ea_send, ea_recv, ea_loc, pos, base)
        swap_wait(norm_ref, norm_out, no_send, no_recv, no_loc, pos, base)

        def add_up(c, _):
            rows = pl.ds(pl.multiple_of(c * MINI, MINI), MINI)
            acc = early_got[0, rows, :].astype(f32)
            for p in range(1, CHAIN):
                acc = acc + early_got[p, rows, :].astype(f32)
            early_out[rows, :] = acc
            return 0

        lax.fori_loop(0, early_out.shape[0] // MINI, add_up, 0)
        for j in range(heads):
            @pl.when(pos != FIRST + j)
            def _():
                await_bytes(dout.at[pos], gm_send.at[j])

            await_bytes(grads_ref.at[j], bc_recv.at[j])
            await_bytes(ends_ref.at[j], en_recv.at[j])

        @pl.when(owner)
        def _():
            for d in range(1, CHAIN):
                await_bytes(packed, bc_send.at[d - 1])
                await_bytes(ends, en_send.at[d - 1])


def chain_backward(grad_mixed, early, normed, gain, bias, saved, block=128, unroll=4):
    heads, rows, width = grad_mixed.shape
    tokens = rows * CHAIN
    hidden = saved[5].shape[1]
    nblk = tokens // block
    nb = block // MINI
    whole = lambda a: pl.BlockSpec(a.shape, lambda i: (0,) * a.ndim)
    rowblk = lambda w: pl.BlockSpec((block, w), lambda i: (nblk - 1 - i, 0))
    stepblk = lambda r: pl.BlockSpec((nb, r, hidden), lambda i: (nblk - 1 - i, 0, 0))
    anywhere = pl.BlockSpec(memory_space=pl.ANY)
    dma = pltpu.SemaphoreType.DMA
    seven = dma((CHAIN - 1,))
    share = early.shape[1:]
    return pl.pallas_call(
        functools.partial(bwd_kernel, block, unroll, heads),
        grid=(nblk,),
        in_specs=[anywhere] * 3 + [whole(gain), whole(bias), rowblk(AUG), rowblk(AUG), rowblk(2 * width),
                                   stepblk(AUG), stepblk(width), rowblk(hidden), rowblk(hidden), rowblk(width),
                                   rowblk(width), rowblk(hidden), rowblk(width)],
        out_specs=[anywhere, anywhere, pl.BlockSpec(share, lambda i: (0, 0)), anywhere],
        out_shape=[jax.ShapeDtypeStruct((heads, tokens, PACK), bf16),
                   jax.ShapeDtypeStruct((heads, ENDS, hidden), bf16),
                   jax.ShapeDtypeStruct(share, f32),
                   jax.ShapeDtypeStruct(normed.shape, bf16)],
        scratch_shapes=[pltpu.VMEM((CHAIN, rows, width), bf16), pltpu.VMEM(early.shape, bf16),
                        pltpu.VMEM((tokens, PACK), bf16), pltpu.VMEM((ENDS, hidden), bf16),
                        pltpu.VMEM((AUG, hidden), f32), pltpu.VMEM((width, hidden), f32), pltpu.VMEM((1, width), f32),
                        pltpu.VMEM((1, width), f32), pltpu.VMEM((1, width), f32),
                        dma((heads,)), dma((CHAIN,)), seven, seven, dma, seven, seven, dma,
                        seven, dma((heads,)), seven, dma((heads,))],
        compiler_params=pltpu.CompilerParams(collective_id=1, has_side_effects=True),
        name="inner_backward",
    )(grad_mixed, early, normed, gain, bias, *saved)


def head_place():
    return lax.axis_index("head"), lax.axis_size("head")


def meet_heads(me, count):
    barrier = pltpu.get_barrier_semaphore()
    for d in range(1, count):
        pl.semaphore_signal(barrier, inc=1, device_id={"head": lax.rem(me + d, count)}, device_id_type=MESH)
    pl.semaphore_wait(barrier, count - 1)


def push_head(src, dst, send_sem, recv_sem, target):
    return pltpu.make_async_remote_copy(
        src_ref=src, dst_ref=dst, send_sem=send_sem, recv_sem=recv_sem,
        device_id={"head": target}, device_id_type=MESH)


def row_totals(first, second):
    ones = jnp.ones((8, first.shape[1]), f32)

    def total(x):
        return lax.dot_general(ones, x, (((1,), (1,)), ((), ())), precision=lax.Precision.HIGHEST,
                               preferred_element_type=f32)

    top, low = total(first), total(second)
    row = lax.broadcasted_iota(jnp.int32, top.shape, 0)
    return jnp.where(row == 0, top, low)


def mid_kernel(count, mixed_ref, x_ref, ct_ref, gate_pre_ref, normed_ref, w_out_ref, w_gate_ref, w_up_ref, w_down_ref,
               post_gain_ref, post_bias_ref, ffn_gain_ref,
               gm_ref, early_ref, ggp_ref, out_ref, grc_ref, small_ref,
               st_mine, st_got, pa_mine, pa_got, nt_all, rc_mine, rc_all, gn_mine, gn_got, dn_mine, dn_got, gov_all,
               gc_mine, gc_all, sb_mine, sb_got, gt_mine, gt_got, gh, gated, hidden, ggv, guv, resid,
               st_s, st_r, pa_s, pa_r, nt_s, nt_r, rc_s, rc_r, gn_s, gn_r, dn_s, dn_r, go_s, go_r, gc_s, gc_r, sb_s, sb_r,
               gt_s, gt_r):
    me, _ = head_place()
    heads, rows, width = mixed_ref.shape
    cols = heads * width
    full = cols * count
    part = rows // count
    peers = [(d, lax.rem(me + d, count)) for d in range(1, count)]
    meet_heads(me, count)

    def rows_of(device):
        return pl.ds(pl.multiple_of(device * part, part), part)

    def send_all(src, dst, send, recv):
        for d, peer in peers:
            push_head(src, dst.at[d - 1], send.at[d - 1], recv.at[d - 1], peer).start()

    def wait_all(src, dst, send, recv):
        for d, peer in peers:
            push_head(src, dst.at[d - 1], send.at[d - 1], recv.at[d - 1], peer).wait()

    z = jnp.concatenate([mixed_ref[j] for j in range(heads)], axis=1).astype(f32)
    st_mine[...] = row_totals(z, z * z)
    send_all(st_mine, st_got, st_s, st_r)
    gate_pre = gate_pre_ref[...]
    gate_act, gate_der = gelu_first(gate_pre)
    gh[...] = dot_nt(ct_ref[...], w_down_ref[...])
    wait_all(st_mine, st_got, st_s, st_r)
    tot = st_mine[...]
    for d, _ in peers:
        tot = tot + st_got[d - 1]
    tot = tot.T * (1.0 / full)
    mean_z = tot[:, 0:1]
    inv_z = lax.rsqrt(tot[:, 1:2] - mean_z * mean_z + eps_norm)
    z_hat = (z - mean_z) * inv_z
    post_out = z_hat * post_gain_ref[...] + post_bias_ref[...]
    gated[...] = (post_out * gate_act).astype(bf16)

    def spread_rows(make, mine, got, send, recv):
        pending = None
        for d, peer in peers:
            mine[d - 1] = make(rows_of(peer)).astype(bf16)
            if pending is not None:
                pending.start()
            pending = push_head(mine.at[d - 1], got.at[d - 1], send.at[d - 1], recv.at[d - 1], peer)
        own = make(rows_of(me))
        pending.start()
        return own

    def add_rows(own, mine, got, send, recv):
        for d, peer in peers:
            push_head(mine.at[d - 1], got.at[d - 1], send.at[d - 1], recv.at[d - 1], peer).wait()
            own = own + got[d - 1].astype(f32)
        return own

    def gather_rows(all_ref, send, recv):
        for d, peer in peers:
            view = all_ref.at[rows_of(me), :]
            push_head(view, view, send.at[d - 1], recv.at[d - 1], peer).start()

    def gather_wait(all_ref, send, recv):
        for d, peer in peers:
            view = all_ref.at[rows_of(me), :]
            push_head(view, view, send.at[d - 1], recv.at[d - 1], peer).wait_send()
            await_bytes(all_ref.at[rows_of(lax.rem(me + count - d, count)), :], recv.at[d - 1])

    def turn_columns(value, mine, all_ref, send, recv):
        for b in range(count):
            mine[b] = value[:, b * cols : (b + 1) * cols]
        all_ref[rows_of(me), :] = mine[me]

    def turn_start(mine, all_ref, send, recv):
        for d, peer in peers:
            push_head(mine.at[peer], all_ref.at[rows_of(me), :], send.at[d - 1], recv.at[d - 1], peer).start()

    def turn_wait(mine, all_ref, send, recv):
        for d, peer in peers:
            push_head(mine.at[peer], all_ref.at[rows_of(me), :], send.at[d - 1], recv.at[d - 1], peer).wait_send()
            await_bytes(all_ref.at[rows_of(lax.rem(me + count - d, count)), :], recv.at[d - 1])

    w_out = w_out_ref[...]
    own = spread_rows(lambda r: dot_nn(gated[r, :], w_out), pa_mine, pa_got, pa_s, pa_r)
    res = x_ref[rows_of(me), :].astype(f32) + add_rows(own, pa_mine, pa_got, pa_s, pa_r)
    rms_two = lax.rsqrt(mean_row(res * res) + eps_norm)
    ffn_gain = ffn_gain_ref[...]
    nt_all[rows_of(me), :] = (res * rms_two * ffn_gain).astype(bf16)
    turn_columns(res, rc_mine, rc_all, rc_s, rc_r)
    resid[...] = res
    gather_rows(nt_all, nt_s, nt_r)
    turn_start(rc_mine, rc_all, rc_s, rc_r)
    gather_wait(nt_all, nt_s, nt_r)
    def forward_rows(b, _):
        r = pl.ds(pl.multiple_of(b * part, part), part)
        nt = nt_all[r, :]
        gate_val = dot_nn(nt, w_gate_ref[...])
        up_val = dot_nn(nt, w_up_ref[...])
        sig = 1.0 / (1.0 + jnp.exp(-gate_val))
        silu = gate_val * sig
        hidden[r, :] = (silu * up_val).astype(bf16)
        g = gh[r, :]
        ggv[r, :] = (g * up_val * sig * (1.0 + gate_val * (1.0 - sig))).astype(bf16)
        guv[r, :] = (g * silu).astype(bf16)
        return 0

    lax.fori_loop(0, count, forward_rows, 0)
    own = spread_rows(lambda r: dot_nt(ggv[r, :], w_gate_ref[...]) + dot_nt(guv[r, :], w_up_ref[...]),
                      gn_mine, gn_got, gn_s, gn_r)
    for b in range(count):
        r = pl.ds(b * part, part)
        down = dot_nn(hidden[r, :], w_down_ref[...]).astype(bf16)
        for c in range(count):
            dn_mine[c, r, :] = down[:, c * cols : (c + 1) * cols]
    ffn = w_gate_ref.shape[1]
    half = full // 2
    for b in range(2):
        r = slice(b * half, (b + 1) * half)
        early_ref[r, 0:ffn] = dot_tn(nt_all[:, r], ggv[...]).astype(bf16)
    for d, peer in peers:
        push_head(dn_mine.at[peer], dn_got.at[d - 1], dn_s.at[d - 1], dn_r.at[d - 1], peer).start()
    gnt = add_rows(own, gn_mine, gn_got, gn_s, gn_r)
    res = resid[...]
    rms_two = lax.rsqrt(mean_row(res * res) + eps_norm)
    scaled = gnt * ffn_gain
    grad_res = ct_ref[rows_of(me), :].astype(f32) + rms_two * (
        scaled - res * rms_two * rms_two * mean_row(scaled * res))
    gov_all[rows_of(me), :] = grad_res.astype(bf16)
    gt_mine[...] = jnp.broadcast_to(jnp.sum(gnt * res * rms_two, axis=0, keepdims=True), gt_mine.shape)
    turn_columns(grad_res, gc_mine, gc_all, gc_s, gc_r)
    gather_rows(gov_all, go_s, go_r)
    turn_start(gc_mine, gc_all, gc_s, gc_r)
    send_all(gt_mine, gt_got, gt_s, gt_r)
    for b in range(2):
        r = slice(b * half, (b + 1) * half)
        early_ref[r, ffn : 2 * ffn] = dot_tn(nt_all[:, r], guv[...]).astype(bf16)
    gather_wait(gov_all, go_s, go_r)
    gov = gov_all[...]
    grad_gated = dot_nt(gov, w_out_ref[...])
    grad_post = grad_gated * gate_act
    grad_zhat = grad_post * post_gain_ref[...]
    sb_mine[...] = row_totals(grad_zhat, grad_zhat * z_hat)
    ggp = (grad_gated * post_out * gate_der).astype(bf16)
    ggp_ref[...] = ggp
    send_all(sb_mine, sb_got, sb_s, sb_r)
    early_ref[:, 3 * ffn : 3 * ffn + 2 * cols] = jnp.concatenate(
        [dot_tn(normed_ref[...], ggp).astype(bf16), dot_tn(gov, gated[...]).astype(bf16)], axis=1)
    row = lax.broadcasted_iota(jnp.int32, (8, cols), 0)
    wait_all(sb_mine, sb_got, sb_s, sb_r)
    tot = sb_mine[...]
    for d, _ in peers:
        tot = tot + sb_got[d - 1]
    tot = tot.T * (1.0 / full)
    grad_mixed = (inv_z * (grad_zhat - tot[:, 0:1] - z_hat * tot[:, 1:2])).astype(bf16)
    for j in range(heads):
        gm_ref[j] = grad_mixed[:, j * width : (j + 1) * width]
    for b in range(2):
        r = slice(b * half, (b + 1) * half)
        early_ref[r, 2 * ffn : 3 * ffn] = dot_tn(ct_ref[:, r], hidden[...]).astype(bf16)
    turn_wait(rc_mine, rc_all, rc_s, rc_r)
    out = rc_all[...] + dn_mine[me].astype(f32)
    for d, peer in peers:
        push_head(dn_mine.at[peer], dn_got.at[d - 1], dn_s.at[d - 1], dn_r.at[d - 1], peer).wait()
        out = out + dn_got[d - 1].astype(f32)
    out_ref[...] = out
    turn_wait(gc_mine, gc_all, gc_s, gc_r)
    grc_ref[...] = gc_all[...]
    wait_all(gt_mine, gt_got, gt_s, gt_r)
    gain_two = gt_mine[...]
    for d, _ in peers:
        gain_two = gain_two + gt_got[d - 1]
    post = jnp.where(row == 1, jnp.sum(grad_post * z_hat, axis=0, keepdims=True),
                     jnp.sum(grad_post, axis=0, keepdims=True))
    line = lax.broadcasted_iota(jnp.int32, (8, full), 0)
    small_ref[...] = jnp.where(
        line == 0, gain_two, jnp.concatenate([post] + [jnp.zeros_like(post)] * (count - 1), axis=1))


def middle(mixed, x, ct, gate_pre, normed, w_out, w_gate, w_up, w_down, post_gain, post_bias, ffn_gain):
    count = lax.axis_size("head")
    heads, rows, width = mixed.shape
    cols = heads * width
    full = cols * count
    part = rows // count
    ffn = w_gate.shape[1]
    ins = (mixed, x, ct, gate_pre, normed, w_out, w_gate, w_up, w_down, post_gain, post_bias, ffn_gain)
    vmem = pl.BlockSpec(memory_space=pltpu.VMEM)
    V = pltpu.VMEM
    trio = count - 1
    sem = pltpu.SemaphoreType.DMA((trio,))
    return pl.pallas_call(
        functools.partial(mid_kernel, count),
        in_specs=[vmem] * len(ins),
        out_specs=[vmem] * 6,
        out_shape=[jax.ShapeDtypeStruct((heads, rows, width), bf16),
                   jax.ShapeDtypeStruct((full, 3 * ffn + 2 * cols), bf16),
                   jax.ShapeDtypeStruct((rows, cols), bf16),
                   jax.ShapeDtypeStruct((rows, cols), f32),
                   jax.ShapeDtypeStruct((rows, cols), f32),
                   jax.ShapeDtypeStruct((8, full), f32)],
        scratch_shapes=[
            V((8, rows), f32), V((trio, 8, rows), f32),
            V((trio, part, full), bf16), V((trio, part, full), bf16),
            V((rows, full), bf16),
            V((count, part, cols), f32), V((rows, cols), f32),
            V((trio, part, full), bf16), V((trio, part, full), bf16),
            V((count, rows, cols), bf16), V((trio, rows, cols), bf16),
            V((rows, full), bf16),
            V((count, part, cols), f32), V((rows, cols), f32),
            V((8, rows), f32), V((trio, 8, rows), f32),
            V((8, full), f32), V((trio, 8, full), f32),
            V((rows, ffn), f32), V((rows, cols), bf16),
            V((rows, ffn), bf16), V((rows, ffn), bf16), V((rows, ffn), bf16),
            V((part, full), f32)] + [sem] * 20,
        compiler_params=pltpu.CompilerParams(
            collective_id=2, has_side_effects=True, vmem_limit_bytes=56 * 1024 * 1024),
        name="middle",
    )(*ins)


def stretch_groups(axis):
    count = lax.axis_size(axis)
    return [[start + step for step in range(0, count, CHAIN)] for start in range(CHAIN)]


def bf_product(form, left, right):
    return jnp.einsum(form, left, right, preferred_element_type=f32)


def local(
    inputs,
    pre_gain,
    w_query,
    w_key,
    w_value,
    mix_gate,
    w_rate,
    rate_bias,
    inner_gain,
    inner_bias,
    init_w_one,
    init_b_one,
    init_w_two,
    init_b_two,
    post_gain,
    post_bias,
    w_out,
    ffn_gain,
    w_gate,
    w_up,
    w_down,
    cotangent,
):
    full_width = pre_gain.shape[0]
    rows, local_cols = inputs.shape
    heads, head_dim = inner_gain.shape
    head_index = lax.axis_index("head")
    position = lax.axis_index("seq") % CHAIN
    whole_low = lax.all_gather(inputs, "head", axis=1, tiled=True)
    whole_in = whole_low.astype(f32)
    grad_whole = lax.all_gather(cotangent, "head", axis=1, tiled=True)
    rms_one = lax.rsqrt(jnp.mean(whole_in * whole_in, axis=1, keepdims=True) + eps_norm)
    normed_one = (whole_in * rms_one * pre_gain).astype(bf16)
    stretches = lax.axis_size("seq") // CHAIN
    spare = PACK - 3 * head_dim

    def by_head(weight):
        return weight.reshape(full_width, heads, -1)

    rate_cols = by_head(w_rate)
    packed_w = jnp.concatenate(
        [by_head(w_query), by_head(w_key), by_head(w_value), rate_cols, rate_cols,
         jnp.zeros((full_width, heads, spare - 2), bf16)], axis=2).reshape(full_width, heads * PACK)
    lane = lax.broadcasted_iota(jnp.int32, (1, heads, PACK), 2)
    rate_lane = (lane == 3 * head_dim) | (lane == 3 * head_dim + 1)
    packed_bias = jnp.where(rate_lane, rate_bias[None, :, None], 0.0).reshape(1, heads * PACK)
    low_lane = (lane == 3 * head_dim + 1).reshape(1, heads * PACK)
    pre = bf_product("rd,dc->rc", normed_one, packed_w) + packed_bias
    payload = (pre - jnp.where(low_lane, lax.reduce_precision(pre, 8, 7), 0.0)).astype(bf16)
    gate_pre = bf_product("rd,dc->rc", normed_one, mix_gate)
    mixed_h, *saved = chain_forward(
        payload, init_w_one, init_b_one, init_w_two, init_b_two, inner_gain, inner_bias)
    grad_mixed, early, grad_gate_pre, outputs, grad_resid_cols, small = middle(
        mixed_h, whole_low, grad_whole, gate_pre, normed_one, w_out, w_gate, w_up, w_down,
        post_gain[None], post_bias[None], ffn_gain[None])
    share = full_width // CHAIN
    grads, ends, early_sum, normed_cols = chain_backward(
        grad_mixed,
        early.reshape(CHAIN, share, early.shape[1]),
        normed_one.reshape(rows, CHAIN, share).transpose(1, 0, 2), inner_gain, inner_bias, saved)
    wide = 3 * head_dim
    late = bf_product("tc,jtk->jck", normed_cols.reshape(CHAIN * rows, share), grads[:, :, :wide])
    back = lax.dynamic_slice_in_dim(grads, position * rows, rows, 1)

    def join_heads(lo, hi):
        return back[:, :, lo:hi].transpose(1, 0, 2).reshape(rows, -1)

    grad_q_low = join_heads(0, head_dim)
    grad_k_low = join_heads(head_dim, 2 * head_dim)
    grad_v_low = join_heads(2 * head_dim, 3 * head_dim)
    grad_logits = join_heads(3 * head_dim, 3 * head_dim + 1).astype(f32) + join_heads(
        3 * head_dim + 1, 3 * head_dim + 2).astype(f32)
    rate_bias_term = jnp.sum(grad_logits, axis=0)
    grad_logit_low = grad_logits.astype(bf16)
    rate_weight_term = bf_product("rd,rc->dc", normed_one, grad_logit_low)
    grad_normed_one = (
        bf_product("rc,dc->rd", grad_q_low, w_query)
        + bf_product("rc,dc->rd", grad_k_low, w_key)
        + bf_product("rc,dc->rd", grad_v_low, w_value)
        + bf_product("rc,dc->rd", grad_gate_pre, mix_gate)
        + bf_product("rc,dc->rd", grad_logit_low, w_rate)
    )
    scaled_one = grad_normed_one * pre_gain
    input_back = rms_one * (
        scaled_one
        - whole_in * rms_one * rms_one * jnp.mean(scaled_one * whole_in, axis=1, keepdims=True)
    )
    gain_one_term = jnp.sum(grad_normed_one * whole_in * rms_one, axis=0)
    input_local = lax.psum_scatter(
        input_back.astype(bf16), "head", scatter_dimension=1, tiled=True).astype(f32)
    grad_inputs = grad_resid_cols + input_local
    ends = ends.astype(f32)
    hidden = ends.shape[2]
    late = late.reshape(heads, share, 3, head_dim).transpose(2, 1, 0, 3).reshape(3, share, local_cols)
    if stretches > 1:
        ends = lax.psum(ends, "seq", axis_index_groups=stretch_groups("seq"))
        seq_index = lax.axis_index("seq")

        def spread(mine_rows):
            summed = lax.psum(mine_rows, "seq", axis_index_groups=stretch_groups("seq"))
            total = lax.all_gather(
                summed, "seq", axis=summed.ndim - 2, tiled=True,
                axis_index_groups=[list(range(s, s + CHAIN)) for s in range(0, stretches * CHAIN, CHAIN)])
            return lax.dynamic_slice_in_dim(
                total, seq_index * (share // stretches), share // stretches, summed.ndim - 2)

        late = spread(late)
        early_sum = spread(early_sum)
    end_two = ends[:, AUG : AUG + head_dim]
    tails = ends[:, AUG + head_dim :, :head_dim]
    grad_one = ends[:, :head_dim]
    grad_b_one = ends[:, head_dim]
    grad_two = (end_two - jnp.mean(end_two, axis=1, keepdims=True)).transpose(0, 2, 1)
    grad_b_two = tails[:, 0] - jnp.mean(tails[:, 0], axis=1, keepdims=True)
    grad_gain = tails[:, 1]
    grad_bias = tails[:, 2]
    flat = lax.psum(
        jnp.concatenate([small[1, :local_cols], small[2, :local_cols], rate_weight_term.reshape(-1), rate_bias_term]), "seq")
    at = 0

    def take(shape):
        nonlocal at
        size = 1
        for extent in shape:
            size *= extent
        at += size
        return flat[at - size : at].reshape(shape)

    grad_post_gain = take((local_cols,))
    grad_post_bias = take((local_cols,))
    grad_rate_w = take((full_width, heads))
    grad_rate_b = take((heads,))
    gain_both = lax.psum(
        jnp.concatenate([gain_one_term, small[0] / lax.axis_size("head")]), ("seq", "head"))
    gain_one = lax.dynamic_slice_in_dim(gain_both, head_index * local_cols, local_cols, 0)
    gain_two = gain_both[full_width:]
    ffn = w_gate.shape[1]
    return (
        outputs,
        grad_inputs,
        gain_one,
        late[0],
        late[1],
        late[2],
        early_sum[:, 3 * ffn : 3 * ffn + local_cols],
        grad_rate_w,
        grad_rate_b,
        grad_gain,
        grad_bias,
        grad_one,
        grad_b_one,
        grad_two,
        grad_b_two,
        grad_post_gain,
        grad_post_bias,
        early_sum[:, 3 * ffn + local_cols :].T,
        gain_two,
        early_sum[:, :ffn],
        early_sum[:, ffn : 2 * ffn],
        early_sum[:, 2 * ffn : 3 * ffn].T,
    )


def solution(mesh):
    in_specs = (
        P("seq", "head"),
        P(),
        P(None, "head"),
        P(None, "head"),
        P(None, "head"),
        P(None, "head"),
        P(None, "head"),
        P("head"),
        P("head", None),
        P("head", None),
        P("head", None, None),
        P("head", None),
        P("head", None, None),
        P("head", None),
        P("head"),
        P("head"),
        P("head", None),
        P(),
        P(None, "head"),
        P(None, "head"),
        P("head", None),
        P("seq", "head"),
    )
    out_specs = (
        P("seq", "head"),
        P("seq", "head"),
        P("head"),
        P("seq", "head"),
        P("seq", "head"),
        P("seq", "head"),
        P("seq", "head"),
        P(None, "head"),
        P("head"),
        P("head", None),
        P("head", None),
        P("head", None, None),
        P("head", None),
        P("head", None, None),
        P("head", None),
        P("head"),
        P("head"),
        P("head", "seq"),
        P(),
        P("seq", "head"),
        P("seq", "head"),
        P("head", "seq"),
    )
    return jax.shard_map(local, mesh=mesh, in_specs=in_specs, out_specs=out_specs, check_vma=False)
```

time: 673 us -> 462 us (0.69)
  waiting for transfers between devices: 261 us -> 0.02 us
  Pallas kernels: 197 us -> 319 us
  local copies, waits for them, and re-layouts: 55.6 us -> 23.7 us
  matrix products: 28.6 us -> 7.18 us
  starting transfers between devices: 15.5 us -> 0.04 us
  other arithmetic: 15.4 us -> 5.59 us
  blocking collectives: 81.9 us -> 90.2 us
    unnamed x11 -> x2, waiting for transfers between devices: 149 us -> 0.02 us
    pallas_call x2 -> x3, Pallas kernels: 197 us -> 319 us  [the longest x1 243 us: chain_backward(): pl.pallas_call(functools.partial(bwd_kernel, block, unroll, heads), grid=...]
    psum x3 -> x0, waiting for transfers between devices: 70.9 us -> none  [the longest x1 32.6 us: local(): resid_sum = lax.psum(resid_back.astype(bf16), 'head').astype(f32)]
    all_to_all x3 -> x0, waiting for transfers between devices: 40.9 us -> none  [the longest x2 23.3 us: to_owners(): lax.all_to_all(padded, 'seq', 0, 0, axis_index_groups=groups_of('seq'), t...]
    psum x3 -> x2, blocking collectives: 49.3 us -> 75.3 us  [the longest x1 38.4 us: local(): lax.psum(jnp.concatenate([small[1, :local_cols], small[2, :local_cols], r...]
    dot_general x27 -> x9, matrix products: 28.6 us -> 7.18 us  [bf_product(): return jnp.einsum(form, left, right, preferred_element_type=f32)]
    all_to_all x1 -> x0, blocking collectives: 18.2 us -> none  [from_owners(): lax.all_to_all(rows_of_head.reshape(CHAIN, total // CHAIN, width), 'seq',...]
    all_to_all x3 -> x0, starting transfers between devices: 15.2 us -> none  [the longest x2 11.5 us: to_owners(): lax.all_to_all(padded, 'seq', 0, 0, axis_index_groups=groups_of('seq'), t...]
  transfers between devices with their start and end apart: 10 -> 1, of which waited for: 9 -> 0; matrix products, arithmetic and copies ran while one was open for 10% -> 4% of each run, Pallas kernels for 18% -> 0%
where the time goes in v2:
time: 462 us; the launch traced here: 461 us
  Pallas kernels  319 us (69%)
  blocking collectives  90.2 us (20%)
  local copies, waits for them, and re-layouts  23.7 us (5%)
  between operations  14.5 us (3%)
  matrix products  7.18 us (2%)
  other arithmetic  5.59 us (1%)
    pallas_call x1, Pallas kernels, chain_backward(): pl.pallas_call(functools.partial(bwd_kernel, block, unroll, heads), grid=...  243 us
    pallas_call x1, Pallas kernels, middle(): pl.pallas_call(functools.partial(mid_kernel, count), in_specs=[vmem] * le...  44.5 us
    psum x1, blocking collectives, local(): lax.psum(jnp.concatenate([small[1, :local_cols], small[2, :local_cols], r...  38.4 us
    psum x1, blocking collectives, local(): lax.psum(jnp.concatenate([gain_one_term, small[0] / lax.axis_size('head')...  36.9 us
    pallas_call x1, Pallas kernels, chain_forward(): pl.pallas_call(functools.partial(fwd_kernel, block, unroll, heads), grid=...  32.4 us
    unnamed x46, local copies, waits for them, and re-layouts  10.3 us
  transfers between devices with their start and end apart: 1, of which 0 were waited for; matrix products, arithmetic and copies ran while one was open for 4% of the time, Pallas kernels for 0%

profile of v2, /device:TPU:0, one launch (start us, length us, event | category | flops | bytes accessed | tf_op | source)
XLA Modules:
  0.0 460.7 jit_solution(13428689810500872587)
XLA Ops:
  7.2 0.0 copy-start
  7.2 0.0 reduce-scatter.4.cloned.1.call-start
  7.3 8.1 %all_gather.6 = bf16[256,768]{0,1:T(8,128)(2,1)S(1)} all-gather(bf16[256,192]{0,1:T(8,128)(2,1)} %param.22), channel_id=1, replica_groups=mesh['seq'=8,'head'=4] {'head'}, dimensions={1}, use_global_device_ids=true | all-gather | bytes 491520 | tf_op jit(solution)/shard_map/all_gather | solution.py:862
  15.4 0.2 copy.80.x_ref
  15.6 0.0 copy-start.7
  15.7 0.2 fusion.9
  15.8 0.9 copy.81
  16.8 0.7 broadcast_reduce_fusion
  17.5 1.9 copy.83.w2_in
  19.4 6.8 %all_gather.7 = bf16[256,768]{0,1:T(8,128)(2,1)S(1)} all-gather(bf16[256,192]{0,1:T(8,128)(2,1)} %param.43), channel_id=1, replica_groups=mesh['seq'=8,'head'=4] {'head'}, dimensions={1}, use_global_device_ids=true | all-gather | bytes 491520 | tf_op jit(solution)/shard_map/all_gather | solution.py:864
  26.2 0.9 copy.85.ct_ref
  27.1 0.2 fusion.4.normed_ref
  27.3 0.2 copy.87
  27.5 1.0 fusion.21.gate_pre_ref
  28.5 0.6 broadcast_in_dim.53.ffn_gain_ref
  29.0 1.0 copy.88
  30.1 1.1 concatenate.9
  31.2 1.3 subtract_convert_fusion.pay_ref
  32.5 32.4 %inner_forward.1 = (bf16[3,256,64]{2,1,0:T(8,128)(2,1)}, bf16[2048,80]{1,0:T(8,128)(2,1)}, bf16[2048,80]{1,0:T(8,128)(2,1)}, f32[2048,128]{1,0:T(8,128)}, bf16[1...) custom-call(bf16[256,768]{1,0:T(8,128)(2,1)} %subtract_convert_fusio, ...), custom_call_target="tpu_custom_call" | custom-call | tf_op jit(solution)/shard_map/inner_forward/pallas_call | solution.py:386
  64.9 44.5 %middle.1 = (bf16[3,256,64]{2,1,0:T(8,128)(2,1)}, bf16[768,1920]{1,0:T(8,128)(2,1)}, bf16[256,192]{1,0:T(8,128)(2,1)}, f32[256,192]{1,0:T(8,128)}, f32[256,192]{1,0:T(8,128)}, /*index=5*/f32[8,768]{1,0:T(8,128)}) custom-call(bf16[3,256,64]{2,1,0:T(8,128)(2,1)} %get-tuple-element.44.mixed_ref, bf16[256,768]{1,0:T(8,128)(2,1)} %copy-done.1, ...), custom_call_target="tpu_custom_call" | custom-call | tf_op jit(solution)/shard_map/middle/pallas_call | solution.py:794
  109.4 242.6 %inner_backward.1 = (bf16[3,2048,256]{2,1,0:T(8,128)(2,1)}, bf16[3,160,256]{2,1,0:T(8,128)(2,1)}, f32[96,1920]{1,0:T(8,128)}, bf16[8,256,96]{2,1,0:T(8,128)(2,1)}) custom-call(bf16[3,256,64]{2,1,0:T(8,128)(2,1)} %get-tuple-element.47.gm_ref, bf16[8,96,1920]{2,1,0:T(8,128)(2,1)} %bitcast.71, bf16[8,256,96]{2,1,0:T(8,128)(2,1)} %bitcast.72, f32[3,64]{1,0:T(4,128)} %gain_in.3, ...), custom_call_target="tpu_custom_call" | custom-call | tf_op jit(solution)/shard_map/inner_backward/pallas_call | solution.py:550
  352.0 1.3 dynamic-slice_bitcast_fusion
  353.3 0.1 copy.89
  353.4 0.3 fusion.22
  353.7 0.1 copy.90
  353.9 0.1 copy.91
  354.0 0.3 convolution_add_fusion.3
  354.3 0.3 convolution_add_fusion.2
  354.7 0.3 convolution_add_fusion.1
  354.9 1.4 fusion.16
  356.3 0.5 fusion.12
  356.9 0.2 fusion.8
  357.1 0.9 copy.108
  358.1 0.0 reduce-scatter.4.cloned.1.call-update
  358.1 0.8 multiply_reduce_fusion
  358.8 0.8 fusion.19
  359.6 0.3 fusion.23
  359.9 1.3 fusion.13
  361.3 0.2 reshape.168
  361.5 0.1 concatenate.11
  361.6 38.4 %psum.15 = f32[2691]{0:T(1024)S(1)} all-reduce(f32[2691]{0:T(1024)S(1)} %concatenate.11), channel_id=1, replica_groups=mesh['seq'=8,'head'=4] {'seq'}, use_global_device_ids=true, to_apply=%region_6.7 | all-reduce | flops 2691 | bytes 21528 | tf_op jit(solution)/shard_map/psum | solution.py:950
  399.9 0.5 slice.132
  400.5 0.7 slice.135
  401.2 0.1 slice_reduce_fusion.1
  401.3 0.6 fusion.20
  402.0 0.8 copy.96
  402.8 3.0 fusion
  405.8 0.7 slice_bitcast_fusion.1
  406.5 0.7 bitcast_subtract_fusion
  407.2 36.9 %psum.14 = f32[1536]{0:T(1024)S(1)} all-reduce(f32[1536]{0:T(1024)S(1)} %pad_maximum_fusion), channel_id=1, replica_groups=mesh['seq'=8,'head'=4] {'seq','head'}, use_global_device_ids=true, to_apply=%region_4.5 | all-reduce | flops 1536 | bytes 12288 | tf_op jit(solution)/shard_map/psum | solution.py:966
  444.1 0.6 slice.141
  444.7 0.6 dynamic_slice.7
  445.3 0.7 copy.98
  446.0 0.7 copy.99
  446.8 0.7 copy.100
  447.5 0.3 reshape.169
  447.8 0.8 copy.101
  448.5 0.6 copy.120
  449.1 0.7 copy.102
  449.9 0.6 copy_bitcast_fusion.2
  450.5 0.7 subtract_bitcast_fusion
  451.1 0.8 slice_bitcast_fusion
  452.0 1.0 copy.109
  453.0 0.8 copy.97
  (55 shorter events, 0.3 us)
Async XLA Ops:
  7.2 20.3 %copy-start = (bf16[768,192]{0,1:T(8,128)(2,1)S(1)}, bf16[768,192]{0,1:T(8,128)(2,1)}, u32[]{:S(2)}) copy-start(bf16[768,192]{0,1:T(8,128)(2,1)} %param.27) | copy-start | bytes 884740
  7.2 19.9 %copy-start.13 = (f32[768]{0:T(1024)S(1)}, f32[768]{0:T(1024)}, u32[]{:S(2)}) copy-start(f32[768]{0:T(1024)} %param.23) | copy-start | bytes 9220
  7.2 21.2 %copy-start.15 = (f32[768]{0:T(1024)S(1)}, f32[768]{0:T(1024)}, u32[]{:S(2)}) copy-start(f32[768]{0:T(1024)} %param.39) | copy-start | bytes 9220
  7.2 444.7 %reduce-scatter.4.cloned.1.call-start = ((), (), s32[]{:S(2)}) async-start(), calls=%async_computation.1 | async-start | bytes 491520
  15.6 15.6 %copy-start.1 = (bf16[256,768]{1,0:T(8,128)(2,1)}, bf16[256,768]{1,0:T(8,128)(2,1)S(1)}, u32[]{:S(2)}) copy-start(bf16[256,768]{1,0:T(8,128)(2,1)S(1)} %copy.80.x_ref) | copy-start | bytes 1179652
  15.6 14.4 %copy-start.5 = (bf16[768,192]{0,1:T(8,128)(2,1)S(1)}, bf16[768,192]{0,1:T(8,128)(2,1)}, u32[]{:S(2)}) copy-start(bf16[768,192]{0,1:T(8,128)(2,1)} %param.24) | copy-start | bytes 884740
  15.6 14.4 %copy-start.6 = (bf16[768,192]{0,1:T(8,128)(2,1)S(1)}, bf16[768,192]{0,1:T(8,128)(2,1)}, u32[]{:S(2)}) copy-start(bf16[768,192]{0,1:T(8,128)(2,1)} %param.25) | copy-start | bytes 884740
  15.6 14.4 %copy-start.7 = (bf16[768,192]{0,1:T(8,128)(2,1)S(1)}, bf16[768,192]{0,1:T(8,128)(2,1)}, u32[]{:S(2)}) copy-start(bf16[768,192]{0,1:T(8,128)(2,1)} %param.26) | copy-start | bytes 884740
  27.3 5.2 %copy-start.3 = (bf16[256,768]{1,0:T(8,128)(2,1)}, bf16[256,768]{1,0:T(8,128)(2,1)S(1)}, u32[]{:S(2)}) copy-start(bf16[256,768]{1,0:T(8,128)(2,1)S(1)} %fusion.4.normed_ref) | copy-start | bytes 1179652
  353.3 1.3 copy-start.12
  354.0 2.3 copy-start.2
  354.0 2.3 copy-start.14
  354.6 5.0 %copy-start.4 = (bf16[256,768]{1,0:T(8,128)(2,1)S(1)}, bf16[256,768]{1,0:T(8,128)(2,1)}, u32[]{:S(2)}) copy-start(bf16[256,768]{1,0:T(8,128)(2,1)} %copy-done.3) | copy-start | bytes 1179652
  356.3 44.2 %copy-start.9 = (bf16[3,160,256]{2,1,0:T(8,128)(2,1)S(1)}, bf16[3,160,256]{2,1,0:T(8,128)(2,1)}, u32[]{:S(2)}) copy-start(bf16[3,160,256]{2,1,0:T(8,128)(2,1)} %get-tuple-element.65) | copy-start | bytes 737284
  356.9 45.1 %copy-start.10 = (f32[256,192]{1,0:T(8,128)S(1)}, f32[256,192]{1,0:T(8,128)}, u32[]{:S(2)}) copy-start(f32[256,192]{1,0:T(8,128)} %get-tuple-element.110) | copy-start | bytes 589828
  356.9 45.9 %copy-start.16 = (bf16[8,256,96]{2,1,0:T(8,128)(2,1)S(1)}, bf16[8,256,96]{2,1,0:T(8,128)(2,1)}, u32[]{:S(2)}) copy-start(bf16[8,256,96]{2,1,0:T(8,128)(2,1)} %get-tuple-element.63) | copy-start | bytes 1179652
  402.8 3.1 copy-start.8
  405.8 47.2 %copy-start.11 = (f32[256,192]{1,0:T(8,128)S(1)}, f32[256,192]{1,0:T(8,128)}, u32[]{:S(2)}) copy-start(f32[256,192]{1,0:T(8,128)} %get-tuple-element.46) | copy-start | bytes 589828
Sparse Core Ops, SparseCore 0:
  358.2 23.5 reduce-scatter.3

commit v3 on v2

--- a/solution.py
+++ b/solution.py
@@ -232,10 +232,10 @@
     await_bytes(dst.at[pos], local_sem)
 
 
-def fwd_kernel(block, unroll, heads, pay_ref, w1_in, b1_in, w2_in, b2_in, gain_in, bias_in,
-               mixed_ref, k_out, q_out, aux_out, w1s_ref, w2s_ref, z1s_ref, upd_ref, zc_ref, s2_ref, z1b_ref, z2b_ref,
+def fwd_kernel(block, unroll, heads, pay_ref, norm_ref, w1_in, b1_in, w2_in, b2_in, gain_in, bias_in,
+               mixed_ref, norm_out, k_out, q_out, aux_out, w1s_ref, w2s_ref, z1s_ref, upd_ref, zc_ref, s2_ref, z1b_ref, z2b_ref,
                got, k_all, q_all, base_all, aux_all, mixed_all, w1, w2t, b2, z1,
-               pay_send, pay_recv, mix_send, mix_recv):
+               pay_send, pay_recv, mix_send, mix_recv, no_send, no_recv, no_loc):
     blk = pl.program_id(0)
     last = pl.num_programs(0) - 1
     pos, base = seq_place()
@@ -264,6 +264,8 @@
             @pl.when(pos == FIRST + j)
             def _():
                 pltpu.make_async_copy(src, dst, pay_recv.at[pos]).start()
+
+        swap_start(norm_ref, norm_out, no_send, no_recv, no_loc, pos, base)
 
     def take_in(p):
         await_bytes(got.at[p], pay_recv.at[p])
@@ -361,6 +363,7 @@
             others = mixed_all.at[pl.ds(0, (CHAIN - 1) * rows_each), :]
             await_bytes(others, mix_send)
 
+        swap_wait(norm_ref, norm_out, no_send, no_recv, no_loc, pos, base)
         for j in range(heads):
             @pl.when(pos != FIRST + j)
             def _():
@@ -369,7 +372,7 @@
             await_bytes(mixed_ref.at[j], mix_recv.at[j])
 
 
-def chain_forward(payload, w1, b1, w2, b2, gain, bias, block=128, unroll=8):
+def chain_forward(payload, normed, w1, b1, w2, b2, gain, bias, block=128, unroll=8):
     rows = payload.shape[0]
     heads, width, hidden = w1.shape
     tokens = rows * CHAIN
@@ -386,10 +389,11 @@
     return pl.pallas_call(
         functools.partial(fwd_kernel, block, unroll, heads),
         grid=(tokens // block,),
-        in_specs=[anywhere] + [whole(a) for a in small],
-        out_specs=[anywhere, rowblk(AUG), rowblk(AUG), rowblk(2 * width), stepblk(AUG), stepblk(width),
+        in_specs=[anywhere, anywhere] + [whole(a) for a in small],
+        out_specs=[anywhere, anywhere, rowblk(AUG), rowblk(AUG), rowblk(2 * width), stepblk(AUG), stepblk(width),
                    rowblk(hidden), rowblk(hidden), rowblk(width), rowblk(width), rowblk(hidden), rowblk(width)],
         out_shape=[jax.ShapeDtypeStruct((heads, rows, width), bf16),
+                   jax.ShapeDtypeStruct(normed.shape, bf16),
                    jax.ShapeDtypeStruct((tokens, AUG), bf16),
                    jax.ShapeDtypeStruct((tokens, AUG), bf16),
                    jax.ShapeDtypeStruct((tokens, 2 * width), f32),
@@ -402,17 +406,18 @@
                         pltpu.VMEM((tokens, width), bf16),
                         pltpu.VMEM((AUG, hidden), f32), pltpu.VMEM((width, hidden), f32),
                         pltpu.VMEM((1, width), f32), pltpu.VMEM((MINI, hidden), f32),
-                        dma((heads,)), dma((CHAIN,)), dma, dma((heads,))],
+                        dma((heads,)), dma((CHAIN,)), dma, dma((heads,)),
+                        dma((CHAIN - 1,)), dma((CHAIN - 1,)), dma],
         compiler_params=pltpu.CompilerParams(collective_id=0, has_side_effects=True),
         name="inner_forward",
-    )(payload, *small)
-
-
-def bwd_kernel(block, unroll, heads, gm_ref, early_ref, norm_ref, gain_in, bias_in,
+    )(payload, normed, *small)
+
+
+def bwd_kernel(block, unroll, heads, turn, gm_ref, early_ref, small_ref, gain_in, bias_in,
                k_ref, q_ref, aux_ref, w1s_ref, w2s_ref, z1s_ref, upd_ref, zc_ref, s2_ref, z1b_ref, z2b_ref,
-               grads_ref, ends_ref, early_out, norm_out,
-               dout, early_got, packed, ends, p1, p2t, p2, dg, db,
-               gm_send, gm_recv, ea_send, ea_recv, ea_loc, no_send, no_recv, no_loc, bc_send, bc_recv, en_send, en_recv):
+               grads_ref, ends_ref, early_out, small_out,
+               dout, half_got, half_mine, quarter, quarter_got, packed, ends, p1, p2t, p2, dg, db,
+               gm_send, gm_recv, ha_send, ha_recv, ha_loc, qu_send, qu_recv, sm_send, sm_recv, sm_loc, bc_send, bc_recv, en_send, en_recv):
     pid = pl.program_id(0)
     last = pl.num_programs(0) - 1
     blk = last - pid
@@ -427,6 +432,9 @@
     gain_sq = gain * gain
     tri = tri_mask()
     count = block // MINI
+    side = lax.rem(pos, 2)
+    rank = lax.div(pos, 2)
+    partner = pos + 1 - 2 * side
 
     @pl.when(pid == 0)
     def _():
@@ -440,8 +448,29 @@
             def _():
                 pltpu.make_async_copy(gm_ref.at[j], dout.at[pos], gm_recv.at[pos]).start()
 
-        swap_start(early_ref, early_got, ea_send, ea_recv, ea_loc, pos, base)
-        swap_start(norm_ref, norm_out, no_send, no_recv, no_loc, pos, base)
+        for d in range(1, CHAIN):
+            push(small_ref, small_out.at[pos], sm_send.at[d - 1], sm_recv.at[d - 1],
+                 base + lax.rem(pos + d, CHAIN)).start()
+        pltpu.make_async_copy(small_ref, small_out.at[pos], sm_loc).start()
+        push(early_ref.at[:, 1 - side], half_got, ha_send, ha_recv, base + partner).start()
+        pltpu.make_async_copy(early_ref.at[:, side], half_mine, ha_loc).start()
+
+    @pl.when(pid == turn)
+    def _():
+        push(early_ref.at[:, 1 - side], half_got, ha_send, ha_recv, base + partner).wait()
+        await_bytes(half_mine, ha_loc)
+
+        def pair_up(c, _):
+            rows = pl.ds(pl.multiple_of(c * MINI, MINI), MINI)
+            for r in range(CHAIN // 2):
+                quarter[r, rows, :] = (half_mine[r, rows, :].astype(f32) + half_got[r, rows, :].astype(f32)).astype(bf16)
+            return 0
+
+        lax.fori_loop(0, half_mine.shape[1] // MINI, pair_up, 0)
+        for d in range(1, CHAIN // 2):
+            other = lax.rem(rank + d, CHAIN // 2)
+            push(quarter.at[other], quarter_got.at[d - 1], qu_send.at[d - 1], qu_recv.at[d - 1],
+                 base + 2 * other + side).start()
 
     def share_block(b):
         rows = pl.ds(pl.multiple_of(b * block, block), block)
@@ -507,14 +536,21 @@
 
     @pl.when(pid == last)
     def _():
-        swap_wait(early_ref, early_got, ea_send, ea_recv, ea_loc, pos, base)
-        swap_wait(norm_ref, norm_out, no_send, no_recv, no_loc, pos, base)
+        for d in range(1, CHAIN // 2):
+            other = lax.rem(rank + d, CHAIN // 2)
+            push(quarter.at[other], quarter_got.at[d - 1], qu_send.at[d - 1], qu_recv.at[d - 1],
+                 base + 2 * other + side).wait()
+        for d in range(1, CHAIN):
+            push(small_ref, small_out.at[pos], sm_send.at[d - 1], sm_recv.at[d - 1],
+                 base + lax.rem(pos + d, CHAIN)).wait_send()
+            await_bytes(small_out.at[lax.rem(pos + CHAIN - d, CHAIN)], sm_recv.at[d - 1])
+        await_bytes(small_out.at[pos], sm_loc)
 
         def add_up(c, _):
             rows = pl.ds(pl.multiple_of(c * MINI, MINI), MINI)
-            acc = early_got[0, rows, :].astype(f32)
-            for p in range(1, CHAIN):
-                acc = acc + early_got[p, rows, :].astype(f32)
+            acc = quarter[rank, rows, :].astype(f32)
+            for d in range(1, CHAIN // 2):
+                acc = acc + quarter_got[d - 1, rows, :].astype(f32)
             early_out[rows, :] = acc
             return 0
 
@@ -534,7 +570,7 @@
                 await_bytes(ends, en_send.at[d - 1])
 
 
-def chain_backward(grad_mixed, early, normed, gain, bias, saved, block=128, unroll=4):
+def chain_backward(grad_mixed, early, small, gain, bias, saved, block=128, unroll=4, turn=6):
     heads, rows, width = grad_mixed.shape
     tokens = rows * CHAIN
     hidden = saved[5].shape[1]
@@ -546,9 +582,10 @@
     anywhere = pl.BlockSpec(memory_space=pl.ANY)
     dma = pltpu.SemaphoreType.DMA
     seven = dma((CHAIN - 1,))
-    share = early.shape[1:]
+    share = early.shape[2:]
+    three = dma((CHAIN // 2 - 1,))
     return pl.pallas_call(
-        functools.partial(bwd_kernel, block, unroll, heads),
+        functools.partial(bwd_kernel, block, unroll, heads, turn),
         grid=(nblk,),
         in_specs=[anywhere] * 3 + [whole(gain), whole(bias), rowblk(AUG), rowblk(AUG), rowblk(2 * width),
                                    stepblk(AUG), stepblk(width), rowblk(hidden), rowblk(hidden), rowblk(width),
@@ -557,16 +594,18 @@
         out_shape=[jax.ShapeDtypeStruct((heads, tokens, PACK), bf16),
                    jax.ShapeDtypeStruct((heads, ENDS, hidden), bf16),
                    jax.ShapeDtypeStruct(share, f32),
-                   jax.ShapeDtypeStruct(normed.shape, bf16)],
-        scratch_shapes=[pltpu.VMEM((CHAIN, rows, width), bf16), pltpu.VMEM(early.shape, bf16),
+                   jax.ShapeDtypeStruct((CHAIN,) + small.shape, f32)],
+        scratch_shapes=[pltpu.VMEM((CHAIN, rows, width), bf16), pltpu.VMEM((CHAIN // 2,) + share, bf16),
+                        pltpu.VMEM((CHAIN // 2,) + share, bf16), pltpu.VMEM((CHAIN // 2,) + share, bf16),
+                        pltpu.VMEM((CHAIN // 2 - 1,) + share, bf16),
                         pltpu.VMEM((tokens, PACK), bf16), pltpu.VMEM((ENDS, hidden), bf16),
                         pltpu.VMEM((AUG, hidden), f32), pltpu.VMEM((width, hidden), f32), pltpu.VMEM((1, width), f32),
                         pltpu.VMEM((1, width), f32), pltpu.VMEM((1, width), f32),
-                        dma((heads,)), dma((CHAIN,)), seven, seven, dma, seven, seven, dma,
+                        dma((heads,)), dma((CHAIN,)), dma, dma, dma, three, three, seven, seven, dma,
                         seven, dma((heads,)), seven, dma((heads,))],
         compiler_params=pltpu.CompilerParams(collective_id=1, has_side_effects=True),
         name="inner_backward",
-    )(grad_mixed, early, normed, gain, bias, *saved)
+    )(grad_mixed, early, small, gain, bias, *saved)
 
 
 def head_place():
@@ -600,9 +639,9 @@
 
 def mid_kernel(count, mixed_ref, x_ref, ct_ref, gate_pre_ref, normed_ref, w_out_ref, w_gate_ref, w_up_ref, w_down_ref,
                post_gain_ref, post_bias_ref, ffn_gain_ref,
-               gm_ref, early_ref, ggp_ref, out_ref, grc_ref, small_ref,
+               gm_ref, early_ref, ggp_ref, out_ref, rco_ref, grc_ref, small_ref,
                st_mine, st_got, pa_mine, pa_got, nt_all, rc_mine, rc_all, gn_mine, gn_got, dn_mine, dn_got, gov_all,
-               gc_mine, gc_all, sb_mine, sb_got, gt_mine, gt_got, gh, gated, hidden, ggv, guv, resid,
+               gc_mine, gc_all, sb_mine, sb_got, gt_all, gh, gated, hidden, ggv, guv, resid,
                st_s, st_r, pa_s, pa_r, nt_s, nt_r, rc_s, rc_r, gn_s, gn_r, dn_s, dn_r, go_s, go_r, gc_s, gc_r, sb_s, sb_r,
                gt_s, gt_r):
     me, _ = head_place()
@@ -729,11 +768,12 @@
     grad_res = ct_ref[rows_of(me), :].astype(f32) + rms_two * (
         scaled - res * rms_two * rms_two * mean_row(scaled * res))
     gov_all[rows_of(me), :] = grad_res.astype(bf16)
-    gt_mine[...] = jnp.broadcast_to(jnp.sum(gnt * res * rms_two, axis=0, keepdims=True), gt_mine.shape)
+    gt_all[me] = jnp.broadcast_to(jnp.sum(gnt * res * rms_two, axis=0, keepdims=True), gt_all.shape[1:])
     turn_columns(grad_res, gc_mine, gc_all, gc_s, gc_r)
     gather_rows(gov_all, go_s, go_r)
     turn_start(gc_mine, gc_all, gc_s, gc_r)
-    send_all(gt_mine, gt_got, gt_s, gt_r)
+    for d, peer in peers:
+        push_head(gt_all.at[me], gt_all.at[me], gt_s.at[d - 1], gt_r.at[d - 1], peer).start()
     for b in range(2):
         r = slice(b * half, (b + 1) * half)
         early_ref[r, ffn : 2 * ffn] = dot_tn(nt_all[:, r], guv[...]).astype(bf16)
@@ -761,17 +801,20 @@
         r = slice(b * half, (b + 1) * half)
         early_ref[r, 2 * ffn : 3 * ffn] = dot_tn(ct_ref[:, r], hidden[...]).astype(bf16)
     turn_wait(rc_mine, rc_all, rc_s, rc_r)
-    out = rc_all[...] + dn_mine[me].astype(f32)
+    rco_ref[...] = rc_all[...]
+    out = dn_mine[me].astype(f32)
     for d, peer in peers:
         push_head(dn_mine.at[peer], dn_got.at[d - 1], dn_s.at[d - 1], dn_r.at[d - 1], peer).wait()
         out = out + dn_got[d - 1].astype(f32)
     out_ref[...] = out
     turn_wait(gc_mine, gc_all, gc_s, gc_r)
     grc_ref[...] = gc_all[...]
-    wait_all(gt_mine, gt_got, gt_s, gt_r)
-    gain_two = gt_mine[...]
-    for d, _ in peers:
-        gain_two = gain_two + gt_got[d - 1]
+    for d, peer in peers:
+        push_head(gt_all.at[me], gt_all.at[me], gt_s.at[d - 1], gt_r.at[d - 1], peer).wait_send()
+        await_bytes(gt_all.at[lax.rem(me + count - d, count)], gt_r.at[d - 1])
+    gain_two = gt_all[0]
+    for b in range(1, count):
+        gain_two = gain_two + gt_all[b]
     post = jnp.where(row == 1, jnp.sum(grad_post * z_hat, axis=0, keepdims=True),
                      jnp.sum(grad_post, axis=0, keepdims=True))
     line = lax.broadcasted_iota(jnp.int32, (8, full), 0)
@@ -794,10 +837,11 @@
     return pl.pallas_call(
         functools.partial(mid_kernel, count),
         in_specs=[vmem] * len(ins),
-        out_specs=[vmem] * 6,
+        out_specs=[vmem] * 7,
         out_shape=[jax.ShapeDtypeStruct((heads, rows, width), bf16),
                    jax.ShapeDtypeStruct((full, 3 * ffn + 2 * cols), bf16),
                    jax.ShapeDtypeStruct((rows, cols), bf16),
+                   jax.ShapeDtypeStruct((rows, cols), f32),
                    jax.ShapeDtypeStruct((rows, cols), f32),
                    jax.ShapeDtypeStruct((rows, cols), f32),
                    jax.ShapeDtypeStruct((8, full), f32)],
@@ -811,13 +855,170 @@
             V((rows, full), bf16),
             V((count, part, cols), f32), V((rows, cols), f32),
             V((8, rows), f32), V((trio, 8, rows), f32),
-            V((8, full), f32), V((trio, 8, full), f32),
+            V((count, 8, full), f32),
             V((rows, ffn), f32), V((rows, cols), bf16),
             V((rows, ffn), bf16), V((rows, ffn), bf16), V((rows, ffn), bf16),
             V((part, full), f32)] + [sem] * 20,
         compiler_params=pltpu.CompilerParams(
             collective_id=2, has_side_effects=True, vmem_limit_bytes=56 * 1024 * 1024),
         name="middle",
+    )(*ins)
+
+
+def tail_kernel(count, at_mix, grads_ref, packed_w_ref, mix_gate_ref, ggp_ref, x_ref, pre_gain_ref, cols_ref, early_ref,
+                late_ref, back_ref, tiles_ref,
+                near, mine, got, tile, tile_got, near_sem, ib_s, ib_r, th_s, th_r, ts_s, ts_r, ts_loc):
+    me, _ = head_place()
+    pos, base = seq_place()
+    heads = grads_ref.shape[0]
+    rows = x_ref.shape[0]
+    cols = ggp_ref.shape[1]
+    full = x_ref.shape[1]
+    share = early_ref.shape[0]
+    rate_lane = PACK - PACK // 4
+    peers = [(d, lax.rem(me + d, count)) for d in range(1, count)]
+    barrier = pltpu.get_barrier_semaphore()
+    for d, peer in peers:
+        pl.semaphore_signal(barrier, inc=1, device_id={"head": peer}, device_id_type=MESH)
+    for d in range(1, CHAIN):
+        pl.semaphore_signal(
+            barrier, inc=1, device_id={"seq": base + lax.rem(pos + d, CHAIN)}, device_id_type=MESH)
+    pl.semaphore_wait(barrier, count - 1 + CHAIN - 1)
+    here = pl.ds(pl.multiple_of(pos * rows, rows), rows)
+    part = rows // count
+
+    def back_rows(b, _):
+        r = pl.ds(pl.multiple_of(b * part, part), part)
+        away = pl.ds(pl.multiple_of(pos * rows + b * part, part), part)
+        grad = dot_nt(ggp_ref[r, :], mix_gate_ref[...])
+        for j in range(heads):
+            grad = grad + dot_nt(grads_ref[j, away, :], packed_w_ref[:, j * PACK : (j + 1) * PACK])
+        x = x_ref[r, :].astype(f32)
+        rms = lax.rsqrt(mean_row(x * x) + eps_norm)
+        scaled = grad * pre_gain_ref[...]
+        back = (rms * (scaled - x * rms * rms * mean_row(scaled * x))).astype(bf16)
+        for c in range(count):
+            mine[c, r, :] = back[:, c * cols : (c + 1) * cols]
+        return 0
+
+    lax.fori_loop(0, count, back_rows, 0)
+    turned = cols_ref[...]
+    ones = jnp.ones((MINI, turned.shape[0]), bf16)
+    lane = lax.broadcasted_iota(jnp.int32, (share, 128), 1)
+    spot = lax.broadcasted_iota(jnp.int32, (8, 128), 1)
+    line = lax.broadcasted_iota(jnp.int32, (8, 128), 0)
+    w_rows = pl.ds(pl.multiple_of(pos * share, share), share)
+    gain = jnp.sum(early_ref[:, at_mix : at_mix + cols] * mix_gate_ref[w_rows, :].astype(f32), axis=1, keepdims=True)
+    table = jnp.zeros((share, 128), f32)
+    extra = jnp.zeros((8, 128), f32)
+    for j in range(heads):
+        late = dot_tn(turned, grads_ref[j])
+        late_ref[j] = late
+        gain = gain + jnp.sum(
+            late * packed_w_ref[w_rows, j * PACK : (j + 1) * PACK].astype(f32), axis=1, keepdims=True)
+        rate = late[:, rate_lane : rate_lane + 1] + late[:, rate_lane + 1 : rate_lane + 2]
+        table = jnp.where(lane == j, rate, table)
+        if j == 0:
+            for d, peer in peers:
+                push_head(mine.at[peer], got.at[d - 1], ib_s.at[d - 1], ib_r.at[d - 1], peer).start()
+        total = dot_nn(ones, grads_ref[j])[0:8]
+        total = total[:, rate_lane : rate_lane + 1] + total[:, rate_lane + 1 : rate_lane + 2]
+        extra = jnp.where((line == heads + 1) & (spot == j), total, extra)
+    table = jnp.where(lane == heads, gain, table)
+    flat = jnp.concatenate([table, jnp.zeros((128 - share, 128), f32)], axis=0).T[0:8]
+    tile[...] = flat + extra
+    for d, peer in peers:
+        push_head(tile, tile_got.at[d - 1], th_s.at[d - 1], th_r.at[d - 1], peer).start()
+    back = mine[me].astype(f32)
+    for d, peer in peers:
+        push_head(tile, tile_got.at[d - 1], th_s.at[d - 1], th_r.at[d - 1], peer).wait()
+    summed = flat
+    for d, peer in peers:
+        summed = summed + tile_got[d - 1]
+    tile[...] = jnp.where(line == heads, summed, flat + extra)
+    for d in range(1, CHAIN):
+        push(tile, tiles_ref.at[pos], ts_s.at[d - 1], ts_r.at[d - 1], base + lax.rem(pos + d, CHAIN)).start()
+    pltpu.make_async_copy(tile, tiles_ref.at[pos], ts_loc).start()
+    for d, peer in peers:
+        push_head(mine.at[peer], got.at[d - 1], ib_s.at[d - 1], ib_r.at[d - 1], peer).wait()
+        back = back + got[d - 1].astype(f32)
+    back_ref[...] = back
+    for d in range(1, CHAIN):
+        push(tile, tiles_ref.at[pos], ts_s.at[d - 1], ts_r.at[d - 1], base + lax.rem(pos + d, CHAIN)).wait_send()
+        await_bytes(tiles_ref.at[lax.rem(pos + CHAIN - d, CHAIN)], ts_r.at[d - 1])
+    await_bytes(tiles_ref.at[pos], ts_loc)
+
+
+def tail(at_mix, grads, packed_w, mix_gate, ggp, x, pre_gain, cols, early):
+    count = lax.axis_size("head")
+    heads, tokens, _ = grads.shape
+    rows, full = x.shape
+    width = ggp.shape[1]
+    share = early.shape[0]
+    vmem = pl.BlockSpec(memory_space=pltpu.VMEM)
+    V = pltpu.VMEM
+    dma = pltpu.SemaphoreType.DMA
+    trio, seven = dma((count - 1,)), dma((CHAIN - 1,))
+    return pl.pallas_call(
+        functools.partial(tail_kernel, count, at_mix),
+        in_specs=[vmem] * 8,
+        out_specs=[vmem] * 3,
+        out_shape=[jax.ShapeDtypeStruct((heads, share, PACK), f32),
+                   jax.ShapeDtypeStruct((rows, width), f32),
+                   jax.ShapeDtypeStruct((CHAIN, 8, 128), f32)],
+        scratch_shapes=[V((8, 128), f32), V((count, rows, width), bf16), V((count - 1, rows, width), bf16),
+                        V((8, 128), f32), V((count - 1, 8, 128), f32),
+                        dma, trio, trio, trio, trio, seven, seven, dma],
+        compiler_params=pltpu.CompilerParams(
+            collective_id=3, has_side_effects=True, vmem_limit_bytes=56 * 1024 * 1024),
+        name="tail",
+    )(grads, packed_w, mix_gate, ggp, x, pre_gain, cols, early)
+
+
+def final_kernel(at_mix, ffn, down_ref, resid_ref, back_ref, grc_ref, late_ref, early_ref, ends_ref, tiles_ref, small_ref,
+                 out_ref, gin_ref, gq_ref, gk_ref, gv_ref, gmix_ref, rate_ref, gwout_ref, gwg_ref, gwu_ref, gwd_ref,
+                 w1_ref, b1_ref, w2_ref, b2_ref, ig_ref, ib_ref, vec_ref):
+    heads, width, hidden = w1_ref.shape
+    cols = heads * width
+    out_ref[...] = down_ref[...] + resid_ref[...]
+    gin_ref[...] = back_ref[...] + grc_ref[...]
+    for i, ref in enumerate((gq_ref, gk_ref, gv_ref)):
+        ref[...] = jnp.concatenate([late_ref[j, :, i * width : (i + 1) * width] for j in range(heads)], axis=1)
+    gwg_ref[...] = early_ref[:, 0:ffn]
+    gwu_ref[...] = early_ref[:, ffn : 2 * ffn]
+    gwd_ref[...] = early_ref[:, 2 * ffn : 3 * ffn].T
+    both = early_ref[:, at_mix : at_mix + 2 * cols]
+    gmix_ref[...] = both[:, 0:cols]
+    gwout_ref[...] = both[:, cols:].T
+    for j in range(heads):
+        w1_ref[j] = ends_ref[j, 0:width, :].astype(f32)
+        b1_ref[pl.ds(j, 1), :] = ends_ref[j, width : AUG, :].astype(f32)[0:1]
+        second = ends_ref[j, AUG : AUG + width, :].astype(f32)
+        w2_ref[j] = (second - jnp.mean(second, axis=0, keepdims=True)).T
+        rest = ends_ref[j, AUG + width :, :].astype(f32)[0:8, 0:width]
+        b2_ref[pl.ds(j, 1), :] = rest[0:1] - mean_row(rest[0:1])
+        ig_ref[pl.ds(j, 1), :] = rest[1:2]
+        ib_ref[pl.ds(j, 1), :] = rest[2:3]
+    each = rate_ref.shape[0] // CHAIN
+    for p in range(CHAIN):
+        turned = jnp.concatenate([tiles_ref[p]] * 16, axis=0).T
+        rate_ref[pl.ds(p * each, each), :] = turned[0:each, 0:heads]
+    acc = small_ref[0]
+    for p in range(1, CHAIN):
+        acc = acc + small_ref[p]
+    vec_ref[...] = acc
+
+
+def finish(at_mix, ffn, down, resid, back, grc, late, early, ends, tiles, small, shapes):
+    ins = (down, resid, back, grc, late, early, ends, tiles, small)
+    vmem = pl.BlockSpec(memory_space=pltpu.VMEM)
+    return pl.pallas_call(
+        functools.partial(final_kernel, at_mix, ffn),
+        in_specs=[vmem] * len(ins),
+        out_specs=[vmem] * len(shapes),
+        out_shape=[jax.ShapeDtypeStruct(s, f32) for s in shapes],
+        compiler_params=pltpu.CompilerParams(vmem_limit_bytes=48 * 1024 * 1024),
+        name="final",
     )(*ins)
 
 
@@ -858,7 +1059,6 @@
     rows, local_cols = inputs.shape
     heads, head_dim = inner_gain.shape
     head_index = lax.axis_index("head")
-    position = lax.axis_index("seq") % CHAIN
     whole_low = lax.all_gather(inputs, "head", axis=1, tiled=True)
     whole_in = whole_low.astype(f32)
     grad_whole = lax.all_gather(cotangent, "head", axis=1, tiled=True)
@@ -881,116 +1081,69 @@
     pre = bf_product("rd,dc->rc", normed_one, packed_w) + packed_bias
     payload = (pre - jnp.where(low_lane, lax.reduce_precision(pre, 8, 7), 0.0)).astype(bf16)
     gate_pre = bf_product("rd,dc->rc", normed_one, mix_gate)
-    mixed_h, *saved = chain_forward(
-        payload, init_w_one, init_b_one, init_w_two, init_b_two, inner_gain, inner_bias)
-    grad_mixed, early, grad_gate_pre, outputs, grad_resid_cols, small = middle(
+    share = full_width // CHAIN
+    mixed_h, normed_cols, *saved = chain_forward(
+        payload, normed_one.reshape(rows, CHAIN, share).transpose(1, 0, 2), init_w_one, init_b_one, init_w_two, init_b_two, inner_gain, inner_bias)
+    ffn = w_gate.shape[1]
+    at_mix = 3 * ffn
+    grad_mixed, early, grad_gate_pre, down_cols, resid_cols, grad_resid_cols, small = middle(
         mixed_h, whole_low, grad_whole, gate_pre, normed_one, w_out, w_gate, w_up, w_down,
         post_gain[None], post_bias[None], ffn_gain[None])
-    share = full_width // CHAIN
-    grads, ends, early_sum, normed_cols = chain_backward(
-        grad_mixed,
-        early.reshape(CHAIN, share, early.shape[1]),
-        normed_one.reshape(rows, CHAIN, share).transpose(1, 0, 2), inner_gain, inner_bias, saved)
-    wide = 3 * head_dim
-    late = bf_product("tc,jtk->jck", normed_cols.reshape(CHAIN * rows, share), grads[:, :, :wide])
-    back = lax.dynamic_slice_in_dim(grads, position * rows, rows, 1)
-
-    def join_heads(lo, hi):
-        return back[:, :, lo:hi].transpose(1, 0, 2).reshape(rows, -1)
-
-    grad_q_low = join_heads(0, head_dim)
-    grad_k_low = join_heads(head_dim, 2 * head_dim)
-    grad_v_low = join_heads(2 * head_dim, 3 * head_dim)
-    grad_logits = join_heads(3 * head_dim, 3 * head_dim + 1).astype(f32) + join_heads(
-        3 * head_dim + 1, 3 * head_dim + 2).astype(f32)
-    rate_bias_term = jnp.sum(grad_logits, axis=0)
-    grad_logit_low = grad_logits.astype(bf16)
-    rate_weight_term = bf_product("rd,rc->dc", normed_one, grad_logit_low)
-    grad_normed_one = (
-        bf_product("rc,dc->rd", grad_q_low, w_query)
-        + bf_product("rc,dc->rd", grad_k_low, w_key)
-        + bf_product("rc,dc->rd", grad_v_low, w_value)
-        + bf_product("rc,dc->rd", grad_gate_pre, mix_gate)
-        + bf_product("rc,dc->rd", grad_logit_low, w_rate)
-    )
-    scaled_one = grad_normed_one * pre_gain
-    input_back = rms_one * (
-        scaled_one
-        - whole_in * rms_one * rms_one * jnp.mean(scaled_one * whole_in, axis=1, keepdims=True)
-    )
-    gain_one_term = jnp.sum(grad_normed_one * whole_in * rms_one, axis=0)
-    input_local = lax.psum_scatter(
-        input_back.astype(bf16), "head", scatter_dimension=1, tiled=True).astype(f32)
-    grad_inputs = grad_resid_cols + input_local
-    ends = ends.astype(f32)
-    hidden = ends.shape[2]
-    late = late.reshape(heads, share, 3, head_dim).transpose(2, 1, 0, 3).reshape(3, share, local_cols)
+    grads, ends, early_sum, small = chain_backward(
+        grad_mixed, early.reshape(CHAIN // 2, 2, share, early.shape[1]), small, inner_gain, inner_bias, saved)
+    late, back_cols, tiles = tail(
+        at_mix, grads, packed_w, mix_gate, grad_gate_pre, whole_low, pre_gain[None],
+        normed_cols.reshape(CHAIN * rows, share), early_sum)
     if stretches > 1:
-        ends = lax.psum(ends, "seq", axis_index_groups=stretch_groups("seq"))
+        groups = stretch_groups("seq")
+        ends, tiles, small = lax.psum((ends.astype(f32), tiles, small), "seq", axis_index_groups=groups)
         seq_index = lax.axis_index("seq")
+        stretch_lists = [list(range(s, s + CHAIN)) for s in range(0, stretches * CHAIN, CHAIN)]
 
         def spread(mine_rows):
-            summed = lax.psum(mine_rows, "seq", axis_index_groups=stretch_groups("seq"))
+            summed = lax.psum(mine_rows, "seq", axis_index_groups=groups)
             total = lax.all_gather(
-                summed, "seq", axis=summed.ndim - 2, tiled=True,
-                axis_index_groups=[list(range(s, s + CHAIN)) for s in range(0, stretches * CHAIN, CHAIN)])
+                summed, "seq", axis=summed.ndim - 2, tiled=True, axis_index_groups=stretch_lists)
             return lax.dynamic_slice_in_dim(
                 total, seq_index * (share // stretches), share // stretches, summed.ndim - 2)
 
         late = spread(late)
         early_sum = spread(early_sum)
-    end_two = ends[:, AUG : AUG + head_dim]
-    tails = ends[:, AUG + head_dim :, :head_dim]
-    grad_one = ends[:, :head_dim]
-    grad_b_one = ends[:, head_dim]
-    grad_two = (end_two - jnp.mean(end_two, axis=1, keepdims=True)).transpose(0, 2, 1)
-    grad_b_two = tails[:, 0] - jnp.mean(tails[:, 0], axis=1, keepdims=True)
-    grad_gain = tails[:, 1]
-    grad_bias = tails[:, 2]
-    flat = lax.psum(
-        jnp.concatenate([small[1, :local_cols], small[2, :local_cols], rate_weight_term.reshape(-1), rate_bias_term]), "seq")
-    at = 0
-
-    def take(shape):
-        nonlocal at
-        size = 1
-        for extent in shape:
-            size *= extent
-        at += size
-        return flat[at - size : at].reshape(shape)
-
-    grad_post_gain = take((local_cols,))
-    grad_post_bias = take((local_cols,))
-    grad_rate_w = take((full_width, heads))
-    grad_rate_b = take((heads,))
-    gain_both = lax.psum(
-        jnp.concatenate([gain_one_term, small[0] / lax.axis_size("head")]), ("seq", "head"))
-    gain_one = lax.dynamic_slice_in_dim(gain_both, head_index * local_cols, local_cols, 0)
-    gain_two = gain_both[full_width:]
-    ffn = w_gate.shape[1]
+    held = share // stretches
+    hidden = init_w_one.shape[2]
+    square = (held, local_cols)
+    (outputs, grad_inputs, grad_q, grad_k, grad_v, grad_mix, grad_rate_w, grad_w_out, grad_w_gate, grad_w_up, grad_w_down,
+     grad_one, grad_b_one, grad_two, grad_b_two, grad_gain, grad_bias, vectors) = finish(
+        at_mix, ffn, down_cols, resid_cols, back_cols, grad_resid_cols, late, early_sum, ends, tiles, small,
+        ((rows, local_cols), (rows, local_cols), square, square, square, square, (full_width, heads),
+         (local_cols, held), (held, ffn), (held, ffn), (ffn, held),
+         (heads, head_dim, hidden), (heads, hidden), (heads, hidden, head_dim), (heads, head_dim),
+         (heads, head_dim), (heads, head_dim), (8, full_width)))
+    gain_all = tiles[:, heads, :share].reshape(full_width) / pre_gain
+    gain_one = lax.dynamic_slice_in_dim(gain_all, head_index * local_cols, local_cols, 0)
     return (
         outputs,
         grad_inputs,
         gain_one,
-        late[0],
-        late[1],
-        late[2],
-        early_sum[:, 3 * ffn : 3 * ffn + local_cols],
+        grad_q,
+        grad_k,
+        grad_v,
+        grad_mix,
         grad_rate_w,
-        grad_rate_b,
+        tiles[0, heads + 1, :heads],
         grad_gain,
         grad_bias,
         grad_one,
         grad_b_one,
         grad_two,
         grad_b_two,
-        grad_post_gain,
-        grad_post_bias,
-        early_sum[:, 3 * ffn + local_cols :].T,
-        gain_two,
-        early_sum[:, :ffn],
-        early_sum[:, ffn : 2 * ffn],
-        early_sum[:, 2 * ffn : 3 * ffn].T,
+        vectors[1, :local_cols],
+        vectors[2, :local_cols],
+        grad_w_out,
+        vectors[0],
+        grad_w_gate,
+        grad_w_up,
+        grad_w_down,
     )
 
 

time: 462 us -> 358 us (0.77)
  blocking collectives: 90.2 us -> 14.6 us
  between operations: 14.5 us -> 0.98 us
  local copies, waits for them, and re-layouts: 23.7 us -> 18.6 us
  matrix products: 7.18 us -> 2.27 us
    psum x2 -> x0, blocking collectives: 75.3 us -> none  [the longest x1 38.4 us: local(): lax.psum(jnp.concatenate([small[1, :local_cols], small[2, :local_cols], r...]
    dot_general x9 -> x2, matrix products: 7.18 us -> 2.27 us  [bf_product(): return jnp.einsum(form, left, right, preferred_element_type=f32)]
    unnamed x46 -> x49, local copies, waits for them, and re-layouts: 10.3 us -> 8.59 us
    pallas_call x1 -> x3, Pallas kernels: 243 us -> 242 us  [the longest x1 216 us: chain_backward(): pl.pallas_call(functools.partial(bwd_kernel, block, unroll, heads, turn),...]
  transfers between devices with their start and end apart: 1 -> 0, of which waited for: 0 -> 0; matrix products, arithmetic and copies ran while one was open for 4% -> 0% of each run, Pallas kernels for 0% -> 0%
where the time goes in v3:
time: 358 us; the launch traced here: 357 us
  Pallas kernels  320 us (89%)
  local copies, waits for them, and re-layouts  18.6 us (5%)
  blocking collectives  14.6 us (4%)
    pallas_call x1, Pallas kernels, chain_backward(): pl.pallas_call(functools.partial(bwd_kernel, block, unroll, heads, turn),...  216 us
    pallas_call x1, Pallas kernels, middle(): pl.pallas_call(functools.partial(mid_kernel, count), in_specs=[vmem] * le...  44.6 us
    pallas_call x1, Pallas kernels, chain_forward(): pl.pallas_call(functools.partial(fwd_kernel, block, unroll, heads), grid=...  33.3 us
    pallas_call x1, Pallas kernels, tail(): pl.pallas_call(functools.partial(tail_kernel, count, at_mix), in_specs=[v...  24.6 us
    unnamed x49, local copies, waits for them, and re-layouts  8.59 us
    all_gather x1, blocking collectives, local(): whole_low = lax.all_gather(inputs, 'head', axis=1, tiled=True)  8.25 us

profile of v3, /device:TPU:0, one launch (start us, length us, event | category | flops | bytes accessed | tf_op | source)
XLA Modules:
  0.0 357.3 jit_solution(12003602019462034955)
XLA Ops:
  0.7 0.0 copy-start
  0.7 0.0 copy-start.19
  0.7 0.0 copy-start.13
  0.7 0.0 copy-start.14
  0.7 0.0 copy-start.15
  0.7 8.2 %all_gather.6 = bf16[256,768]{0,1:T(8,128)(2,1)S(1)} all-gather(bf16[256,192]{0,1:T(8,128)(2,1)} %param.22), channel_id=1, replica_groups=mesh['seq'=8,'head'=4] {'head'}, dimensions={1}, use_global_device_ids=true | all-gather | bytes 491520 | tf_op jit(solution)/shard_map/all_gather | solution.py:1062
  9.0 0.2 copy.88.x_ref
  9.1 0.0 copy-start.10
  9.2 0.2 fusion
  9.3 0.8 fusion.2.normed_ref
  10.2 0.0 copy-start.11
  10.2 0.0 copy-done.19
  10.2 0.0 copy-done.13
  10.3 0.0 copy-done.14
  10.3 0.0 copy-done.15
  10.3 1.1 concatenate.3
  11.4 0.0 copy-done
  11.4 0.1 broadcast_reduce_fusion
  11.6 1.3 subtract_convert_fusion.pay_ref
  12.9 0.0 copy-done.10
  12.9 0.2 copy.91
  13.1 0.0 copy-start.17
  13.1 1.0 copy.92
  14.1 0.0 copy-done.16
  14.1 0.9 copy.93.w2_in
  15.0 33.3 %inner_forward.1 = (bf16[3,256,64]{2,1,0:T(8,128)(2,1)}, bf16[8,256,96]{2,1,0:T(8,128)(2,1)}, bf16[2048,80]{1,0:T(8,128)(2,1)}, bf16[2048,80]{1,0:T(8,128)(2,1)}...) custom-call(bf16[256,768]{1,0:T(8,128)(2,1)} %subtract_convert_fusio, ...), custom_call_target="tpu_custom_call" | custom-call | tf_op jit(solution)/shard_map/inner_forward/pallas_call | solution.py:389
  48.3 0.0 copy-done.11
  48.3 0.0 copy-done.12
  48.3 1.0 fusion.4.gate_pre_ref
  49.3 0.0 copy-done.17
  49.3 6.3 %all_gather.7 = bf16[256,768]{0,1:T(8,128)(2,1)S(1)} all-gather(bf16[256,192]{0,1:T(8,128)(2,1)S(1)} %copy-done.17), channel_id=1, replica_groups=mesh['seq'=8,'head'=4] {'head'}, dimensions={1}, use_global_device_ids=true | all-gather | bytes 491520 | tf_op jit(solution)/shard_map/all_gather | solution.py:1064
  55.7 0.9 copy.95.ct_ref
  56.6 0.0 copy-done.20
  56.6 0.6 broadcast_in_dim.52.ffn_gain_ref
  57.2 44.6 %middle.1 = (bf16[3,256,64]{2,1,0:T(8,128)(2,1)}, bf16[768,1920]{1,0:T(8,128)(2,1)}, bf16[256,192]{1,0:T(8,128)(2,1)}, f32[256,192]{1,0:T(8,128)}, f32[256,192]{...) custom-call(bf16[3,256,64]{2,1,0:T(8,128)(2,1)} %get-tuple-element.67.mixed_ref, bf16[256,768]{1,0:T(8,128)(2,1)} %copy-done.10, ...), custom_call_target="tpu_custom_call" | custom-call | tf_op jit(solution)/shard_map/middle/pallas_call | solution.py:837
  101.7 216.0 %inner_backward.1 = (bf16[3,2048,256]{2,1,0:T(8,128)(2,1)}, bf16[3,160,256]{2,1,0:T(8,128)(2,1)}, f32[96,1920]{1,0:T(8,128)}, f32[8,8,768]{2,1,0:T(8,128)}) custom-call(bf16[3,256,64]{2,1,0:T(8,128)(2,1)} %get-tuple-element.70.gm_ref, bf16[4,2,96,1920]{3,2,1,0:T(8,128)(2,1)} %bitcast.21, f32[8,768]{1,0:T(8,128)} %get-tuple-element.72.small_ref, ...), custom_call_target="tpu_custom_call" | custom-call | tf_op jit(solution)/shard_map/inner_backward/pallas_call | solution.py:587
  317.7 0.0 copy-start.18
  317.7 1.4 copy.97.packed_w_ref
  319.2 0.9 copy.98.mix_gate_ref
  320.1 0.0 copy-done.18
  320.1 0.6 broadcast_in_dim.53.pre_gain_ref
  320.7 24.6 %tail.1 = (f32[3,96,256]{2,1,0:T(8,128)}, f32[256,192]{1,0:T(8,128)}, f32[8,8,128]{2,1,0:T(8,128)}) custom-call(bf16[3,2048,256]{2,1,0:T(8,128)(2,1)} %get-tuple-element.84.grads_ref, bf16[768,768]{1,0:T(8,128)(2,1)} %copy.97.packed_w_ref, bf16[768,192]{1,0:T(8,128)(2,1)} %copy.98.mix_gate_ref, bf16[256,192]{1,0:T(8,128)(2,1)} %get-tuple-element.85.ggp_ref, ...), custom_call_target="tpu_custom_call" | custom-call | tf_op jit(solution)/shard_map/tail/pallas_call | solution.py:962
  345.4 0.0 copy-done.1
  345.4 0.0 copy-done.3
  345.4 0.0 copy-done.4
  345.4 0.0 copy-done.5
  345.4 0.0 copy-done.7
  345.4 0.0 copy-done.8
  345.4 0.0 copy-start.2
  345.4 1.0 copy-done.2
  346.4 0.9 copy-done.6
  347.3 0.8 copy-done.9
  348.1 1.4 final.1
  349.5 0.8 copy.100
  350.3 0.8 copy.101
  351.1 0.8 copy.103
  351.9 0.8 copy.104
  352.7 0.7 copy.102
  353.5 0.6 slice_reduce_fusion.1
  354.1 0.6 fusion.3
  354.7 0.8 slice_reduce_fusion
  355.4 0.1 reshape_squeeze.3
  355.5 0.6 dynamic_slice.3
  356.2 1.2 slice_bitcast_fusion
  (23 shorter events, 0.2 us)
Async XLA Ops:
  0.7 10.8 %copy-start = (f32[3]{0:T(128)S(1)}, f32[3]{0:T(128)}, u32[]{:S(2)}) copy-start(f32[3]{0:T(128)} %param.29) | copy-start | bytes 40
  0.7 9.5 %copy-start.19 = (bf16[768,3]{0,1:T(4,128)(2,1)S(1)}, bf16[768,3]{0,1:T(4,128)(2,1)}, u32[]{:S(2)}) copy-start(bf16[768,3]{0,1:T(4,128)(2,1)} %param.28) | copy-start | bytes 13828
  0.7 9.6 %copy-start.13 = (bf16[768,192]{0,1:T(8,128)(2,1)S(1)}, bf16[768,192]{0,1:T(8,128)(2,1)}, u32[]{:S(2)}) copy-start(bf16[768,192]{0,1:T(8,128)(2,1)} %param.24) | copy-start | bytes 884740
  0.7 9.6 %copy-start.14 = (bf16[768,192]{0,1:T(8,128)(2,1)S(1)}, bf16[768,192]{0,1:T(8,128)(2,1)}, u32[]{:S(2)}) copy-start(bf16[768,192]{0,1:T(8,128)(2,1)} %param.25) | copy-start | bytes 884740
  0.7 9.6 %copy-start.15 = (bf16[768,192]{0,1:T(8,128)(2,1)S(1)}, bf16[768,192]{0,1:T(8,128)(2,1)}, u32[]{:S(2)}) copy-start(bf16[768,192]{0,1:T(8,128)(2,1)} %param.26) | copy-start | bytes 884740
  9.1 3.8 %copy-start.10 = (bf16[256,768]{1,0:T(8,128)(2,1)}, bf16[256,768]{1,0:T(8,128)(2,1)S(1)}, u32[]{:S(2)}) copy-start(bf16[256,768]{1,0:T(8,128)(2,1)S(1)} %copy.88.x_ref) | copy-start | bytes 1179652
  10.2 38.2 %copy-start.11 = (bf16[256,768]{1,0:T(8,128)(2,1)}, bf16[256,768]{1,0:T(8,128)(2,1)S(1)}, u32[]{:S(2)}) copy-start(bf16[256,768]{1,0:T(8,128)(2,1)S(1)} %fusion.2.normed_ref) | copy-start | bytes 1179652
  11.6 2.5 copy-start.16
  12.9 35.4 %copy-start.12 = (bf16[768,192]{0,1:T(8,128)(2,1)S(1)}, bf16[768,192]{0,1:T(8,128)(2,1)}, u32[]{:S(2)}) copy-start(bf16[768,192]{0,1:T(8,128)(2,1)} %param.27) | copy-start | bytes 884740
  13.1 36.3 %copy-start.17 = (bf16[256,192]{0,1:T(8,128)(2,1)S(1)}, bf16[256,192]{0,1:T(8,128)(2,1)}, u32[]{:S(2)}) copy-start(bf16[256,192]{0,1:T(8,128)(2,1)} %param.43) | copy-start | bytes 294916
  14.1 42.5 %copy-start.20 = (f32[768]{0:T(1024)S(1)}, f32[768]{0:T(1024)}, u32[]{:S(2)}) copy-start(f32[768]{0:T(1024)} %param.39) | copy-start | bytes 9220
  317.7 2.4 copy-start.18
  320.7 24.7 %copy-start.1 = (f32[96,1920]{1,0:T(8,128)S(1)}, f32[96,1920]{1,0:T(8,128)}, u32[]{:S(2)}) copy-start(f32[96,1920]{1,0:T(8,128)} %get-tuple-element.87.early_ref) | copy-start | bytes 2211844
  320.7 24.7 %copy-start.3 = (f32[256,192]{1,0:T(8,128)S(1)}, f32[256,192]{1,0:T(8,128)}, u32[]{:S(2)}) copy-start(f32[256,192]{1,0:T(8,128)} %get-tuple-element.68.down_ref) | copy-start | bytes 589828
  320.7 24.7 %copy-start.4 = (f32[256,192]{1,0:T(8,128)S(1)}, f32[256,192]{1,0:T(8,128)}, u32[]{:S(2)}) copy-start(f32[256,192]{1,0:T(8,128)} %get-tuple-element.69.resid_ref) | copy-start | bytes 589828
  320.7 24.7 %copy-start.5 = (f32[256,192]{1,0:T(8,128)S(1)}, f32[256,192]{1,0:T(8,128)}, u32[]{:S(2)}) copy-start(f32[256,192]{1,0:T(8,128)} %get-tuple-element.89.grc_ref) | copy-start | bytes 589828
  320.7 24.7 %copy-start.7 = (bf16[3,160,256]{2,1,0:T(8,128)(2,1)S(1)}, bf16[3,160,256]{2,1,0:T(8,128)(2,1)}, u32[]{:S(2)}) copy-start(bf16[3,160,256]{2,1,0:T(8,128)(2,1)} %get-tuple-element.91.ends_ref) | copy-start | bytes 737284
  320.7 24.7 %copy-start.8 = (f32[8,8,768]{2,1,0:T(8,128)S(1)}, f32[8,8,768]{2,1,0:T(8,128)}, u32[]{:S(2)}) copy-start(f32[8,8,768]{2,1,0:T(8,128)} %get-tuple-element.93.small_ref) | copy-start | bytes 589828
  345.4 1.0 copy-start.2
  346.4 0.9 copy-start.6
  347.3 0.8 copy-start.9

commit v4 on v3

--- a/solution.py
+++ b/solution.py
@@ -110,81 +110,150 @@
     return (new_w1, new_w2t, new_b2), z1_next, out, (w1_h, w2_h, upd, zc, s2, z1b, z2b)
 
 
-def backward_step(carry, saved, d_out, key_aug, query_aug, target, rate, keep, gain, gain_sq, bias, tri):
-    p1, p2t, p2 = carry
+def prepare_back(store, saved, d_out, key_aug, query_aug, target, rate, gain, gain_sq, bias, tri):
     w1_h, w2_h, z1, upd, zc, s2, z1b, z2b = saved
+    width = gain.shape[1]
+    s2_h = s2.astype(bf16)
+    actb, derb = gelu_first(z1b)
+    actb_h = actb.astype(bf16)
+    invb = lax.rsqrt(mean_row(z2b * z2b) + eps_norm)
+    dn = d_out * gain
+    m_dn = mean_row(dn)
+    yield
     act, der, curve = gelu_second(z1)
     act_h = act.astype(bf16)
-    actb, derb = gelu_first(z1b)
-    actb_h = actb.astype(bf16)
-    s2_h = s2.astype(bf16)
     s1_h = (upd * der).astype(bf16)
+    store.update(act=act_h, der=der, bend=upd * curve, actb=actb_h, s1=s1_h, s2=s2_h)
+    yield
+    att2 = dot_nt(actb_h, act_h)
+    att1 = dot_nt(query_aug, key_aug)
+    nb = z2b * invb
+    d_z2b = invb * (dn - m_dn - nb * mean_row(dn * nb))
+    d_z2b_h = d_z2b.astype(bf16)
+    yield
+    inv = lax.rsqrt(mean_row(zc * zc) + eps_norm)
+    d_att2 = dot_nt(d_z2b_h, s2_h)
+    d_actb = dot_nn(d_z2b_h, w2_h)
+    base = (bias - target) * gain
+    m_sq = mean_row(gain_sq)
+    yield
+    att2 = ((att2 + 1.0) * tri).astype(bf16)
+    att1 = (att1 * tri).astype(bf16)
+    n = zc * inv
+    ng = n * gain_sq
+    big_g = ng + base
+    m_g = mean_row(big_g)
+    m_gn = mean_row(big_g * n)
+    yield
+    d_att2 = (-d_att2 * tri).astype(bf16)
+    d_actb = d_actb + dot_nn(d_att2, act_h)
+    c2 = dot_tn(att2, d_z2b_h)
+    m_ng = mean_row(ng)
+    m_nng = mean_row(n * ng)
+    yield
+    c3 = dot_tn(d_att2, actb_h)
+    inv2 = inv * inv
+    g = inv * (big_g - m_g - n * m_gn)
+    fac = rate * inv2 * (gain_sq - m_gn)
+    scale = rate * (1.0 / width)
+    weights = (jnp.broadcast_to(scale, n.shape), scale * n, scale * gain_sq, scale * (ng * inv2 + g * inv))
+    store.update(c2=c2, c3=c3, fac=fac, weights=weights, inv=inv, inv2=inv2, n=n)
+    yield
+    d_z1b_h = (d_actb * derb).astype(bf16)
+    c1 = dot_tn(att1, d_z1b_h)
+    row1 = inv2 * (gain_sq - (m_sq + m_gn) - n * m_ng)
+    row2 = inv2 * (ng + big_g - (m_ng + m_g) - n * (m_nng + 2.0 * m_gn))
+    store.update(dz2b=d_z2b_h, dz2bf=d_z2b, dz1b=d_z1b_h, c1=c1, row1=row1, row2=row2)
+    yield
+    fixed = dot_nn(jnp.concatenate([row1, row2, jnp.broadcast_to(inv2, n.shape), n], axis=0).astype(bf16), w2_h)
+    d_att1 = dot_nt(d_z1b_h, s1_h)
+    d_query = dot_nt(d_z1b_h, w1_h)
+    yield
+    prods = tuple(fixed[i * MINI : (i + 1) * MINI] for i in range(4))
+    store.update(prods=prods)
+    d_att1 = (-d_att1 * tri).astype(bf16)
+    d_query = (d_query + dot_nn(d_att1, key_aug))[:, :width] + d_out
+    d_key = dot_tn(d_att1, query_aug)[:, :width]
+    yield
+    d_gain = jnp.sum(d_out * nb, axis=0, keepdims=True)
+    d_bias = jnp.sum(d_out, axis=0, keepdims=True)
+    store.update(dq=d_query, dk=d_key, d_gain=d_gain, d_bias=d_bias, rate=rate, w1=w1_h, w2=w2_h, s2f=s2,
+                 key=key_aug, query=query_aug, gslope=2.0 * n * gain + bias - target)
+    yield
+
+
+PIECES = 11
+
+
+def settle(post, width):
+    if post is None:
+        return
+    pre, d_s2, a1, a2, d_z1_h, p1_h, keep, gain, sink = post
+    d_g = pre["inv"] * (pre["rate"] * d_s2 - a1 - pre["n"] * a2)
+    d_gg = d_g * gain
+    key_part = dot_nt(d_z1_h, pre["w1"])
+    late_part = dot_nt(pre["s1"], p1_h)
+    d_logit = keep * jnp.sum(d_s2 * pre["s2f"], axis=1, keepdims=True)
+    yield
+    d_gain = pre["d_gain"] + jnp.sum(d_g * pre["gslope"], axis=0, keepdims=True)
+    d_bias = pre["d_bias"] + jnp.sum(d_gg, axis=0, keepdims=True)
+    d_key = pre["dk"] + d_gg + (key_part - late_part)[:, :width]
+    sink(pre["dq"], d_key, -d_gg, d_logit, d_gain, d_bias)
+    yield
+
+
+def drain(maker):
+    for _ in maker:
+        pass
+
+
+def backward_chain(carry, pre, post, fill, keep, gain, sink):
+    p1, p2t, p2, dz, kq, left, right, dsum = carry
+    width = gain.shape[1]
+    key, act, der, w2_h = pre["key"], pre["act"], pre["der"], pre["w2"]
+    after = settle(post, width)
     p1_h = p1.astype(bf16)
+    coef1 = dot_nt(key, kq).astype(bf16)
+    base1 = pre["c1"] + dot_nn(key, p1_h)
+    d_s1 = -base1 - dot_nn(coef1, dz)
     p2_h = p2t.astype(bf16)
-    invb = lax.rsqrt(mean_row(z2b * z2b) + eps_norm)
-    nb = z2b * invb
-    dn = d_out * gain
-    d_z2b = invb * (dn - mean_row(dn) - nb * mean_row(dn * nb))
-    d_z2b_h = d_z2b.astype(bf16)
-    d_att2 = (-dot_nt(d_z2b_h, s2_h) * tri).astype(bf16)
-    d_actb = dot_nn(d_z2b_h, w2_h) + dot_nn(d_att2, act_h)
-    d_z1b_h = (d_actb * derb).astype(bf16)
-    att2 = ((dot_nt(actb_h, act_h) + 1.0) * tri).astype(bf16)
-    att1 = (dot_nt(query_aug, key_aug) * tri).astype(bf16)
-    c2 = dot_tn(att2, d_z2b_h)
-    c3 = dot_tn(d_att2, actb_h)
-    c1 = dot_tn(att1, d_z1b_h)
-    d_att1 = (-dot_nt(d_z1b_h, s1_h) * tri).astype(bf16)
-    d_query = dot_nt(d_z1b_h, w1_h) + dot_nn(d_att1, key_aug)
-    d_key = dot_tn(d_att1, query_aug)
-    d_s1 = -c1 - dot_nn(key_aug, p1_h)
+    coef2 = dot_nt(act, right).astype(bf16)
+    p2 = p2 + dsum
+    base2 = pre["c2"] + p2 + dot_nt(act, p2_h)
+    fill(2)
+    side = base2 + dot_nn(coef2, left)
+    p1 = p1 + dot_tn(kq, dz)
+    p2t = p2t + dot_tn(left, right)
+    next(after, None)
+    fill(1)
     d_upd = d_s1 * der
     d_upd_h = d_upd.astype(bf16)
-    d_s2 = dot_nt(d_upd_h, w2_h) - c2 - dot_nt(act_h, p2_h) - p2
-    h = rate * d_s2
-    inv = lax.rsqrt(mean_row(zc * zc) + eps_norm)
-    n = zc * inv
-    base = (bias - target) * gain
-    big_g = n * gain_sq + base
-    m_g = mean_row(big_g)
-    m_gn = mean_row(big_g * n)
-    m_sq = mean_row(gain_sq)
-    ng = n * gain_sq
-    m_ng = mean_row(ng)
-    m_nng = mean_row(n * ng)
-    g = inv * (big_g - m_g - n * m_gn)
-    a1 = mean_row(h)
-    a2 = mean_row(h * n)
-    a3 = mean_row(h * gain_sq)
-    a4 = mean_row(h * ng)
-    a5 = mean_row(h * g)
-    proj = h - a1 - n * a2
-    d_g = inv * proj
-    dnn = inv * (proj * gain_sq - h * m_gn - big_g * a2)
-    m_dn = inv * (a3 - a1 * (m_sq + m_gn) - a2 * (m_ng + m_g))
-    m_dnn = inv * (a4 - a1 * m_ng - a2 * (m_nng + 2.0 * m_gn))
-    d_zc = inv * (dnn - m_dn - n * (m_dnn + a5))
+    d_s2 = dot_nt(d_upd_h, w2_h) - side
+    rest = pre["c3"] - dot_nn(pre["s2"], p2t.astype(bf16))
+    p1_h = p1.astype(bf16)
+    bend = d_s1 * pre["bend"]
+    next(after, None)
+    fill(3)
+    d_fac = d_s2 * pre["fac"]
+    main = dot_nn(d_fac.astype(bf16), w2_h)
+    a1, a2, a3, a4 = (jnp.sum(d_s2 * w, axis=1, keepdims=True) for w in pre["weights"])
+    fill(5)
+    y1, y2, y3, y4 = pre["prods"]
+    d_act = (main + rest) - ((a1 * y1 + a2 * y2) + (a3 * y3 + a4 * y4))
+    d_z1_h = (d_act * der + bend).astype(bf16)
+    d_zc = d_fac - ((a1 * pre["row1"] + a2 * pre["row2"]) + (a3 * pre["inv2"] + a4 * pre["n"]))
     d_zc_h = d_zc.astype(bf16)
-    d_act = dot_nn(d_zc_h, w2_h) + c3 - dot_nn(s2_h, p2_h)
-    d_z1 = d_act * der + d_s1 * upd * curve
-    d_z1_h = d_z1.astype(bf16)
-    d_gg = d_g * gain
-    d_key = d_key + dot_nt(d_z1_h, w1_h) - dot_nt(s1_h, p1_h)
-    d_key = d_key[:, : gain.shape[1]] + d_gg
-    d_query = d_query[:, : gain.shape[1]] + d_out
-    d_value = -d_gg
-    d_logit = keep * jnp.sum(d_s2 * s2, axis=1, keepdims=True)
-    new_p1 = p1 + dot_tn(
-        jnp.concatenate([key_aug, query_aug], axis=0), jnp.concatenate([d_z1_h, d_z1b_h], axis=0)
-    )
-    new_p2t = p2t + dot_tn(
-        jnp.concatenate([s2_h, d_zc_h, d_z2b_h], axis=0),
-        jnp.concatenate([d_upd_h, act_h, actb_h], axis=0),
-    )
-    new_p2 = p2 + jnp.sum(d_zc + d_z2b, axis=0, keepdims=True)
-    d_bias = jnp.sum(d_out + d_gg, axis=0, keepdims=True)
-    d_gain = jnp.sum(d_out * nb + d_g * (2.0 * n * gain + bias - target), axis=0, keepdims=True)
-    return (new_p1, new_p2t, new_p2), (d_query, d_key, d_value, d_logit), d_gain, d_bias
+    carry = (p1, p2t, p2, jnp.concatenate([d_z1_h, pre["dz1b"]], axis=0),
+             jnp.concatenate([key, pre["query"]], axis=0),
+             jnp.concatenate([pre["s2"], d_zc_h, pre["dz2b"]], axis=0),
+             jnp.concatenate([d_upd_h, act, pre["actb"]], axis=0),
+             jnp.sum(d_zc + pre["dz2bf"], axis=0, keepdims=True))
+    return carry, (pre, d_s2, a1, a2, d_z1_h, p1_h, keep, gain, sink)
+
+
+def backward_close(carry):
+    p1, p2t, p2, dz, kq, left, right, dsum = carry
+    return p1 + dot_tn(kq, dz), p2t + dot_tn(left, right), p2 + dsum
 
 
 MESH = pl.DeviceIdType.MESH
@@ -235,7 +304,7 @@
 def fwd_kernel(block, unroll, heads, pay_ref, norm_ref, w1_in, b1_in, w2_in, b2_in, gain_in, bias_in,
                mixed_ref, norm_out, k_out, q_out, aux_out, w1s_ref, w2s_ref, z1s_ref, upd_ref, zc_ref, s2_ref, z1b_ref, z2b_ref,
                got, k_all, q_all, base_all, aux_all, mixed_all, w1, w2t, b2, z1,
-               pay_send, pay_recv, mix_send, mix_recv, no_send, no_recv, no_loc):
+               pay_send, pay_recv, mix_send, mix_recv, no_send, no_recv):
     blk = pl.program_id(0)
     last = pl.num_programs(0) - 1
     pos, base = seq_place()
@@ -265,7 +334,14 @@
             def _():
                 pltpu.make_async_copy(src, dst, pay_recv.at[pos]).start()
 
-        swap_start(norm_ref, norm_out, no_send, no_recv, no_loc, pos, base)
+        for j in range(heads):
+            @pl.when(pos != FIRST + j)
+            def _():
+                push(norm_ref, norm_out.at[pos], no_send.at[j], no_recv.at[pos], base + FIRST + j).start()
+
+            @pl.when(pos == FIRST + j)
+            def _():
+                pltpu.make_async_copy(norm_ref, norm_out.at[pos], no_recv.at[pos]).start()
 
     def take_in(p):
         await_bytes(got.at[p], pay_recv.at[p])
@@ -362,12 +438,14 @@
             send_mixed(last)
             others = mixed_all.at[pl.ds(0, (CHAIN - 1) * rows_each), :]
             await_bytes(others, mix_send)
-
-        swap_wait(norm_ref, norm_out, no_send, no_recv, no_loc, pos, base)
+            for p in range(CHAIN):
+                await_bytes(norm_out.at[p], no_recv.at[p])
+
         for j in range(heads):
             @pl.when(pos != FIRST + j)
             def _():
                 await_bytes(got.at[pos], pay_send.at[j])
+                await_bytes(norm_ref, no_send.at[j])
 
             await_bytes(mixed_ref.at[j], mix_recv.at[j])
 
@@ -393,7 +471,7 @@
         out_specs=[anywhere, anywhere, rowblk(AUG), rowblk(AUG), rowblk(2 * width), stepblk(AUG), stepblk(width),
                    rowblk(hidden), rowblk(hidden), rowblk(width), rowblk(width), rowblk(hidden), rowblk(width)],
         out_shape=[jax.ShapeDtypeStruct((heads, rows, width), bf16),
-                   jax.ShapeDtypeStruct(normed.shape, bf16),
+                   jax.ShapeDtypeStruct((CHAIN,) + normed.shape, bf16),
                    jax.ShapeDtypeStruct((tokens, AUG), bf16),
                    jax.ShapeDtypeStruct((tokens, AUG), bf16),
                    jax.ShapeDtypeStruct((tokens, 2 * width), f32),
@@ -407,17 +485,18 @@
                         pltpu.VMEM((AUG, hidden), f32), pltpu.VMEM((width, hidden), f32),
                         pltpu.VMEM((1, width), f32), pltpu.VMEM((MINI, hidden), f32),
                         dma((heads,)), dma((CHAIN,)), dma, dma((heads,)),
-                        dma((CHAIN - 1,)), dma((CHAIN - 1,)), dma],
+                        dma((heads,)), dma((CHAIN,))],
         compiler_params=pltpu.CompilerParams(collective_id=0, has_side_effects=True),
         name="inner_forward",
     )(payload, normed, *small)
 
 
-def bwd_kernel(block, unroll, heads, turn, gm_ref, early_ref, small_ref, gain_in, bias_in,
+def bwd_kernel(block, heads, turn, gm_ref, early_ref, small_ref, gain_in, bias_in, norm_ref,
                k_ref, q_ref, aux_ref, w1s_ref, w2s_ref, z1s_ref, upd_ref, zc_ref, s2_ref, z1b_ref, z2b_ref,
-               grads_ref, ends_ref, early_out, small_out,
-               dout, half_got, half_mine, quarter, quarter_got, packed, ends, p1, p2t, p2, dg, db,
-               gm_send, gm_recv, ha_send, ha_recv, ha_loc, qu_send, qu_recv, sm_send, sm_recv, sm_loc, bc_send, bc_recv, en_send, en_recv):
+               grads_ref, ends_ref, late_ref, early_out, small_out,
+               dout, half_got, half_mine, quarter, quarter_got, packed, ends, weights, late,
+               p1, p2t, p2, dz, kq, left, right, dsum, dg, db, dl,
+               gm_send, gm_recv, ha_send, ha_recv, ha_loc, qu_send, qu_recv, sm_send, sm_recv, sm_loc, bc_send, bc_recv, en_send, en_recv, la_send, la_recv):
     pid = pl.program_id(0)
     last = pl.num_programs(0) - 1
     blk = last - pid
@@ -435,6 +514,7 @@
     side = lax.rem(pos, 2)
     rank = lax.div(pos, 2)
     partner = pos + 1 - 2 * side
+    state = (p1, p2t, p2, dz, kq, left, right, dsum)
 
     @pl.when(pid == 0)
     def _():
@@ -473,17 +553,29 @@
                  base + 2 * other + side).start()
 
     def share_block(b):
+        p = lax.div(b, per)
+        src = packed.at[pl.ds(pl.multiple_of(b * block, block), block), :]
+        dst = grads_ref.at[mine, pl.ds(pl.multiple_of(lax.rem(b, per) * block, block), block), :]
+
+        @pl.when(p != pos)
+        def _():
+            push(src, dst, bc_send, bc_recv.at[mine], base + p).start()
+
+        @pl.when(p == pos)
+        def _():
+            pltpu.make_async_copy(src, dst, bc_recv.at[mine]).start()
+
+    share = late.shape[1]
+
+    def weigh(b, lo, hi):
         rows = pl.ds(pl.multiple_of(b * block, block), block)
-        for d in range(1, CHAIN):
-            push(packed.at[rows, :], grads_ref.at[mine, rows, :], bc_send.at[d - 1], bc_recv.at[mine],
-                 base + lax.rem(pos + d, CHAIN)).start()
-        pltpu.make_async_copy(packed.at[rows, :], grads_ref.at[mine, rows, :], bc_recv.at[mine]).start()
+        weights[lo:hi, :] += dot_tn(norm_ref[:, lo:hi], packed[rows, :])
 
     @pl.when(owner)
     def _():
         @pl.when(pid == 0)
         def _():
-            for r in (p1, p2t, p2, dg, db):
+            for r in state + (dg, db, dl, weights):
                 r[...] = jnp.zeros_like(r)
 
         @pl.when(lax.rem(pid, per) == 0)
@@ -495,40 +587,67 @@
         def _():
             share_block(blk + 1)
 
-        def group(it, _):
-            for u in range(unroll):
-                loc = count - 1 - (it * unroll + u)
-                row = pl.multiple_of(blk * block + loc * MINI, MINI)
-                lr = pl.ds(pl.multiple_of(loc * MINI, MINI), MINI)
-                inner = pl.ds(pl.multiple_of(lax.rem(blk, per) * block + loc * MINI, MINI), MINI)
-                saved = (w1s_ref[loc], w2s_ref[loc], z1s_ref[lr, :], upd_ref[lr, :], zc_ref[lr, :], s2_ref[lr, :],
-                         z1b_ref[lr, :], z2b_ref[lr, :])
-                aux = aux_ref[lr, :]
-                carry, outs, dgn, dbn = backward_step(
-                    (p1[...], p2t[...], p2[...]), saved, dout[lax.div(blk, per), inner, :].astype(f32), k_ref[lr, :],
-                    q_ref[lr, :], aux[:, :width], aux[:, width : width + 1], aux[:, width + 1 : width + 2],
-                    gain, gain_sq, bias, tri)
-                p1[...], p2t[...], p2[...] = carry
-                dg[...] += dgn
-                db[...] += dbn
-                d_query, d_key, d_value, d_logit = outs
+        carry = tuple(r[...] for r in state)
+        totals = [dg[...], db[...], dl[...]]
+        made = {}
+
+        def start(loc):
+            made[loc] = {}
+            lr = pl.ds(loc * MINI, MINI)
+            inner = pl.ds(pl.multiple_of(lax.rem(blk, per) * block + loc * MINI, MINI), MINI)
+            saved = (w1s_ref[loc], w2s_ref[loc], z1s_ref[lr, :], upd_ref[lr, :], zc_ref[lr, :], s2_ref[lr, :],
+                     z1b_ref[lr, :], z2b_ref[lr, :])
+            return prepare_back(made[loc], saved, dout[lax.div(blk, per), inner, :].astype(f32), k_ref[lr, :],
+                                q_ref[lr, :], aux_ref[lr, 0:width], aux_ref[lr, width : width + 1],
+                                gain, gain_sq, bias, tri)
+
+        drain(start(count - 1))
+        post = None
+        for loc in range(count - 1, -1, -1):
+            ahead = start(loc - 1) if loc > 0 else iter(())
+
+            def fill(pieces, ahead=ahead):
+                for _ in range(pieces):
+                    next(ahead, None)
+
+            def sink(d_query, d_key, d_value, d_logit, d_gain, d_bias, loc=loc):
+                totals[0] = totals[0] + d_gain
+                totals[1] = totals[1] + d_bias
+                totals[2] = totals[2] + jnp.sum(d_logit, axis=0, keepdims=True)
                 high = d_logit.astype(bf16).astype(f32)
                 lane = lax.broadcasted_iota(jnp.int32, (MINI, width), 1)
                 extra = jnp.where(lane == 0, high, jnp.where(lane == 1, d_logit - high, 0.0))
-                packed[pl.ds(row, MINI), :] = jnp.concatenate([d_query, d_key, d_value, extra], axis=1).astype(bf16)
-            return 0
-
-        lax.fori_loop(0, count // unroll, group, 0)
+                rows = pl.ds(pl.multiple_of(blk * block + loc * MINI, MINI), MINI)
+                packed[rows, :] = jnp.concatenate([d_query, d_key, d_value, extra], axis=1).astype(bf16)
+
+            carry, post = backward_chain(
+                carry, made.pop(loc), post, fill, aux_ref[pl.ds(loc * MINI, MINI), width + 1 : width + 2], gain, sink)
+        drain(settle(post, width))
+        for r, v in zip(state, carry):
+            r[...] = v
+        dg[...], db[...], dl[...] = totals
+        quarter_rows = norm_ref.shape[1] // 4
+        for i in range(4):
+            weigh(blk, i * quarter_rows, (i + 1) * quarter_rows)
 
         @pl.when(pid == last)
         def _():
-            ends[pl.ds(0, AUG), :] = p1[...].astype(bf16)
-            ends[pl.ds(AUG, width), :] = p2t[...].astype(bf16)
+            end_one, end_two, end_b_two = backward_close(tuple(r[...] for r in state))
+            ends[pl.ds(0, AUG), :] = end_one.astype(bf16)
+            ends[pl.ds(AUG, width), :] = end_two.astype(bf16)
             rest = ENDS - AUG - width
             row = lax.broadcasted_iota(jnp.int32, (rest, width), 0)
-            tailing = jnp.where(row == 0, p2[...], jnp.where(row == 1, dg[...], jnp.where(row == 2, db[...], 0.0)))
+            tailing = jnp.where(row == 0, end_b_two, jnp.where(row == 1, dg[...], jnp.where(row == 2, db[...], 0.0)))
+            high = dl[...].astype(bf16).astype(f32)
+            tailing = tailing + jnp.where(row == 3, high, jnp.where(row == 4, dl[...] - high, 0.0))
             ends[pl.ds(AUG + width, rest), :] = jnp.concatenate([tailing] * 4, axis=1).astype(bf16)
             share_block(0)
+            for p in range(CHAIN):
+                late[p] = weights[p * share : (p + 1) * share, :].astype(bf16)
+            for d in range(1, CHAIN):
+                peer = lax.rem(pos + d, CHAIN)
+                push(late.at[peer], late_ref.at[mine], la_send.at[d - 1], la_recv.at[mine], base + peer).start()
+            pltpu.make_async_copy(late.at[pos], late_ref.at[mine], la_recv.at[mine]).start()
             for d in range(1, CHAIN):
                 push(ends, ends_ref.at[mine], en_send.at[d - 1], en_recv.at[mine],
                      base + lax.rem(pos + d, CHAIN)).start()
@@ -562,15 +681,17 @@
 
             await_bytes(grads_ref.at[j], bc_recv.at[j])
             await_bytes(ends_ref.at[j], en_recv.at[j])
+            await_bytes(late_ref.at[j], la_recv.at[j])
 
         @pl.when(owner)
         def _():
+            await_bytes(packed.at[pl.ds(0, (CHAIN - 1) * rows_each), :], bc_send)
             for d in range(1, CHAIN):
-                await_bytes(packed, bc_send.at[d - 1])
                 await_bytes(ends, en_send.at[d - 1])
-
-
-def chain_backward(grad_mixed, early, small, gain, bias, saved, block=128, unroll=4, turn=6):
+                await_bytes(late.at[0], la_send.at[d - 1])
+
+
+def chain_backward(grad_mixed, early, small, gain, bias, normed, saved, block=128, turn=6):
     heads, rows, width = grad_mixed.shape
     tokens = rows * CHAIN
     hidden = saved[5].shape[1]
@@ -585,27 +706,32 @@
     share = early.shape[2:]
     three = dma((CHAIN // 2 - 1,))
     return pl.pallas_call(
-        functools.partial(bwd_kernel, block, unroll, heads, turn),
+        functools.partial(bwd_kernel, block, heads, turn),
         grid=(nblk,),
-        in_specs=[anywhere] * 3 + [whole(gain), whole(bias), rowblk(AUG), rowblk(AUG), rowblk(2 * width),
-                                   stepblk(AUG), stepblk(width), rowblk(hidden), rowblk(hidden), rowblk(width),
+        in_specs=[anywhere] * 3 + [whole(gain), whole(bias), rowblk(normed.shape[1]), rowblk(AUG), rowblk(AUG),
+                                   rowblk(2 * width), stepblk(AUG), stepblk(width), rowblk(hidden), rowblk(hidden), rowblk(width),
                                    rowblk(width), rowblk(hidden), rowblk(width)],
-        out_specs=[anywhere, anywhere, pl.BlockSpec(share, lambda i: (0, 0)), anywhere],
-        out_shape=[jax.ShapeDtypeStruct((heads, tokens, PACK), bf16),
+        out_specs=[anywhere, anywhere, anywhere, pl.BlockSpec(share, lambda i: (0, 0)), anywhere],
+        out_shape=[jax.ShapeDtypeStruct((heads, rows, PACK), bf16),
                    jax.ShapeDtypeStruct((heads, ENDS, hidden), bf16),
+                   jax.ShapeDtypeStruct((heads, share[0], PACK), bf16),
                    jax.ShapeDtypeStruct(share, f32),
                    jax.ShapeDtypeStruct((CHAIN,) + small.shape, f32)],
         scratch_shapes=[pltpu.VMEM((CHAIN, rows, width), bf16), pltpu.VMEM((CHAIN // 2,) + share, bf16),
                         pltpu.VMEM((CHAIN // 2,) + share, bf16), pltpu.VMEM((CHAIN // 2,) + share, bf16),
                         pltpu.VMEM((CHAIN // 2 - 1,) + share, bf16),
                         pltpu.VMEM((tokens, PACK), bf16), pltpu.VMEM((ENDS, hidden), bf16),
+                        pltpu.VMEM((CHAIN * share[0], PACK), f32), pltpu.VMEM((CHAIN, share[0], PACK), bf16),
                         pltpu.VMEM((AUG, hidden), f32), pltpu.VMEM((width, hidden), f32), pltpu.VMEM((1, width), f32),
-                        pltpu.VMEM((1, width), f32), pltpu.VMEM((1, width), f32),
+                        pltpu.VMEM((2 * MINI, hidden), bf16), pltpu.VMEM((2 * MINI, AUG), bf16),
+                        pltpu.VMEM((3 * MINI, width), bf16), pltpu.VMEM((3 * MINI, hidden), bf16),
+                        pltpu.VMEM((1, width), f32), pltpu.VMEM((1, width), f32), pltpu.VMEM((1, width), f32),
+                        pltpu.VMEM((1, 1), f32),
                         dma((heads,)), dma((CHAIN,)), dma, dma, dma, three, three, seven, seven, dma,
-                        seven, dma((heads,)), seven, dma((heads,))],
+                        dma, dma((heads,)), seven, dma((heads,)), seven, dma((heads,))],
         compiler_params=pltpu.CompilerParams(collective_id=1, has_side_effects=True),
         name="inner_backward",
-    )(grad_mixed, early, small, gain, bias, *saved)
+    )(grad_mixed, early, small, gain, bias, normed, *saved)
 
 
 def head_place():
@@ -865,9 +991,9 @@
     )(*ins)
 
 
-def tail_kernel(count, at_mix, grads_ref, packed_w_ref, mix_gate_ref, ggp_ref, x_ref, pre_gain_ref, cols_ref, early_ref,
-                late_ref, back_ref, tiles_ref,
-                near, mine, got, tile, tile_got, near_sem, ib_s, ib_r, th_s, th_r, ts_s, ts_r, ts_loc):
+def tail_kernel(count, at_mix, grads_ref, packed_w_ref, mix_gate_ref, ggp_ref, x_ref, pre_gain_ref, late_ref, early_ref,
+                back_ref, tiles_ref,
+                mine, got, tile, tile_got, ib_s, ib_r, th_s, th_r, ts_s, ts_r, ts_loc):
     me, _ = head_place()
     pos, base = seq_place()
     heads = grads_ref.shape[0]
@@ -884,15 +1010,13 @@
         pl.semaphore_signal(
             barrier, inc=1, device_id={"seq": base + lax.rem(pos + d, CHAIN)}, device_id_type=MESH)
     pl.semaphore_wait(barrier, count - 1 + CHAIN - 1)
-    here = pl.ds(pl.multiple_of(pos * rows, rows), rows)
     part = rows // count
 
     def back_rows(b, _):
         r = pl.ds(pl.multiple_of(b * part, part), part)
-        away = pl.ds(pl.multiple_of(pos * rows + b * part, part), part)
         grad = dot_nt(ggp_ref[r, :], mix_gate_ref[...])
         for j in range(heads):
-            grad = grad + dot_nt(grads_ref[j, away, :], packed_w_ref[:, j * PACK : (j + 1) * PACK])
+            grad = grad + dot_nt(grads_ref[j, r, :], packed_w_ref[:, j * PACK : (j + 1) * PACK])
         x = x_ref[r, :].astype(f32)
         rms = lax.rsqrt(mean_row(x * x) + eps_norm)
         scaled = grad * pre_gain_ref[...]
@@ -902,18 +1026,13 @@
         return 0
 
     lax.fori_loop(0, count, back_rows, 0)
-    turned = cols_ref[...]
-    ones = jnp.ones((MINI, turned.shape[0]), bf16)
     lane = lax.broadcasted_iota(jnp.int32, (share, 128), 1)
-    spot = lax.broadcasted_iota(jnp.int32, (8, 128), 1)
     line = lax.broadcasted_iota(jnp.int32, (8, 128), 0)
     w_rows = pl.ds(pl.multiple_of(pos * share, share), share)
     gain = jnp.sum(early_ref[:, at_mix : at_mix + cols] * mix_gate_ref[w_rows, :].astype(f32), axis=1, keepdims=True)
     table = jnp.zeros((share, 128), f32)
-    extra = jnp.zeros((8, 128), f32)
     for j in range(heads):
-        late = dot_tn(turned, grads_ref[j])
-        late_ref[j] = late
+        late = late_ref[j].astype(f32)
         gain = gain + jnp.sum(
             late * packed_w_ref[w_rows, j * PACK : (j + 1) * PACK].astype(f32), axis=1, keepdims=True)
         rate = late[:, rate_lane : rate_lane + 1] + late[:, rate_lane + 1 : rate_lane + 2]
@@ -921,12 +1040,9 @@
         if j == 0:
             for d, peer in peers:
                 push_head(mine.at[peer], got.at[d - 1], ib_s.at[d - 1], ib_r.at[d - 1], peer).start()
-        total = dot_nn(ones, grads_ref[j])[0:8]
-        total = total[:, rate_lane : rate_lane + 1] + total[:, rate_lane + 1 : rate_lane + 2]
-        extra = jnp.where((line == heads + 1) & (spot == j), total, extra)
     table = jnp.where(lane == heads, gain, table)
     flat = jnp.concatenate([table, jnp.zeros((128 - share, 128), f32)], axis=0).T[0:8]
-    tile[...] = flat + extra
+    tile[...] = flat
     for d, peer in peers:
         push_head(tile, tile_got.at[d - 1], th_s.at[d - 1], th_r.at[d - 1], peer).start()
     back = mine[me].astype(f32)
@@ -935,7 +1051,7 @@
     summed = flat
     for d, peer in peers:
         summed = summed + tile_got[d - 1]
-    tile[...] = jnp.where(line == heads, summed, flat + extra)
+    tile[...] = jnp.where(line == heads, summed, flat)
     for d in range(1, CHAIN):
         push(tile, tiles_ref.at[pos], ts_s.at[d - 1], ts_r.at[d - 1], base + lax.rem(pos + d, CHAIN)).start()
     pltpu.make_async_copy(tile, tiles_ref.at[pos], ts_loc).start()
@@ -949,12 +1065,10 @@
     await_bytes(tiles_ref.at[pos], ts_loc)
 
 
-def tail(at_mix, grads, packed_w, mix_gate, ggp, x, pre_gain, cols, early):
+def tail(at_mix, grads, packed_w, mix_gate, ggp, x, pre_gain, late, early):
     count = lax.axis_size("head")
-    heads, tokens, _ = grads.shape
     rows, full = x.shape
     width = ggp.shape[1]
-    share = early.shape[0]
     vmem = pl.BlockSpec(memory_space=pltpu.VMEM)
     V = pltpu.VMEM
     dma = pltpu.SemaphoreType.DMA
@@ -962,28 +1076,27 @@
     return pl.pallas_call(
         functools.partial(tail_kernel, count, at_mix),
         in_specs=[vmem] * 8,
-        out_specs=[vmem] * 3,
-        out_shape=[jax.ShapeDtypeStruct((heads, share, PACK), f32),
-                   jax.ShapeDtypeStruct((rows, width), f32),
+        out_specs=[vmem] * 2,
+        out_shape=[jax.ShapeDtypeStruct((rows, width), f32),
                    jax.ShapeDtypeStruct((CHAIN, 8, 128), f32)],
-        scratch_shapes=[V((8, 128), f32), V((count, rows, width), bf16), V((count - 1, rows, width), bf16),
+        scratch_shapes=[V((count, rows, width), bf16), V((count - 1, rows, width), bf16),
                         V((8, 128), f32), V((count - 1, 8, 128), f32),
-                        dma, trio, trio, trio, trio, seven, seven, dma],
+                        trio, trio, trio, trio, seven, seven, dma],
         compiler_params=pltpu.CompilerParams(
             collective_id=3, has_side_effects=True, vmem_limit_bytes=56 * 1024 * 1024),
         name="tail",
-    )(grads, packed_w, mix_gate, ggp, x, pre_gain, cols, early)
+    )(grads, packed_w, mix_gate, ggp, x, pre_gain, late, early)
 
 
 def final_kernel(at_mix, ffn, down_ref, resid_ref, back_ref, grc_ref, late_ref, early_ref, ends_ref, tiles_ref, small_ref,
                  out_ref, gin_ref, gq_ref, gk_ref, gv_ref, gmix_ref, rate_ref, gwout_ref, gwg_ref, gwu_ref, gwd_ref,
-                 w1_ref, b1_ref, w2_ref, b2_ref, ig_ref, ib_ref, vec_ref):
+                 w1_ref, b1_ref, w2_ref, b2_ref, ig_ref, ib_ref, rb_ref, vec_ref):
     heads, width, hidden = w1_ref.shape
     cols = heads * width
     out_ref[...] = down_ref[...] + resid_ref[...]
     gin_ref[...] = back_ref[...] + grc_ref[...]
     for i, ref in enumerate((gq_ref, gk_ref, gv_ref)):
-        ref[...] = jnp.concatenate([late_ref[j, :, i * width : (i + 1) * width] for j in range(heads)], axis=1)
+        ref[...] = jnp.concatenate([late_ref[j, :, i * width : (i + 1) * width].astype(f32) for j in range(heads)], axis=1)
     gwg_ref[...] = early_ref[:, 0:ffn]
     gwu_ref[...] = early_ref[:, ffn : 2 * ffn]
     gwd_ref[...] = early_ref[:, 2 * ffn : 3 * ffn].T
@@ -999,6 +1112,7 @@
         b2_ref[pl.ds(j, 1), :] = rest[0:1] - mean_row(rest[0:1])
         ig_ref[pl.ds(j, 1), :] = rest[1:2]
         ib_ref[pl.ds(j, 1), :] = rest[2:3]
+        rb_ref[pl.ds(j, 1), :] = rest[3:4] + rest[4:5]
     each = rate_ref.shape[0] // CHAIN
     for p in range(CHAIN):
         turned = jnp.concatenate([tiles_ref[p]] * 16, axis=0).T
@@ -1082,18 +1196,19 @@
     payload = (pre - jnp.where(low_lane, lax.reduce_precision(pre, 8, 7), 0.0)).astype(bf16)
     gate_pre = bf_product("rd,dc->rc", normed_one, mix_gate)
     share = full_width // CHAIN
-    mixed_h, normed_cols, *saved = chain_forward(
-        payload, normed_one.reshape(rows, CHAIN, share).transpose(1, 0, 2), init_w_one, init_b_one, init_w_two, init_b_two, inner_gain, inner_bias)
+    mixed_h, normed_all, *saved = chain_forward(
+        payload, normed_one, init_w_one, init_b_one, init_w_two, init_b_two, inner_gain, inner_bias)
     ffn = w_gate.shape[1]
     at_mix = 3 * ffn
     grad_mixed, early, grad_gate_pre, down_cols, resid_cols, grad_resid_cols, small = middle(
         mixed_h, whole_low, grad_whole, gate_pre, normed_one, w_out, w_gate, w_up, w_down,
         post_gain[None], post_bias[None], ffn_gain[None])
-    grads, ends, early_sum, small = chain_backward(
-        grad_mixed, early.reshape(CHAIN // 2, 2, share, early.shape[1]), small, inner_gain, inner_bias, saved)
-    late, back_cols, tiles = tail(
+    grads, ends, late, early_sum, small = chain_backward(
+        grad_mixed, early.reshape(CHAIN // 2, 2, share, early.shape[1]), small, inner_gain, inner_bias,
+        normed_all.reshape(CHAIN * rows, full_width), saved)
+    back_cols, tiles = tail(
         at_mix, grads, packed_w, mix_gate, grad_gate_pre, whole_low, pre_gain[None],
-        normed_cols.reshape(CHAIN * rows, share), early_sum)
+        late, early_sum)
     if stretches > 1:
         groups = stretch_groups("seq")
         ends, tiles, small = lax.psum((ends.astype(f32), tiles, small), "seq", axis_index_groups=groups)
@@ -1107,18 +1222,18 @@
             return lax.dynamic_slice_in_dim(
                 total, seq_index * (share // stretches), share // stretches, summed.ndim - 2)
 
-        late = spread(late)
+        late = spread(late.astype(f32))
         early_sum = spread(early_sum)
     held = share // stretches
     hidden = init_w_one.shape[2]
     square = (held, local_cols)
     (outputs, grad_inputs, grad_q, grad_k, grad_v, grad_mix, grad_rate_w, grad_w_out, grad_w_gate, grad_w_up, grad_w_down,
-     grad_one, grad_b_one, grad_two, grad_b_two, grad_gain, grad_bias, vectors) = finish(
+     grad_one, grad_b_one, grad_two, grad_b_two, grad_gain, grad_bias, rate_b, vectors) = finish(
         at_mix, ffn, down_cols, resid_cols, back_cols, grad_resid_cols, late, early_sum, ends, tiles, small,
         ((rows, local_cols), (rows, local_cols), square, square, square, square, (full_width, heads),
          (local_cols, held), (held, ffn), (held, ffn), (ffn, held),
          (heads, head_dim, hidden), (heads, hidden), (heads, hidden, head_dim), (heads, head_dim),
-         (heads, head_dim), (heads, head_dim), (8, full_width)))
+         (heads, head_dim), (heads, head_dim), (heads, head_dim), (8, full_width)))
     gain_all = tiles[:, heads, :share].reshape(full_width) / pre_gain
     gain_one = lax.dynamic_slice_in_dim(gain_all, head_index * local_cols, local_cols, 0)
     return (
@@ -1130,7 +1245,7 @@
         grad_v,
         grad_mix,
         grad_rate_w,
-        tiles[0, heads + 1, :heads],
+        rate_b[:, 0],
         grad_gain,
         grad_bias,
         grad_one,

time: 358 us -> 332 us (0.927)
  Pallas kernels: 320 us -> 296 us
    pallas_call x1, Pallas kernels: 216 us -> 166 us  [chain_backward(): pl.pallas_call(functools.partial(bwd_kernel, block, heads, turn), grid=(n...]
    pallas_call x1, Pallas kernels: 33.3 us -> 62.3 us  [chain_forward(): pl.pallas_call(functools.partial(fwd_kernel, block, unroll, heads), grid=...]
    pallas_call x1, Pallas kernels: 24.6 us -> 21 us  [tail(): pl.pallas_call(functools.partial(tail_kernel, count, at_mix), in_specs=[v...]
where the time goes in v4:
time: 332 us; the launch traced here: 331 us
  Pallas kernels  296 us (89%)
  local copies, waits for them, and re-layouts  15.9 us (5%)
  blocking collectives  14.4 us (4%)
    pallas_call x1, Pallas kernels, chain_backward(): pl.pallas_call(functools.partial(bwd_kernel, block, heads, turn), grid=(n...  166 us
    pallas_call x1, Pallas kernels, chain_forward(): pl.pallas_call(functools.partial(fwd_kernel, block, unroll, heads), grid=...  62.3 us
    pallas_call x1, Pallas kernels, middle(): pl.pallas_call(functools.partial(mid_kernel, count), in_specs=[vmem] * le...  44.6 us
    pallas_call x1, Pallas kernels, tail(): pl.pallas_call(functools.partial(tail_kernel, count, at_mix), in_specs=[v...  21 us
    all_gather x1, blocking collectives, local(): whole_low = lax.all_gather(inputs, 'head', axis=1, tiled=True)  8.25 us
    unnamed x49, local copies, waits for them, and re-layouts  7.63 us

profile of v4, /device:TPU:0, one launch (start us, length us, event | category | flops | bytes accessed | tf_op | source)
XLA Modules:
  0.0 331.3 jit_solution(2751448410664507729)
XLA Ops:
  0.7 0.0 copy-start
  0.7 0.0 copy-start.19
  0.7 0.0 copy-start.13
  0.7 0.0 copy-start.14
  0.7 0.0 copy-start.15
  0.7 8.2 %all_gather.6 = bf16[256,768]{0,1:T(8,128)(2,1)S(1)} all-gather(bf16[256,192]{0,1:T(8,128)(2,1)} %param.22), channel_id=1, replica_groups=mesh['seq'=8,'head'=4] {'head'}, dimensions={1}, use_global_device_ids=true | all-gather | bytes 491520 | tf_op jit(solution)/shard_map/all_gather | solution.py:1176
  9.0 0.2 copy.83.x_ref
  9.1 0.0 copy-start.10
  9.2 0.2 fusion
  9.3 0.8 fusion.2.norm_ref.normed_ref
  10.2 0.0 copy-start.11
  10.2 0.0 copy-done.19
  10.2 0.0 copy-done.13
  10.3 0.0 copy-done.14
  10.3 0.0 copy-done.15
  10.3 0.0 copy-start.16
  10.3 1.1 concatenate.3
  11.4 0.0 copy-done
  11.4 0.1 broadcast_reduce_fusion
  11.6 1.3 subtract_convert_fusion.pay_ref
  12.9 0.0 copy-done.10
  12.9 0.0 copy-done.11
  12.9 0.0 copy-done.16
  12.9 0.0 copy-start.20
  13.0 1.0 copy.86.w2_in
  13.9 62.3 %inner_forward.1 = (bf16[3,256,64]{2,1,0:T(8,128)(2,1)}, bf16[8,256,768]{2,1,0:T(8,128)(2,1)}, bf16[2048,80]{1,0:T(8,128)(2,1)}, bf16[2048,80]{1,0:T(8,128)(2,1)...) custom-call(bf16[256,768]{1,0:T(8,128)(2,1)} %subtract_convert_fusio, ...), custom_call_target="tpu_custom_call" | custom-call | tf_op jit(solution)/shard_map/inner_forward/pallas_call | solution.py:467
  76.3 0.0 copy-done.12
  76.3 2.0 fusion.4.gate_pre_ref
  78.3 0.0 copy-done.17
  78.3 6.1 %all_gather.7 = bf16[256,768]{0,1:T(8,128)(2,1)S(1)} all-gather(bf16[256,192]{0,1:T(8,128)(2,1)S(1)} %copy-done.17), channel_id=1, replica_groups=mesh['seq'=8,'head'=4] {'head'}, dimensions={1}, use_global_device_ids=true | all-gather | bytes 491520 | tf_op jit(solution)/shard_map/all_gather | solution.py:1178
  84.4 0.9 copy.88.ct_ref
  85.3 0.0 copy-done.20
  85.3 0.6 broadcast_in_dim.52.ffn_gain_ref
  85.9 44.6 %middle.1 = (bf16[3,256,64]{2,1,0:T(8,128)(2,1)}, bf16[768,1920]{1,0:T(8,128)(2,1)}, bf16[256,192]{1,0:T(8,128)(2,1)}, f32[256,192]{1,0:T(8,128)}, f32[256,192]{...) custom-call(bf16[3,256,64]{2,1,0:T(8,128)(2,1)} %get-tuple-element.68.mixed_ref, bf16[256,768]{1,0:T(8,128)(2,1)} %copy-done.10, ...), custom_call_target="tpu_custom_call" | custom-call | tf_op jit(solution)/shard_map/middle/pallas_call | solution.py:963
  130.6 166.3 %inner_backward.1 = (bf16[3,256,256]{2,1,0:T(8,128)(2,1)}, bf16[3,160,256]{2,1,0:T(8,128)(2,1)}, bf16[3,96,256]{2,1,0:T(8,128)(2,1)}, f32[96,1920]{1,0:T(8,128)}, f32[8,8,768]{2,1,0:T(8,128)}) custom-call(bf16[3,256,64]{2,1,0:T(8,128)(2,1)} %get-tuple-element.71.gm_ref, bf16[4,2,96,1920]{3,2,1,0:T(8,128)(2,1)} %bitcast.18, ...), custom_call_target="tpu_custom_call" | custom-call | tf_op jit(solution)/shard_map/inner_backward/pallas_call | solution.py:708
  296.9 0.0 copy-start.18
  296.9 1.5 copy.90.packed_w_ref
  298.4 0.0 copy-start.5
  298.4 0.0 copy-start.7
  298.4 0.9 copy.91.mix_gate_ref
  299.3 0.0 copy-done.18
  299.3 0.6 broadcast_in_dim.53.pre_gain_ref
  299.9 21.0 %tail.1 = (f32[256,192]{1,0:T(8,128)}, f32[8,8,128]{2,1,0:T(8,128)}) custom-call(bf16[3,256,256]{2,1,0:T(8,128)(2,1)} %get-tuple-element.86.grads_ref, bf16[768,768]{1,0:T(8,128)(2,1)} %copy.90.packed_w_ref, bf16[768,192]{1,0:T(8,128)(2,1)} %copy.91.mix_gate_ref, bf16[256,192]{1,0:T(8,128)(2,1)} %get-tuple-element.87.ggp_ref, bf16[256,768]{1,0:T(8,128)(2,1)} %copy-done.10, ...), custom_call_target="tpu_custom_call" | custom-call | tf_op jit(solution)/shard_map/tail/pallas_call | solution.py:1076
  320.8 0.0 copy-done.1
  320.9 0.0 copy-done.2
  320.9 0.0 copy-done.3
  320.9 0.0 copy-done.4
  320.9 0.0 copy-done.5
  320.9 0.0 copy-done.7
  320.9 0.0 copy-done.8
  320.9 0.9 copy-done.6
  321.9 0.8 copy-done.9
  322.6 1.4 final.1
  324.0 0.8 copy.93
  324.8 0.8 copy.94
  325.6 0.8 copy.96
  326.4 0.8 copy.97
  327.3 0.7 copy.95
  328.0 0.6 slice_reduce_fusion.1
  328.6 0.6 fusion.3
  329.2 0.6 slice_reduce_fusion.2
  329.8 0.8 slice_reduce_fusion
  330.6 0.1 reshape_squeeze.3
  330.7 0.6 dynamic_slice.3
  (21 shorter events, 0.1 us)
Async XLA Ops:
  0.7 10.8 %copy-start = (f32[3]{0:T(128)S(1)}, f32[3]{0:T(128)}, u32[]{:S(2)}) copy-start(f32[3]{0:T(128)} %param.29) | copy-start | bytes 40
  0.7 9.5 %copy-start.19 = (bf16[768,3]{0,1:T(4,128)(2,1)S(1)}, bf16[768,3]{0,1:T(4,128)(2,1)}, u32[]{:S(2)}) copy-start(bf16[768,3]{0,1:T(4,128)(2,1)} %param.28) | copy-start | bytes 13828
  0.7 9.6 %copy-start.13 = (bf16[768,192]{0,1:T(8,128)(2,1)S(1)}, bf16[768,192]{0,1:T(8,128)(2,1)}, u32[]{:S(2)}) copy-start(bf16[768,192]{0,1:T(8,128)(2,1)} %param.24) | copy-start | bytes 884740
  0.7 9.6 %copy-start.14 = (bf16[768,192]{0,1:T(8,128)(2,1)S(1)}, bf16[768,192]{0,1:T(8,128)(2,1)}, u32[]{:S(2)}) copy-start(bf16[768,192]{0,1:T(8,128)(2,1)} %param.25) | copy-start | bytes 884740
  0.7 9.6 %copy-start.15 = (bf16[768,192]{0,1:T(8,128)(2,1)S(1)}, bf16[768,192]{0,1:T(8,128)(2,1)}, u32[]{:S(2)}) copy-start(bf16[768,192]{0,1:T(8,128)(2,1)} %param.26) | copy-start | bytes 884740
  9.1 3.8 %copy-start.10 = (bf16[256,768]{1,0:T(8,128)(2,1)}, bf16[256,768]{1,0:T(8,128)(2,1)S(1)}, u32[]{:S(2)}) copy-start(bf16[256,768]{1,0:T(8,128)(2,1)S(1)} %copy.83.x_ref) | copy-start | bytes 1179652
  10.2 2.8 copy-start.11
  10.3 2.7 copy-start.16
  11.6 64.7 %copy-start.12 = (bf16[768,192]{0,1:T(8,128)(2,1)S(1)}, bf16[768,192]{0,1:T(8,128)(2,1)}, u32[]{:S(2)}) copy-start(bf16[768,192]{0,1:T(8,128)(2,1)} %param.27) | copy-start | bytes 884740
  12.9 65.3 %copy-start.17 = (bf16[256,192]{0,1:T(8,128)(2,1)S(1)}, bf16[256,192]{0,1:T(8,128)(2,1)}, u32[]{:S(2)}) copy-start(bf16[256,192]{0,1:T(8,128)(2,1)} %param.43) | copy-start | bytes 294916
  12.9 72.4 %copy-start.20 = (f32[768]{0:T(1024)S(1)}, f32[768]{0:T(1024)}, u32[]{:S(2)}) copy-start(f32[768]{0:T(1024)} %param.39) | copy-start | bytes 9220
  296.9 2.4 copy-start.18
  298.3 22.5 %copy-start.1 = (f32[96,1920]{1,0:T(8,128)S(1)}, f32[96,1920]{1,0:T(8,128)}, u32[]{:S(2)}) copy-start(f32[96,1920]{1,0:T(8,128)} %get-tuple-element.89.early_ref) | copy-start | bytes 2211844
  298.3 22.5 %copy-start.2 = (bf16[3,96,256]{2,1,0:T(8,128)(2,1)S(1)}, bf16[3,96,256]{2,1,0:T(8,128)(2,1)}, u32[]{:S(2)}) copy-start(bf16[3,96,256]{2,1,0:T(8,128)(2,1)} %get-tuple-element.88.late_ref) | copy-start | bytes 442372
  298.3 22.5 %copy-start.3 = (f32[256,192]{1,0:T(8,128)S(1)}, f32[256,192]{1,0:T(8,128)}, u32[]{:S(2)}) copy-start(f32[256,192]{1,0:T(8,128)} %get-tuple-element.69.down_ref) | copy-start | bytes 589828
  298.3 22.5 %copy-start.4 = (f32[256,192]{1,0:T(8,128)S(1)}, f32[256,192]{1,0:T(8,128)}, u32[]{:S(2)}) copy-start(f32[256,192]{1,0:T(8,128)} %get-tuple-element.70.resid_ref) | copy-start | bytes 589828
  298.4 22.5 %copy-start.5 = (f32[256,192]{1,0:T(8,128)S(1)}, f32[256,192]{1,0:T(8,128)}, u32[]{:S(2)}) copy-start(f32[256,192]{1,0:T(8,128)} %get-tuple-element.91.grc_ref) | copy-start | bytes 589828
  298.4 22.5 %copy-start.7 = (bf16[3,160,256]{2,1,0:T(8,128)(2,1)S(1)}, bf16[3,160,256]{2,1,0:T(8,128)(2,1)}, u32[]{:S(2)}) copy-start(bf16[3,160,256]{2,1,0:T(8,128)(2,1)} %get-tuple-element.92.ends_ref) | copy-start | bytes 737284
  299.3 21.6 %copy-start.8 = (f32[8,8,768]{2,1,0:T(8,128)S(1)}, f32[8,8,768]{2,1,0:T(8,128)}, u32[]{:S(2)}) copy-start(f32[8,8,768]{2,1,0:T(8,128)} %get-tuple-element.94.small_ref) | copy-start | bytes 589828
  320.9 1.0 copy-start.6
  321.9 0.8 copy-start.9

commit v5 on v4

--- a/solution.py
+++ b/solution.py
@@ -60,54 +60,76 @@
     return jnp.where(rows >= cols, 1.0, 0.0).astype(f32)
 
 
-def inner_target_grad(z, base, gain_sq, rate):
+def forward_output(kept, gain, bias, tri, sink):
+    z1b, act_h, w2_h, b2, s2_h = kept
+    actb, _ = gelu_first(z1b)
+    actb_h = actb.astype(bf16)
+    yield
+    att = dot_nt(actb_h, act_h)
+    z2b = dot_nt(actb_h, w2_h) + b2
+    yield
+    z2b = z2b - dot_nn(((att + 1.0) * tri).astype(bf16), s2_h)
+    yield
+    z2b = z2b - mean_row(z2b)
+    yield
+    invb = lax.rsqrt(mean_row(z2b * z2b) + eps_norm)
+    sink(z2b * invb * gain + bias, z2b)
+    yield
+
+
+def forward_chain(state, z1, post, key_aug, key_next, query_aug, base, rate, gain_sq, tri, save):
+    w1, w2t, b2 = state
+    width = gain_sq.shape[1]
+    scale = 1.0 / width
+    w2_h = w2t.astype(bf16)
+    act, der = gelu_first(z1)
+    act_h = act.astype(bf16)
+    z = dot_nt(act_h, w2_h) + b2
+    next(post, None)
+    fixed = dot_nn(
+        jnp.concatenate([base, jnp.broadcast_to(gain_sq, (8, width)), jnp.ones((8, width), f32)], axis=0).astype(bf16),
+        w2_h)
+    both = jnp.concatenate([key_next, query_aug], axis=0)
+    coef = dot_nt(both, key_aug)
+    coef = jnp.concatenate([coef[:MINI], coef[MINI:] * tri], axis=0).astype(bf16)
+    m_b = mean_row(base)
+    m_sq = mean_row(gain_sq)
+    w1_h = w1.astype(bf16)
+    next(post, None)
+    zg = z * gain_sq
+    prods = dot_nn(jnp.concatenate([zg, z], axis=0).astype(bf16), w2_h)
     mz = mean_row(z)
     m_zz = mean_row(z * z)
-    zg = z * gain_sq
     m_zg = mean_row(zg)
     m_zzg = mean_row(zg * z)
     m_zb = mean_row(z * base)
-    m_b = mean_row(base)
-    m_sq = mean_row(gain_sq)
+    zz = dot_nn(both, w1_h)
+    next(post, None)
     inv = lax.rsqrt(m_zz - mz * mz + eps_norm)
     c_zg = m_zg - mz * m_sq
     c_zzg = m_zzg - mz * (m_zg + c_zg)
     c_zb = m_zb - mz * m_b
     m_g = inv * c_zg + m_b
     m_gn = inv * (inv * c_zzg + c_zb)
+    rinv = rate * inv
+    rinv2 = rinv * inv
+    skew = rinv2 * m_gn
+    shift = skew * mz - rinv * m_g
+    upd = (rinv2 * prods[:MINI] - skew * prods[MINI:]) + (
+        (rinv * fixed[:MINI] + shift * fixed[MINI + 8 : MINI + 9]) - (rinv2 * mz) * fixed[MINI : MINI + 1])
+    s1_h = (upd * der).astype(bf16)
+    zz = zz - dot_nn(coef, s1_h)
     zc = z - mz
-    n = zc * inv
-    grad = inv * (n * (gain_sq - m_gn) + (base - m_g))
-    return rate * grad, zc
-
-
-def forward_step(state, z1, key_aug, key_next, query_aug, base, rate, gain, gain_sq, bias, tri):
-    w1, w2t, b2 = state
-    act, der = gelu_first(z1)
-    act_h = act.astype(bf16)
-    w1_h = w1.astype(bf16)
-    w2_h = w2t.astype(bf16)
-    s2, zc = inner_target_grad(dot_nt(act_h, w2_h) + b2, base, gain_sq, rate)
+    s2 = rinv2 * zc * gain_sq - skew * zc + (rinv * base - rinv * m_g)
     s2_h = s2.astype(bf16)
-    upd = dot_nn(s2_h, w2_h)
-    s1_h = (upd * der).astype(bf16)
-    both = jnp.concatenate([key_next, query_aug], axis=0)
-    coef = dot_nt(both, key_aug)
-    coef = jnp.concatenate([coef[:MINI], coef[MINI:] * tri], axis=0)
-    zz = dot_nn(both, w1_h) - dot_nn(coef.astype(bf16), s1_h)
-    z1_next = zz[:MINI]
+    new_w2t = w2t - dot_tn(s2_h, act_h)
+    new_w1 = w1 - dot_tn(key_aug, s1_h)
+    new_b2 = b2 - jnp.sum(s2, axis=0, keepdims=True)
+    next(post, None)
+    next(post, None)
     z1b = zz[MINI:]
-    new_w1 = w1 - dot_tn(key_aug, s1_h)
-    new_w2t = w2t - dot_tn(s2_h, act_h)
-    new_b2 = b2 - jnp.sum(s2, axis=0, keepdims=True)
-    actb, _ = gelu_first(z1b)
-    actb_h = actb.astype(bf16)
-    att = (dot_nt(actb_h, act_h) + 1.0) * tri
-    z2b = dot_nt(actb_h, w2_h) + b2 - dot_nn(att.astype(bf16), s2_h)
-    z2b = z2b - mean_row(z2b)
-    invb = lax.rsqrt(mean_row(z2b * z2b) + eps_norm)
-    out = z2b * invb * gain + bias
-    return (new_w1, new_w2t, new_b2), z1_next, out, (w1_h, w2_h, upd, zc, s2, z1b, z2b)
+    save(w1_h, w2_h, z1, upd, zc, s2, z1b)
+    return (new_w1, new_w2t, new_b2), zz[:MINI], (z1b, act_h, w2_h, b2, s2_h)
 
 
 def prepare_back(store, saved, d_out, key_aug, query_aug, target, rate, gain, gain_sq, bias, tri):
@@ -301,10 +323,10 @@
     await_bytes(dst.at[pos], local_sem)
 
 
-def fwd_kernel(block, unroll, heads, pay_ref, norm_ref, w1_in, b1_in, w2_in, b2_in, gain_in, bias_in,
-               mixed_ref, norm_out, k_out, q_out, aux_out, w1s_ref, w2s_ref, z1s_ref, upd_ref, zc_ref, s2_ref, z1b_ref, z2b_ref,
+def fwd_kernel(block, heads, count, pay_ref, ct_ref, w1_in, b1_in, w2_in, b2_in, gain_in, bias_in,
+               mixed_ref, ct_out, k_out, q_out, aux_out, w1s_ref, w2s_ref, z1s_ref, upd_ref, zc_ref, s2_ref, z1b_ref, z2b_ref,
                got, k_all, q_all, base_all, aux_all, mixed_all, w1, w2t, b2, z1,
-               pay_send, pay_recv, mix_send, mix_recv, no_send, no_recv):
+               pay_send, pay_recv, mix_send, mix_recv, ct_send, ct_recv, ct_loc):
     blk = pl.program_id(0)
     last = pl.num_programs(0) - 1
     pos, base = seq_place()
@@ -312,6 +334,8 @@
     hidden = w1.shape[1]
     rows_each = pay_ref.shape[0]
     per = rows_each // block
+    piece = got.shape[1]
+    parts = rows_each // piece
     owner = (pos >= FIRST) & (pos < FIRST + heads)
     mine = jnp.clip(pos - FIRST, 0, heads - 1)
     gain = gain_in[pl.ds(mine, 1), :]
@@ -319,35 +343,41 @@
     gain_sq = gain * gain
     tri = tri_mask()
 
+    me, _ = head_place()
+
     @pl.when(blk == 0)
     def _():
-        meet_group(pos, base)
-        for j in range(heads):
-            src = pay_ref.at[:, pl.ds(j * PACK, PACK)]
-            dst = got.at[pos]
-
-            @pl.when(pos != FIRST + j)
-            def _():
-                push(src, dst, pay_send.at[j], pay_recv.at[pos], base + FIRST + j).start()
-
-            @pl.when(pos == FIRST + j)
-            def _():
-                pltpu.make_async_copy(src, dst, pay_recv.at[pos]).start()
-
-        for j in range(heads):
-            @pl.when(pos != FIRST + j)
-            def _():
-                push(norm_ref, norm_out.at[pos], no_send.at[j], no_recv.at[pos], base + FIRST + j).start()
-
-            @pl.when(pos == FIRST + j)
-            def _():
-                pltpu.make_async_copy(norm_ref, norm_out.at[pos], no_recv.at[pos]).start()
+        barrier = pltpu.get_barrier_semaphore()
+        for d in range(1, count):
+            pl.semaphore_signal(barrier, inc=1, device_id={"head": lax.rem(me + d, count)}, device_id_type=MESH)
+        for d in range(1, CHAIN):
+            pl.semaphore_signal(
+                barrier, inc=1, device_id={"seq": base + lax.rem(pos + d, CHAIN)}, device_id_type=MESH)
+        pl.semaphore_wait(barrier, CHAIN - 1 + count - 1)
+        for s in range(parts):
+            for j in range(heads):
+                src = pay_ref.at[s * piece : (s + 1) * piece, j * PACK : (j + 1) * PACK]
+                dst = got.at[pos * parts + s]
+
+                @pl.when(pos != FIRST + j)
+                def _():
+                    push(src, dst, pay_send.at[j], pay_recv.at[pos * parts + s], base + FIRST + j).start()
+
+                @pl.when(pos == FIRST + j)
+                def _():
+                    pltpu.make_async_copy(src, dst, pay_recv.at[pos * parts + s]).start()
+
+    @pl.when(blk == 1)
+    def _():
+        for d in range(1, count):
+            push_head(ct_ref, ct_out.at[me], ct_send.at[d - 1], ct_recv.at[d - 1], lax.rem(me + d, count)).start()
+        pltpu.make_async_copy(ct_ref, ct_out.at[me], ct_loc).start()
 
     def take_in(p):
         await_bytes(got.at[p], pay_recv.at[p])
         part = got[p]
-        rows = pl.ds(pl.multiple_of(p * rows_each, rows_each), rows_each)
-        lane = lax.broadcasted_iota(jnp.int32, (rows_each, AUG), 1)
+        rows = pl.ds(pl.multiple_of(p * piece, piece), piece)
+        lane = lax.broadcasted_iota(jnp.int32, (piece, AUG), 1)
         one = jnp.ones((), bf16)
         zero = jnp.zeros((), bf16)
         tail = jnp.where(lane == width, one, zero)
@@ -360,7 +390,7 @@
         logit = part[:, 3 * width : 3 * width + 1].astype(f32) + part[:, 3 * width + 1 : 3 * width + 2].astype(f32)
         sig = 1.0 / (1.0 + jnp.exp(-logit))
         base_all[rows, :] = (bias - target) * gain
-        spot = lax.broadcasted_iota(jnp.int32, (rows_each, 2 * width), 1)
+        spot = lax.broadcasted_iota(jnp.int32, (piece, 2 * width), 1)
         wide = jnp.concatenate([target, target], axis=1)
         aux_all[rows, :] = jnp.where(
             spot < width, wide, jnp.where(spot == width, sig * (1.0 / width), 1.0 - sig))
@@ -385,52 +415,62 @@
             row = lax.broadcasted_iota(jnp.int32, (AUG - width, hidden), 0)
             w1[pl.ds(0, width), :] = w1_in[mine]
             w1[pl.ds(width, AUG - width), :] = jnp.where(row == 0, b1_in[pl.ds(mine, 1), :], 0.0)
-            turned = w2_in[mine].T
+            turned = w2_in[mine]
             w2t[...] = turned - jnp.mean(turned, axis=0, keepdims=True)
             start = b2_in[pl.ds(mine, 1), :]
             b2[...] = start - mean_row(start)
             k_all[pl.ds(CHAIN * rows_each, MINI), :] = jnp.zeros((MINI, AUG), bf16)
-            take_in(0)
+
+        @pl.when(blk > 0)
+        def _():
+            send_mixed(blk - 1)
+
+        def bring(p, _):
+            take_in(p)
+            return 0
+
+        lax.fori_loop(jnp.where(blk == 0, 0, 2 * blk + 1), jnp.minimum(2 * blk + 3, 2 * last + 2), bring, 0)
+
+        @pl.when(blk == 0)
+        def _():
             z1[...] = dot_nn(k_all[0:MINI, :], w1[...].astype(bf16))
 
-        @pl.when((lax.rem(blk, per) == 0) & (blk < last + 1 - per))
-        def _():
-            take_in(lax.div(blk, per) + 1)
-
-        @pl.when(blk > 0)
-        def _():
-            send_mixed(blk - 1)
+        state = (w1[...], w2t[...], b2[...])
+        z1_now = z1[...]
+        post = iter(())
+        for loc in range(block // MINI):
+            row = pl.multiple_of(blk * block + loc * MINI, MINI)
+            rows = pl.ds(row, MINI)
+            lr = pl.ds(loc * MINI, MINI)
+            q_aug = q_all[rows, :]
+
+            def save(w1_h, w2_h, z1_v, upd, zc, s2, z1b, loc=loc, lr=lr):
+                w1s_ref[loc] = w1_h
+                w2s_ref[loc] = w2_h
+                z1s_ref[lr, :] = z1_v
+                upd_ref[lr, :] = upd
+                zc_ref[lr, :] = zc
+                s2_ref[lr, :] = s2
+                z1b_ref[lr, :] = z1b
+
+            state, z1_now, kept = forward_chain(
+                state, z1_now, post, k_all[rows, :], k_all[pl.ds(row + MINI, MINI), :], q_aug,
+                base_all[rows, :], aux_all[rows, width : width + 1], gain_sq, tri, save)
+
+            def sink(out, z2b, lr=lr, rows=rows, q_aug=q_aug):
+                z2b_ref[lr, :] = z2b
+                mixed_all[rows, :] = (out + q_aug[:, :width].astype(f32)).astype(bf16)
+
+            post = forward_output(kept, gain, bias, tri, sink)
+        drain(post)
+        w1[...], w2t[...], b2[...] = state
+        z1[...] = z1_now
 
         brows = pl.ds(pl.multiple_of(blk * block, block), block)
         k_out[...] = k_all[brows, :]
         q_out[...] = q_all[brows, :]
         aux_out[...] = aux_all[brows, :]
 
-        def group(it, _):
-            for u in range(unroll):
-                loc = it * unroll + u
-                row = pl.multiple_of(blk * block + loc * MINI, MINI)
-                rows = pl.ds(row, MINI)
-                lrows = pl.ds(pl.multiple_of(loc * MINI, MINI), MINI)
-                q_aug = q_all[rows, :]
-                z1_now = z1[...]
-                state, z1_next, out, saved = forward_step(
-                    (w1[...], w2t[...], b2[...]), z1_now, k_all[rows, :], k_all[pl.ds(row + MINI, MINI), :], q_aug,
-                    base_all[rows, :], aux_all[rows, width : width + 1], gain, gain_sq, bias, tri)
-                w1[...], w2t[...], b2[...] = state
-                z1[...] = z1_next
-                mixed_all[rows, :] = (out + q_aug[:, :width].astype(f32)).astype(bf16)
-                w1s_ref[loc], w2s_ref[loc], upd, zc, s2, z1b, z2b = saved
-                z1s_ref[lrows, :] = z1_now
-                upd_ref[lrows, :] = upd
-                zc_ref[lrows, :] = zc
-                s2_ref[lrows, :] = s2
-                z1b_ref[lrows, :] = z1b
-                z2b_ref[lrows, :] = z2b
-            return 0
-
-        lax.fori_loop(0, block // MINI // unroll, group, 0)
-
     @pl.when(blk == last)
     def _():
         @pl.when(owner)
@@ -438,21 +478,24 @@
             send_mixed(last)
             others = mixed_all.at[pl.ds(0, (CHAIN - 1) * rows_each), :]
             await_bytes(others, mix_send)
-            for p in range(CHAIN):
-                await_bytes(norm_out.at[p], no_recv.at[p])
-
         for j in range(heads):
             @pl.when(pos != FIRST + j)
             def _():
-                await_bytes(got.at[pos], pay_send.at[j])
-                await_bytes(norm_ref, no_send.at[j])
+                await_bytes(got.at[pl.ds(0, parts)], pay_send.at[j])
 
             await_bytes(mixed_ref.at[j], mix_recv.at[j])
 
-
-def chain_forward(payload, normed, w1, b1, w2, b2, gain, bias, block=128, unroll=8):
+        for d in range(1, count):
+            push_head(ct_ref, ct_out.at[me], ct_send.at[d - 1], ct_recv.at[d - 1],
+                      lax.rem(me + d, count)).wait_send()
+            await_bytes(ct_out.at[lax.rem(me + count - d, count)], ct_recv.at[d - 1])
+        await_bytes(ct_out.at[me], ct_loc)
+
+
+def chain_forward(payload, ct, w1, b1, w2, b2, gain, bias, block=256):
     rows = payload.shape[0]
     heads, width, hidden = w1.shape
+    count = lax.axis_size("head")
     tokens = rows * CHAIN
     steps = tokens // MINI
     nb = block // MINI
@@ -465,33 +508,33 @@
     wide = jax.ShapeDtypeStruct((tokens, hidden), f32)
     narrow = jax.ShapeDtypeStruct((tokens, width), f32)
     return pl.pallas_call(
-        functools.partial(fwd_kernel, block, unroll, heads),
+        functools.partial(fwd_kernel, block, heads, count),
         grid=(tokens // block,),
         in_specs=[anywhere, anywhere] + [whole(a) for a in small],
         out_specs=[anywhere, anywhere, rowblk(AUG), rowblk(AUG), rowblk(2 * width), stepblk(AUG), stepblk(width),
                    rowblk(hidden), rowblk(hidden), rowblk(width), rowblk(width), rowblk(hidden), rowblk(width)],
         out_shape=[jax.ShapeDtypeStruct((heads, rows, width), bf16),
-                   jax.ShapeDtypeStruct((CHAIN,) + normed.shape, bf16),
+                   jax.ShapeDtypeStruct((count,) + ct.shape, bf16),
                    jax.ShapeDtypeStruct((tokens, AUG), bf16),
                    jax.ShapeDtypeStruct((tokens, AUG), bf16),
                    jax.ShapeDtypeStruct((tokens, 2 * width), f32),
                    jax.ShapeDtypeStruct((steps, AUG, hidden), bf16),
                    jax.ShapeDtypeStruct((steps, width, hidden), bf16),
                    wide, wide, narrow, narrow, wide, narrow],
-        scratch_shapes=[pltpu.VMEM((CHAIN, rows, PACK), bf16),
+        scratch_shapes=[pltpu.VMEM((2 * tokens // block, block // 2, PACK), bf16),
                         pltpu.VMEM((tokens + MINI, AUG), bf16), pltpu.VMEM((tokens, AUG), bf16),
                         pltpu.VMEM((tokens, width), f32), pltpu.VMEM((tokens, 2 * width), f32),
                         pltpu.VMEM((tokens, width), bf16),
                         pltpu.VMEM((AUG, hidden), f32), pltpu.VMEM((width, hidden), f32),
                         pltpu.VMEM((1, width), f32), pltpu.VMEM((MINI, hidden), f32),
-                        dma((heads,)), dma((CHAIN,)), dma, dma((heads,)),
-                        dma((heads,)), dma((CHAIN,))],
+                        dma((heads,)), dma((2 * tokens // block,)), dma, dma((heads,)),
+                        dma((count - 1,)), dma((count - 1,)), dma],
         compiler_params=pltpu.CompilerParams(collective_id=0, has_side_effects=True),
         name="inner_forward",
-    )(payload, normed, *small)
-
-
-def bwd_kernel(block, heads, turn, gm_ref, early_ref, small_ref, gain_in, bias_in, norm_ref,
+    )(payload, ct, *small)
+
+
+def bwd_kernel(block, heads, turn, gm_ref, early_ref, small_ref, gain_in, bias_in, norm_ref, norm_last_ref,
                k_ref, q_ref, aux_ref, w1s_ref, w2s_ref, z1s_ref, upd_ref, zc_ref, s2_ref, z1b_ref, z2b_ref,
                grads_ref, ends_ref, late_ref, early_out, small_out,
                dout, half_got, half_mine, quarter, quarter_got, packed, ends, weights, late,
@@ -567,9 +610,11 @@
 
     share = late.shape[1]
 
-    def weigh(b, lo, hi):
+    def weigh(norm, b, lo, hi):
         rows = pl.ds(pl.multiple_of(b * block, block), block)
-        weights[lo:hi, :] += dot_tn(norm_ref[:, lo:hi], packed[rows, :])
+        weights[lo:hi, :] += dot_tn(norm[:, lo:hi], packed[rows, :])
+
+    slabs = [(i * 128, i * 128 + 128) for i in range(norm_ref.shape[1] // 128)]
 
     @pl.when(owner)
     def _():
@@ -577,6 +622,7 @@
         def _():
             for r in state + (dg, db, dl, weights):
                 r[...] = jnp.zeros_like(r)
+            packed[pl.ds(0, block), :] = jnp.zeros((block, PACK), bf16)
 
         @pl.when(lax.rem(pid, per) == 0)
         def _():
@@ -620,15 +666,14 @@
                 rows = pl.ds(pl.multiple_of(blk * block + loc * MINI, MINI), MINI)
                 packed[rows, :] = jnp.concatenate([d_query, d_key, d_value, extra], axis=1).astype(bf16)
 
+            if (count - 1 - loc) % 2 == 0 and (count - 1 - loc) // 2 < len(slabs):
+                weigh(norm_ref, jnp.where(pid == 0, 0, blk + 1), *slabs[(count - 1 - loc) // 2])
             carry, post = backward_chain(
                 carry, made.pop(loc), post, fill, aux_ref[pl.ds(loc * MINI, MINI), width + 1 : width + 2], gain, sink)
         drain(settle(post, width))
         for r, v in zip(state, carry):
             r[...] = v
         dg[...], db[...], dl[...] = totals
-        quarter_rows = norm_ref.shape[1] // 4
-        for i in range(4):
-            weigh(blk, i * quarter_rows, (i + 1) * quarter_rows)
 
         @pl.when(pid == last)
         def _():
@@ -642,6 +687,8 @@
             tailing = tailing + jnp.where(row == 3, high, jnp.where(row == 4, dl[...] - high, 0.0))
             ends[pl.ds(AUG + width, rest), :] = jnp.concatenate([tailing] * 4, axis=1).astype(bf16)
             share_block(0)
+            for slab in slabs:
+                weigh(norm_last_ref, 0, *slab)
             for p in range(CHAIN):
                 late[p] = weights[p * share : (p + 1) * share, :].astype(bf16)
             for d in range(1, CHAIN):
@@ -691,7 +738,7 @@
                 await_bytes(late.at[0], la_send.at[d - 1])
 
 
-def chain_backward(grad_mixed, early, small, gain, bias, normed, saved, block=128, turn=6):
+def chain_backward(grad_mixed, early, small, gain, bias, normed, saved, block=256, turn=3):
     heads, rows, width = grad_mixed.shape
     tokens = rows * CHAIN
     hidden = saved[5].shape[1]
@@ -700,6 +747,8 @@
     whole = lambda a: pl.BlockSpec(a.shape, lambda i: (0,) * a.ndim)
     rowblk = lambda w: pl.BlockSpec((block, w), lambda i: (nblk - 1 - i, 0))
     stepblk = lambda r: pl.BlockSpec((nb, r, hidden), lambda i: (nblk - 1 - i, 0, 0))
+    behind = pl.BlockSpec((block, normed.shape[1]), lambda i: (jnp.minimum(nblk - i, nblk - 1), 0))
+    first = pl.BlockSpec((block, normed.shape[1]), lambda i: (0, 0))
     anywhere = pl.BlockSpec(memory_space=pl.ANY)
     dma = pltpu.SemaphoreType.DMA
     seven = dma((CHAIN - 1,))
@@ -708,7 +757,7 @@
     return pl.pallas_call(
         functools.partial(bwd_kernel, block, heads, turn),
         grid=(nblk,),
-        in_specs=[anywhere] * 3 + [whole(gain), whole(bias), rowblk(normed.shape[1]), rowblk(AUG), rowblk(AUG),
+        in_specs=[anywhere] * 3 + [whole(gain), whole(bias), behind, first, rowblk(AUG), rowblk(AUG),
                                    rowblk(2 * width), stepblk(AUG), stepblk(width), rowblk(hidden), rowblk(hidden), rowblk(width),
                                    rowblk(width), rowblk(hidden), rowblk(width)],
         out_specs=[anywhere, anywhere, anywhere, pl.BlockSpec(share, lambda i: (0, 0)), anywhere],
@@ -731,7 +780,7 @@
                         dma, dma((heads,)), seven, dma((heads,)), seven, dma((heads,))],
         compiler_params=pltpu.CompilerParams(collective_id=1, has_side_effects=True),
         name="inner_backward",
-    )(grad_mixed, early, small, gain, bias, normed, *saved)
+    )(grad_mixed, early, small, gain, bias, normed, normed, *saved)
 
 
 def head_place():
@@ -763,20 +812,31 @@
     return jnp.where(row == 0, top, low)
 
 
-def mid_kernel(count, mixed_ref, x_ref, ct_ref, gate_pre_ref, normed_ref, w_out_ref, w_gate_ref, w_up_ref, w_down_ref,
+def mid_kernel(count, mixed_ref, x_ref, ctt_ref, mix_gate_ref, normed_ref, w_out_ref, w_gate_ref, w_up_ref, w_down_ref,
                post_gain_ref, post_bias_ref, ffn_gain_ref,
-               gm_ref, early_ref, ggp_ref, out_ref, rco_ref, grc_ref, small_ref,
+               gm_ref, early_ref, ggp_ref, out_ref, rco_ref, grc_ref, small_ref, norm_out,
                st_mine, st_got, pa_mine, pa_got, nt_all, rc_mine, rc_all, gn_mine, gn_got, dn_mine, dn_got, gov_all,
-               gc_mine, gc_all, sb_mine, sb_got, gt_all, gh, gated, hidden, ggv, guv, resid,
+               gc_mine, gc_all, sb_mine, sb_got, gt_all, ct_ref, gh, gated, hidden, ggv, guv, resid,
                st_s, st_r, pa_s, pa_r, nt_s, nt_r, rc_s, rc_r, gn_s, gn_r, dn_s, dn_r, go_s, go_r, gc_s, gc_r, sb_s, sb_r,
-               gt_s, gt_r):
+               gt_s, gt_r, no_s, no_r):
     me, _ = head_place()
     heads, rows, width = mixed_ref.shape
     cols = heads * width
     full = cols * count
     part = rows // count
     peers = [(d, lax.rem(me + d, count)) for d in range(1, count)]
-    meet_heads(me, count)
+    pos, base = seq_place()
+    owner = (pos >= FIRST) & (pos < FIRST + heads)
+    barrier = pltpu.get_barrier_semaphore()
+    for d in range(1, count):
+        pl.semaphore_signal(barrier, inc=1, device_id={"head": lax.rem(me + d, count)}, device_id_type=MESH)
+    for d in range(1, CHAIN):
+        pl.semaphore_signal(
+            barrier, inc=1, device_id={"seq": base + lax.rem(pos + d, CHAIN)}, device_id_type=MESH)
+    pl.semaphore_wait(barrier, CHAIN - 1 + count - 1)
+    ffn_gain = ffn_gain_ref[...][None, :]
+    post_gain = post_gain_ref[...][None, :]
+    post_bias = post_bias_ref[...][None, :]
 
     def rows_of(device):
         return pl.ds(pl.multiple_of(device * part, part), part)
@@ -792,8 +852,17 @@
     z = jnp.concatenate([mixed_ref[j] for j in range(heads)], axis=1).astype(f32)
     st_mine[...] = row_totals(z, z * z)
     send_all(st_mine, st_got, st_s, st_r)
-    gate_pre = gate_pre_ref[...]
-    gate_act, gate_der = gelu_first(gate_pre)
+    for j in range(heads):
+        @pl.when(pos != FIRST + j)
+        def _():
+            push(normed_ref, norm_out.at[pos], no_s.at[j], no_r.at[pos], base + FIRST + j).start()
+
+        @pl.when(pos == FIRST + j)
+        def _():
+            pltpu.make_async_copy(normed_ref, norm_out.at[pos], no_r.at[pos]).start()
+
+    ct_ref[...] = ctt_ref[...].T
+    gate_act, gate_der = gelu_first(dot_nt(normed_ref[...], mix_gate_ref[...]))
     gh[...] = dot_nt(ct_ref[...], w_down_ref[...])
     wait_all(st_mine, st_got, st_s, st_r)
     tot = st_mine[...]
@@ -803,7 +872,7 @@
     mean_z = tot[:, 0:1]
     inv_z = lax.rsqrt(tot[:, 1:2] - mean_z * mean_z + eps_norm)
     z_hat = (z - mean_z) * inv_z
-    post_out = z_hat * post_gain_ref[...] + post_bias_ref[...]
+    post_out = z_hat * post_gain + post_bias
     gated[...] = (post_out * gate_act).astype(bf16)
 
     def spread_rows(make, mine, got, send, recv):
@@ -852,7 +921,6 @@
     own = spread_rows(lambda r: dot_nn(gated[r, :], w_out), pa_mine, pa_got, pa_s, pa_r)
     res = x_ref[rows_of(me), :].astype(f32) + add_rows(own, pa_mine, pa_got, pa_s, pa_r)
     rms_two = lax.rsqrt(mean_row(res * res) + eps_norm)
-    ffn_gain = ffn_gain_ref[...]
     nt_all[rows_of(me), :] = (res * rms_two * ffn_gain).astype(bf16)
     turn_columns(res, rc_mine, rc_all, rc_s, rc_r)
     resid[...] = res
@@ -907,7 +975,7 @@
     gov = gov_all[...]
     grad_gated = dot_nt(gov, w_out_ref[...])
     grad_post = grad_gated * gate_act
-    grad_zhat = grad_post * post_gain_ref[...]
+    grad_zhat = grad_post * post_gain
     sb_mine[...] = row_totals(grad_zhat, grad_zhat * z_hat)
     ggp = (grad_gated * post_out * gate_der).astype(bf16)
     ggp_ref[...] = ggp
@@ -925,7 +993,7 @@
         gm_ref[j] = grad_mixed[:, j * width : (j + 1) * width]
     for b in range(2):
         r = slice(b * half, (b + 1) * half)
-        early_ref[r, 2 * ffn : 3 * ffn] = dot_tn(ct_ref[:, r], hidden[...]).astype(bf16)
+        early_ref[r, 2 * ffn : 3 * ffn] = dot_nn(ctt_ref[r, :], hidden[...]).astype(bf16)
     turn_wait(rc_mine, rc_all, rc_s, rc_r)
     rco_ref[...] = rc_all[...]
     out = dn_mine[me].astype(f32)
@@ -946,16 +1014,25 @@
     line = lax.broadcasted_iota(jnp.int32, (8, full), 0)
     small_ref[...] = jnp.where(
         line == 0, gain_two, jnp.concatenate([post] + [jnp.zeros_like(post)] * (count - 1), axis=1))
-
-
-def middle(mixed, x, ct, gate_pre, normed, w_out, w_gate, w_up, w_down, post_gain, post_bias, ffn_gain):
+    for j in range(heads):
+        @pl.when(pos != FIRST + j)
+        def _():
+            await_bytes(normed_ref, no_s.at[j])
+
+    @pl.when(owner)
+    def _():
+        for p in range(CHAIN):
+            await_bytes(norm_out.at[p], no_r.at[p])
+
+
+def middle(mixed, x, ct, mix_gate, normed, w_out, w_gate, w_up, w_down, post_gain, post_bias, ffn_gain):
     count = lax.axis_size("head")
     heads, rows, width = mixed.shape
     cols = heads * width
     full = cols * count
     part = rows // count
     ffn = w_gate.shape[1]
-    ins = (mixed, x, ct, gate_pre, normed, w_out, w_gate, w_up, w_down, post_gain, post_bias, ffn_gain)
+    ins = (mixed, x, ct, mix_gate, normed, w_out, w_gate, w_up, w_down, post_gain, post_bias, ffn_gain)
     vmem = pl.BlockSpec(memory_space=pltpu.VMEM)
     V = pltpu.VMEM
     trio = count - 1
@@ -963,14 +1040,15 @@
     return pl.pallas_call(
         functools.partial(mid_kernel, count),
         in_specs=[vmem] * len(ins),
-        out_specs=[vmem] * 7,
+        out_specs=[vmem] * 7 + [pl.BlockSpec(memory_space=pl.ANY)],
         out_shape=[jax.ShapeDtypeStruct((heads, rows, width), bf16),
                    jax.ShapeDtypeStruct((full, 3 * ffn + 2 * cols), bf16),
                    jax.ShapeDtypeStruct((rows, cols), bf16),
                    jax.ShapeDtypeStruct((rows, cols), f32),
                    jax.ShapeDtypeStruct((rows, cols), f32),
                    jax.ShapeDtypeStruct((rows, cols), f32),
-                   jax.ShapeDtypeStruct((8, full), f32)],
+                   jax.ShapeDtypeStruct((8, full), f32),
+                   jax.ShapeDtypeStruct((CHAIN, rows, full), bf16)],
         scratch_shapes=[
             V((8, rows), f32), V((trio, 8, rows), f32),
             V((trio, part, full), bf16), V((trio, part, full), bf16),
@@ -982,18 +1060,80 @@
             V((count, part, cols), f32), V((rows, cols), f32),
             V((8, rows), f32), V((trio, 8, rows), f32),
             V((count, 8, full), f32),
-            V((rows, ffn), f32), V((rows, cols), bf16),
+            V((rows, full), bf16), V((rows, ffn), f32), V((rows, cols), bf16),
             V((rows, ffn), bf16), V((rows, ffn), bf16), V((rows, ffn), bf16),
-            V((part, full), f32)] + [sem] * 20,
+            V((part, full), f32)] + [sem] * 20 + [
+            pltpu.SemaphoreType.DMA((heads,)), pltpu.SemaphoreType.DMA((CHAIN,))],
         compiler_params=pltpu.CompilerParams(
             collective_id=2, has_side_effects=True, vmem_limit_bytes=56 * 1024 * 1024),
         name="middle",
     )(*ins)
 
 
-def tail_kernel(count, at_mix, grads_ref, packed_w_ref, mix_gate_ref, ggp_ref, x_ref, pre_gain_ref, late_ref, early_ref,
+def front_kernel(count, in_ref, gain_ref, bias_ref, wq_ref, wk_ref, wv_ref, wr_ref, x_ref, normed_ref, pay_ref, gathered, send, recv):
+    me, _ = head_place()
+    cols, rows = in_ref.shape
+    heads = wr_ref.shape[0]
+    width = cols // heads
+    part = rows // count
+    meet_heads(me, count)
+    here = pl.ds(pl.multiple_of(me * cols, cols), cols)
+    for d in range(1, count):
+        push_head(in_ref, gathered.at[here, :], send.at[d - 1], recv.at[d - 1], lax.rem(me + d, count)).start()
+    gathered[here, :] = in_ref[...]
+    for d in range(1, count):
+        push_head(in_ref, gathered.at[here, :], send.at[d - 1], recv.at[d - 1], lax.rem(me + d, count)).wait_send()
+        origin = lax.rem(me + count - d, count)
+        await_bytes(gathered.at[pl.ds(pl.multiple_of(origin * cols, cols), cols), :], recv.at[d - 1])
+    gain = gain_ref[...][None, :]
+    rate_bias = bias_ref[...][None, :]
+    x_ref[...] = gathered[...].T
+
+    def project(b, _):
+        r = pl.ds(pl.multiple_of(b * part, part), part)
+        x = x_ref[r, :].astype(f32)
+        nt = (x * lax.rsqrt(mean_row(x * x) + eps_norm) * gain).astype(bf16)
+        normed_ref[r, :] = nt
+        query = dot_nt(nt, wq_ref[...]).astype(bf16)
+        key = dot_nt(nt, wk_ref[...]).astype(bf16)
+        value = dot_nt(nt, wv_ref[...]).astype(bf16)
+        logit = dot_nt(nt, wr_ref[...]) + rate_bias
+        high = logit.astype(bf16)
+        low = (logit - high.astype(f32)).astype(bf16)
+        lane = lax.broadcasted_iota(jnp.int32, (part, width), 1)
+        for j in range(heads):
+            own = slice(j * width, (j + 1) * width)
+            extra = jnp.where(lane == 0, high[:, j : j + 1].astype(f32),
+                              jnp.where(lane == 1, low[:, j : j + 1].astype(f32), 0.0)).astype(bf16)
+            pay_ref[r, j * PACK : (j + 1) * PACK] = jnp.concatenate(
+                [query[:, own], key[:, own], value[:, own], extra], axis=1)
+        return 0
+
+    lax.fori_loop(0, count, project, 0)
+
+
+def front(inputs_t, pre_gain, rate_bias, wq, wk, wv, wr):
+    count = lax.axis_size("head")
+    cols, rows = inputs_t.shape
+    heads = wr.shape[0]
+    vmem = pl.BlockSpec(memory_space=pltpu.VMEM)
+    sem = pltpu.SemaphoreType.DMA((count - 1,))
+    wide = jax.ShapeDtypeStruct((rows, cols * count), bf16)
+    return pl.pallas_call(
+        functools.partial(front_kernel, count),
+        in_specs=[vmem] * 7,
+        out_specs=[vmem] * 3,
+        out_shape=[wide, wide, jax.ShapeDtypeStruct((rows, heads * PACK), bf16)],
+        scratch_shapes=[pltpu.VMEM((cols * count, rows), bf16), sem, sem],
+        compiler_params=pltpu.CompilerParams(collective_id=4, has_side_effects=True),
+        name="front",
+    )(inputs_t, pre_gain, rate_bias, wq, wk, wv, wr)
+
+
+def tail_kernel(count, at_mix, grads_ref, wq_ref, wk_ref, wv_ref, wr_ref, mix_gate_ref, ggp_ref, x_ref, gain_ref,
+                late_ref, early_ref,
                 back_ref, tiles_ref,
-                mine, got, tile, tile_got, ib_s, ib_r, th_s, th_r, ts_s, ts_r, ts_loc):
+                mine, got, tile, tile_got, wcols, ib_s, ib_r, th_s, th_r, ts_s, ts_r, ts_loc):
     me, _ = head_place()
     pos, base = seq_place()
     heads = grads_ref.shape[0]
@@ -1011,35 +1151,50 @@
             barrier, inc=1, device_id={"seq": base + lax.rem(pos + d, CHAIN)}, device_id_type=MESH)
     pl.semaphore_wait(barrier, count - 1 + CHAIN - 1)
     part = rows // count
+    width = PACK // 4
+    pre_gain = gain_ref[...][None, :]
+    sides = (wq_ref, wk_ref, wv_ref)
 
     def back_rows(b, _):
         r = pl.ds(pl.multiple_of(b * part, part), part)
-        grad = dot_nt(ggp_ref[r, :], mix_gate_ref[...])
+        grad = dot_nn(ggp_ref[r, :], mix_gate_ref[...])
+        blocks = [grads_ref[j, r, :] for j in range(heads)]
+        for i, side in enumerate(sides):
+            joined = jnp.concatenate([b[:, i * width : (i + 1) * width] for b in blocks], axis=1)
+            grad = grad + dot_nn(joined, side[...])
         for j in range(heads):
-            grad = grad + dot_nt(grads_ref[j, r, :], packed_w_ref[:, j * PACK : (j + 1) * PACK])
+            rate = blocks[j][:, rate_lane : rate_lane + 1].astype(f32) + blocks[j][
+                :, rate_lane + 1 : rate_lane + 2].astype(f32)
+            grad = grad + rate.astype(bf16).astype(f32) * wr_ref[j : j + 1, :].astype(f32)
         x = x_ref[r, :].astype(f32)
         rms = lax.rsqrt(mean_row(x * x) + eps_norm)
-        scaled = grad * pre_gain_ref[...]
+        scaled = grad * pre_gain
         back = (rms * (scaled - x * rms * rms * mean_row(scaled * x))).astype(bf16)
         for c in range(count):
             mine[c, r, :] = back[:, c * cols : (c + 1) * cols]
         return 0
 
     lax.fori_loop(0, count, back_rows, 0)
+    for d, peer in peers:
+        push_head(mine.at[peer], got.at[d - 1], ib_s.at[d - 1], ib_r.at[d - 1], peer).start()
     lane = lax.broadcasted_iota(jnp.int32, (share, 128), 1)
     line = lax.broadcasted_iota(jnp.int32, (8, 128), 0)
     w_rows = pl.ds(pl.multiple_of(pos * share, share), share)
-    gain = jnp.sum(early_ref[:, at_mix : at_mix + cols] * mix_gate_ref[w_rows, :].astype(f32), axis=1, keepdims=True)
+    slim = jnp.concatenate([wr_ref[j : j + 1, :].astype(f32) for j in range(heads)] + [pre_gain] * (8 - heads), axis=0)
+    wcols[4, :, 0:8] = slim.T
+    for i, side in enumerate(sides + (mix_gate_ref,)):
+        wcols[i] = side[...].astype(f32).T
+    gain = jnp.sum(early_ref[:, at_mix : at_mix + cols] * wcols[3, w_rows, :], axis=1, keepdims=True)
     table = jnp.zeros((share, 128), f32)
+    blocks = [late_ref[j].astype(f32) for j in range(heads)]
+    for i in range(3):
+        joined = jnp.concatenate([b[:, i * width : (i + 1) * width] for b in blocks], axis=1)
+        gain = gain + jnp.sum(joined * wcols[i, w_rows, :], axis=1, keepdims=True)
     for j in range(heads):
-        late = late_ref[j].astype(f32)
-        gain = gain + jnp.sum(
-            late * packed_w_ref[w_rows, j * PACK : (j + 1) * PACK].astype(f32), axis=1, keepdims=True)
-        rate = late[:, rate_lane : rate_lane + 1] + late[:, rate_lane + 1 : rate_lane + 2]
+        rate = blocks[j][:, rate_lane : rate_lane + 1] + blocks[j][:, rate_lane + 1 : rate_lane + 2]
+        gain = gain + rate * wcols[4, w_rows, j : j + 1]
         table = jnp.where(lane == j, rate, table)
-        if j == 0:
-            for d, peer in peers:
-                push_head(mine.at[peer], got.at[d - 1], ib_s.at[d - 1], ib_r.at[d - 1], peer).start()
+    gain = gain / wcols[4, w_rows, heads : heads + 1]
     table = jnp.where(lane == heads, gain, table)
     flat = jnp.concatenate([table, jnp.zeros((128 - share, 128), f32)], axis=0).T[0:8]
     tile[...] = flat
@@ -1065,7 +1220,7 @@
     await_bytes(tiles_ref.at[pos], ts_loc)
 
 
-def tail(at_mix, grads, packed_w, mix_gate, ggp, x, pre_gain, late, early):
+def tail(at_mix, grads, wq, wk, wv, wr, mix_gate, ggp, x, pre_gain, late, early):
     count = lax.axis_size("head")
     rows, full = x.shape
     width = ggp.shape[1]
@@ -1075,31 +1230,32 @@
     trio, seven = dma((count - 1,)), dma((CHAIN - 1,))
     return pl.pallas_call(
         functools.partial(tail_kernel, count, at_mix),
-        in_specs=[vmem] * 8,
+        in_specs=[vmem] * 11,
         out_specs=[vmem] * 2,
         out_shape=[jax.ShapeDtypeStruct((rows, width), f32),
                    jax.ShapeDtypeStruct((CHAIN, 8, 128), f32)],
         scratch_shapes=[V((count, rows, width), bf16), V((count - 1, rows, width), bf16),
-                        V((8, 128), f32), V((count - 1, 8, 128), f32),
+                        V((8, 128), f32), V((count - 1, 8, 128), f32), V((5, full, width), f32),
                         trio, trio, trio, trio, seven, seven, dma],
         compiler_params=pltpu.CompilerParams(
             collective_id=3, has_side_effects=True, vmem_limit_bytes=56 * 1024 * 1024),
         name="tail",
-    )(grads, packed_w, mix_gate, ggp, x, pre_gain, late, early)
+    )(grads, wq, wk, wv, wr, mix_gate, ggp, x, pre_gain, late, early)
 
 
 def final_kernel(at_mix, ffn, down_ref, resid_ref, back_ref, grc_ref, late_ref, early_ref, ends_ref, tiles_ref, small_ref,
                  out_ref, gin_ref, gq_ref, gk_ref, gv_ref, gmix_ref, rate_ref, gwout_ref, gwg_ref, gwu_ref, gwd_ref,
-                 w1_ref, b1_ref, w2_ref, b2_ref, ig_ref, ib_ref, rb_ref, vec_ref):
+                 w1_ref, b1_ref, w2_ref, b2_ref, ig_ref, ib_ref, rb_ref, pre_ref, pg_ref, pb_ref, fg_ref):
     heads, width, hidden = w1_ref.shape
     cols = heads * width
-    out_ref[...] = down_ref[...] + resid_ref[...]
-    gin_ref[...] = back_ref[...] + grc_ref[...]
+    out_ref[...] = (down_ref[...] + resid_ref[...]).T
+    gin_ref[...] = (back_ref[...] + grc_ref[...]).T
     for i, ref in enumerate((gq_ref, gk_ref, gv_ref)):
         ref[...] = jnp.concatenate([late_ref[j, :, i * width : (i + 1) * width].astype(f32) for j in range(heads)], axis=1)
     gwg_ref[...] = early_ref[:, 0:ffn]
     gwu_ref[...] = early_ref[:, ffn : 2 * ffn]
-    gwd_ref[...] = early_ref[:, 2 * ffn : 3 * ffn].T
+    rates = []
+    gwd_ref[...] = early_ref[:, 2 * ffn : 3 * ffn]
     both = early_ref[:, at_mix : at_mix + 2 * cols]
     gmix_ref[...] = both[:, 0:cols]
     gwout_ref[...] = both[:, cols:].T
@@ -1107,20 +1263,25 @@
         w1_ref[j] = ends_ref[j, 0:width, :].astype(f32)
         b1_ref[pl.ds(j, 1), :] = ends_ref[j, width : AUG, :].astype(f32)[0:1]
         second = ends_ref[j, AUG : AUG + width, :].astype(f32)
-        w2_ref[j] = (second - jnp.mean(second, axis=0, keepdims=True)).T
+        w2_ref[j] = second - jnp.mean(second, axis=0, keepdims=True)
         rest = ends_ref[j, AUG + width :, :].astype(f32)[0:8, 0:width]
         b2_ref[pl.ds(j, 1), :] = rest[0:1] - mean_row(rest[0:1])
         ig_ref[pl.ds(j, 1), :] = rest[1:2]
         ib_ref[pl.ds(j, 1), :] = rest[2:3]
-        rb_ref[pl.ds(j, 1), :] = rest[3:4] + rest[4:5]
-    each = rate_ref.shape[0] // CHAIN
-    for p in range(CHAIN):
-        turned = jnp.concatenate([tiles_ref[p]] * 16, axis=0).T
-        rate_ref[pl.ds(p * each, each), :] = turned[0:each, 0:heads]
+        rates.append((rest[3:4] + rest[4:5])[:, 0:1])
+    each = rate_ref.shape[1] // CHAIN
+    strips = jnp.concatenate([tiles_ref[p, :, 0:each] for p in range(CHAIN)], axis=1)
+    rate_ref[...] = strips[0:heads]
+    me, count = head_place()
+    pick = [tiles_ref[me * (CHAIN // count) + i, heads : heads + 1, 0:each] for i in range(CHAIN // count)]
+    pre_ref[...] = jnp.concatenate(pick, axis=1)[0]
+    rb_ref[...] = jnp.concatenate(rates, axis=1)[0]
     acc = small_ref[0]
     for p in range(1, CHAIN):
         acc = acc + small_ref[p]
-    vec_ref[...] = acc
+    fg_ref[...] = acc[0]
+    pg_ref[...] = acc[1:2, 0:cols][0]
+    pb_ref[...] = acc[2:3, 0:cols][0]
 
 
 def finish(at_mix, ffn, down, resid, back, grc, late, early, ends, tiles, small, shapes):
@@ -1139,10 +1300,6 @@
 def stretch_groups(axis):
     count = lax.axis_size(axis)
     return [[start + step for step in range(0, count, CHAIN)] for start in range(CHAIN)]
-
-
-def bf_product(form, left, right):
-    return jnp.einsum(form, left, right, preferred_element_type=f32)
 
 
 def local(
@@ -1172,42 +1329,24 @@
     full_width = pre_gain.shape[0]
     rows, local_cols = inputs.shape
     heads, head_dim = inner_gain.shape
-    head_index = lax.axis_index("head")
-    whole_low = lax.all_gather(inputs, "head", axis=1, tiled=True)
-    whole_in = whole_low.astype(f32)
-    grad_whole = lax.all_gather(cotangent, "head", axis=1, tiled=True)
-    rms_one = lax.rsqrt(jnp.mean(whole_in * whole_in, axis=1, keepdims=True) + eps_norm)
-    normed_one = (whole_in * rms_one * pre_gain).astype(bf16)
     stretches = lax.axis_size("seq") // CHAIN
-    spare = PACK - 3 * head_dim
-
-    def by_head(weight):
-        return weight.reshape(full_width, heads, -1)
-
-    rate_cols = by_head(w_rate)
-    packed_w = jnp.concatenate(
-        [by_head(w_query), by_head(w_key), by_head(w_value), rate_cols, rate_cols,
-         jnp.zeros((full_width, heads, spare - 2), bf16)], axis=2).reshape(full_width, heads * PACK)
-    lane = lax.broadcasted_iota(jnp.int32, (1, heads, PACK), 2)
-    rate_lane = (lane == 3 * head_dim) | (lane == 3 * head_dim + 1)
-    packed_bias = jnp.where(rate_lane, rate_bias[None, :, None], 0.0).reshape(1, heads * PACK)
-    low_lane = (lane == 3 * head_dim + 1).reshape(1, heads * PACK)
-    pre = bf_product("rd,dc->rc", normed_one, packed_w) + packed_bias
-    payload = (pre - jnp.where(low_lane, lax.reduce_precision(pre, 8, 7), 0.0)).astype(bf16)
-    gate_pre = bf_product("rd,dc->rc", normed_one, mix_gate)
     share = full_width // CHAIN
-    mixed_h, normed_all, *saved = chain_forward(
-        payload, normed_one, init_w_one, init_b_one, init_w_two, init_b_two, inner_gain, inner_bias)
+
+    sides = (w_query.T, w_key.T, w_value.T, w_rate.T)
+    whole_low, normed_one, payload = front(inputs.T, pre_gain, rate_bias, *sides)
+    mixed_h, ct_blocks, *saved = chain_forward(
+        payload, cotangent.T, init_w_one, init_b_one, init_w_two.transpose(0, 2, 1), init_b_two,
+        inner_gain, inner_bias)
     ffn = w_gate.shape[1]
     at_mix = 3 * ffn
-    grad_mixed, early, grad_gate_pre, down_cols, resid_cols, grad_resid_cols, small = middle(
-        mixed_h, whole_low, grad_whole, gate_pre, normed_one, w_out, w_gate, w_up, w_down,
-        post_gain[None], post_bias[None], ffn_gain[None])
+    grad_mixed, early, grad_gate_pre, down_cols, resid_cols, grad_resid_cols, small, normed_all = middle(
+        mixed_h, whole_low, ct_blocks.reshape(full_width, rows), mix_gate.T, normed_one, w_out, w_gate, w_up, w_down,
+        post_gain, post_bias, ffn_gain)
     grads, ends, late, early_sum, small = chain_backward(
         grad_mixed, early.reshape(CHAIN // 2, 2, share, early.shape[1]), small, inner_gain, inner_bias,
         normed_all.reshape(CHAIN * rows, full_width), saved)
     back_cols, tiles = tail(
-        at_mix, grads, packed_w, mix_gate, grad_gate_pre, whole_low, pre_gain[None],
+        at_mix, grads, *sides, mix_gate.T, grad_gate_pre, whole_low, pre_gain,
         late, early_sum)
     if stretches > 1:
         groups = stretch_groups("seq")
@@ -1228,37 +1367,36 @@
     hidden = init_w_one.shape[2]
     square = (held, local_cols)
     (outputs, grad_inputs, grad_q, grad_k, grad_v, grad_mix, grad_rate_w, grad_w_out, grad_w_gate, grad_w_up, grad_w_down,
-     grad_one, grad_b_one, grad_two, grad_b_two, grad_gain, grad_bias, rate_b, vectors) = finish(
+     grad_one, grad_b_one, grad_two, grad_b_two, grad_gain, grad_bias, rate_b, grad_pre, grad_post_gain, grad_post_bias,
+     grad_ffn_gain) = finish(
         at_mix, ffn, down_cols, resid_cols, back_cols, grad_resid_cols, late, early_sum, ends, tiles, small,
-        ((rows, local_cols), (rows, local_cols), square, square, square, square, (full_width, heads),
-         (local_cols, held), (held, ffn), (held, ffn), (ffn, held),
-         (heads, head_dim, hidden), (heads, hidden), (heads, hidden, head_dim), (heads, head_dim),
-         (heads, head_dim), (heads, head_dim), (heads, head_dim), (8, full_width)))
-    gain_all = tiles[:, heads, :share].reshape(full_width) / pre_gain
-    gain_one = lax.dynamic_slice_in_dim(gain_all, head_index * local_cols, local_cols, 0)
+        ((local_cols, rows), (local_cols, rows), square, square, square, square, (heads, full_width),
+         (local_cols, held), (held, ffn), (held, ffn), (held, ffn),
+         (heads, head_dim, hidden), (heads, hidden), (heads, head_dim, hidden), (heads, head_dim),
+         (heads, head_dim), (heads, head_dim), (heads,), (local_cols,), (local_cols,), (local_cols,), (full_width,)))
     return (
-        outputs,
-        grad_inputs,
-        gain_one,
+        outputs.T,
+        grad_inputs.T,
+        grad_pre,
         grad_q,
         grad_k,
         grad_v,
         grad_mix,
-        grad_rate_w,
-        rate_b[:, 0],
+        grad_rate_w.T,
+        rate_b,
         grad_gain,
         grad_bias,
         grad_one,
         grad_b_one,
-        grad_two,
+        grad_two.transpose(0, 2, 1),
         grad_b_two,
-        vectors[1, :local_cols],
-        vectors[2, :local_cols],
+        grad_post_gain,
+        grad_post_bias,
         grad_w_out,
-        vectors[0],
+        grad_ffn_gain,
         grad_w_gate,
         grad_w_up,
-        grad_w_down,
+        grad_w_down.T,
     )
 
 

time: 332 us -> 304 us (0.916)
  blocking collectives: 14.4 us -> 0 us
  local copies, waits for them, and re-layouts: 15.9 us -> 1.73 us
  Pallas kernels: 296 us -> 301 us
    pallas_call x1, Pallas kernels: 44.6 us -> 105 us  [middle(): pl.pallas_call(functools.partial(mid_kernel, count), in_specs=[vmem] * le...]
    pallas_call x1, Pallas kernels: 166 us -> 131 us  [chain_backward(): pl.pallas_call(functools.partial(bwd_kernel, block, heads, turn), grid=(n...]
    pallas_call x1 -> x2, Pallas kernels: 62.3 us -> 44.5 us  [the longest x1 32 us: chain_forward(): pl.pallas_call(functools.partial(fwd_kernel, block, heads, count), grid=(...]
    all_gather x2 -> x0, blocking collectives: 14.4 us -> none  [the longest x1 8.25 us: local(): whole_low = lax.all_gather(inputs, 'head', axis=1, tiled=True)]
    unnamed x49 -> x18, local copies, waits for them, and re-layouts: 7.63 us -> 1.73 us
where the time goes in v5:
time: 304 us; the launch traced here: 303 us
  Pallas kernels  301 us (99%)
    pallas_call x1, Pallas kernels, chain_backward(): pl.pallas_call(functools.partial(bwd_kernel, block, heads, turn), grid=(n...  131 us
    pallas_call x1, Pallas kernels, middle(): pl.pallas_call(functools.partial(mid_kernel, count), in_specs=[vmem] * le...  105 us
    pallas_call x1, Pallas kernels, chain_forward(): pl.pallas_call(functools.partial(fwd_kernel, block, heads, count), grid=(...  32 us
    pallas_call x1, Pallas kernels, tail(): pl.pallas_call(functools.partial(tail_kernel, count, at_mix), in_specs=[v...  18.8 us
    pallas_call x1, Pallas kernels, front(): pl.pallas_call(functools.partial(front_kernel, count), in_specs=[vmem] *...  12.5 us

profile of v5, /device:TPU:0, one launch (start us, length us, event | category | flops | bytes accessed | tf_op | source)
XLA Modules:
  0.0 303.3 jit_solution(7432816782888415386)
XLA Ops:
  0.7 12.5 %front.1 = (bf16[256,768]{1,0:T(8,128)(2,1)}, bf16[256,768]{1,0:T(8,128)(2,1)}, bf16[256,768]{1,0:T(8,128)(2,1)}) custom-call(bf16[192,256]{1,0:T(8,128)(2,1)} %bitcast.29, f32[768]{0:T(1024)} %gain_ref.3, f32[3]{0:T(128)} %bias_ref.1, bf16[192,768]{1,0:T(8,128)(2,1)} %bitcast.21, bf16[192,768]{1,0:T(8,128)(2,1)} %bitcast.23, bf16[192,768]{1,0:T(8,128)(2,1)} %bitcast.25, ...), custom_call_target="tpu_custom_call" | custom-call | tf_op jit(solution)/shard_map/front/pallas_call | solution.py:1122
  13.2 32.0 %inner_forward.1 = (bf16[3,256,64]{2,1,0:T(8,128)(2,1)}, bf16[4,192,256]{2,1,0:T(8,128)(2,1)}, bf16[2048,80]{1,0:T(8,128)(2,1)}, bf16[2048,80]{1,0:T(8,128)(2,1)...) custom-call(bf16[256,768]{1,0:T(8,128)(2,1)} %get-tuple-element.75.p, ...), custom_call_target="tpu_custom_call" | custom-call | tf_op jit(solution)/shard_map/inner_forward/pallas_call | solution.py:510
  45.2 104.9 %middle.1 = (bf16[3,256,64]{2,1,0:T(8,128)(2,1)}, bf16[768,1920]{1,0:T(8,128)(2,1)}, bf16[256,192]{1,0:T(8,128)(2,1)}, f32[256,192]{1,0:T(8,128)}, f32[256,192]{...) custom-call(bf16[3,256,64]{2,1,0:T(8,128)(2,1)} %get-tuple-element.76.mixed_ref, ...), custom_call_target="tpu_custom_call" | custom-call | tf_op jit(solution)/shard_map/middle/pallas_call | solution.py:1040
  150.1 130.8 %inner_backward.1 = (bf16[3,256,256]{2,1,0:T(8,128)(2,1)}, bf16[3,160,256]{2,1,0:T(8,128)(2,1)}, bf16[3,96,256]{2,1,0:T(8,128)(2,1)}, f32[96,1920]{1,0:T(8,128)}, f32[8,8,768]{2,1,0:T(8,128)}) custom-call(bf16[3,256,64]{2,1,0:T(8,128)(2,1)} %get-tuple-element.82.gm_ref, bf16[4,2,96,1920]{3,2,1,0:T(8,128)(2,1)} %bitcast.18, ...), custom_call_target="tpu_custom_call" | custom-call | tf_op jit(solution)/shard_map/inner_backward/pallas_call | solution.py:757
  280.9 0.0 copy-start
  280.9 0.0 copy-start.1
  280.9 0.0 copy-start.2
  280.9 0.0 copy-start.3
  280.9 0.0 copy-start.4
  281.0 0.0 copy-start.6
  281.0 0.0 copy-start.7
  281.0 18.8 %tail.1 = (f32[256,192]{1,0:T(8,128)}, f32[8,8,128]{2,1,0:T(8,128)}) custom-call(bf16[3,256,256]{2,1,0:T(8,128)(2,1)} %get-tuple-element.97.grads_ref, bf16[192,768]{1,0:T(8,128)(2,1)} %bitcast.22, bf16[192,768]{1,0:T(8,128)(2,1)} %bitcast.24, bf16[192,768]{1,0:T(8,128)(2,1)} %bitcast.26, bf16[3,768]{1,0:T(4,128)(2,1)} %bitcast.32, ...), custom_call_target="tpu_custom_call" | custom-call | tf_op jit(solution)/shard_map/tail/pallas_call | solution.py:1231
  299.8 0.0 copy-done
  299.8 0.0 copy-done.1
  299.8 0.0 copy-done.2
  299.8 0.0 copy-done.3
  299.9 0.0 copy-done.4
  299.9 0.0 copy-done.6
  299.9 0.0 copy-done.7
  299.9 0.0 copy-start.5
  299.9 0.9 copy-done.5
  300.8 0.0 copy-start.8
  300.8 0.8 copy-done.8
  301.6 1.5 final.1
Async XLA Ops:
  280.9 18.9 %copy-start = (f32[96,1920]{1,0:T(8,128)S(1)}, f32[96,1920]{1,0:T(8,128)}, u32[]{:S(2)}) copy-start(f32[96,1920]{1,0:T(8,128)} %get-tuple-element.100.early_ref) | copy-start | bytes 2211844
  280.9 18.9 %copy-start.1 = (bf16[3,96,256]{2,1,0:T(8,128)(2,1)S(1)}, bf16[3,96,256]{2,1,0:T(8,128)(2,1)}, u32[]{:S(2)}) copy-start(bf16[3,96,256]{2,1,0:T(8,128)(2,1)} %get-tuple-element.99.late_ref) | copy-start | bytes 442372
  280.9 18.9 %copy-start.2 = (f32[256,192]{1,0:T(8,128)S(1)}, f32[256,192]{1,0:T(8,128)}, u32[]{:S(2)}) copy-start(f32[256,192]{1,0:T(8,128)} %get-tuple-element.80.down_ref) | copy-start | bytes 589828
  280.9 18.9 %copy-start.3 = (f32[256,192]{1,0:T(8,128)S(1)}, f32[256,192]{1,0:T(8,128)}, u32[]{:S(2)}) copy-start(f32[256,192]{1,0:T(8,128)} %get-tuple-element.81.resid_ref) | copy-start | bytes 589828
  280.9 18.9 %copy-start.4 = (f32[256,192]{1,0:T(8,128)S(1)}, f32[256,192]{1,0:T(8,128)}, u32[]{:S(2)}) copy-start(f32[256,192]{1,0:T(8,128)} %get-tuple-element.102.grc_ref) | copy-start | bytes 589828
  281.0 18.9 %copy-start.6 = (bf16[3,160,256]{2,1,0:T(8,128)(2,1)S(1)}, bf16[3,160,256]{2,1,0:T(8,128)(2,1)}, u32[]{:S(2)}) copy-start(bf16[3,160,256]{2,1,0:T(8,128)(2,1)} %get-tuple-element.103.ends_ref) | copy-start | bytes 737284
  281.0 18.9 %copy-start.7 = (f32[8,8,768]{2,1,0:T(8,128)S(1)}, f32[8,8,768]{2,1,0:T(8,128)}, u32[]{:S(2)}) copy-start(f32[8,8,768]{2,1,0:T(8,128)} %get-tuple-element.105.small_ref) | copy-start | bytes 589828
  299.9 1.0 copy-start.5
  300.8 0.8 copy-start.8

commit v6 on v5

--- a/solution.py
+++ b/solution.py
@@ -197,8 +197,8 @@
     d_query = (d_query + dot_nn(d_att1, key_aug))[:, :width] + d_out
     d_key = dot_tn(d_att1, query_aug)[:, :width]
     yield
-    d_gain = jnp.sum(d_out * nb, axis=0, keepdims=True)
-    d_bias = jnp.sum(d_out, axis=0, keepdims=True)
+    d_gain = d_out * nb
+    d_bias = d_out
     store.update(dq=d_query, dk=d_key, d_gain=d_gain, d_bias=d_bias, rate=rate, w1=w1_h, w2=w2_h, s2f=s2,
                  key=key_aug, query=query_aug, gslope=2.0 * n * gain + bias - target)
     yield
@@ -217,8 +217,8 @@
     late_part = dot_nt(pre["s1"], p1_h)
     d_logit = keep * jnp.sum(d_s2 * pre["s2f"], axis=1, keepdims=True)
     yield
-    d_gain = pre["d_gain"] + jnp.sum(d_g * pre["gslope"], axis=0, keepdims=True)
-    d_bias = pre["d_bias"] + jnp.sum(d_gg, axis=0, keepdims=True)
+    d_gain = pre["d_gain"] + d_g * pre["gslope"]
+    d_bias = pre["d_bias"] + d_gg
     d_key = pre["dk"] + d_gg + (key_part - late_part)[:, :width]
     sink(pre["dq"], d_key, -d_gg, d_logit, d_gain, d_bias)
     yield
@@ -659,7 +659,7 @@
             def sink(d_query, d_key, d_value, d_logit, d_gain, d_bias, loc=loc):
                 totals[0] = totals[0] + d_gain
                 totals[1] = totals[1] + d_bias
-                totals[2] = totals[2] + jnp.sum(d_logit, axis=0, keepdims=True)
+                totals[2] = totals[2] + d_logit
                 high = d_logit.astype(bf16).astype(f32)
                 lane = lax.broadcasted_iota(jnp.int32, (MINI, width), 1)
                 extra = jnp.where(lane == 0, high, jnp.where(lane == 1, d_logit - high, 0.0))
@@ -682,9 +682,10 @@
             ends[pl.ds(AUG, width), :] = end_two.astype(bf16)
             rest = ENDS - AUG - width
             row = lax.broadcasted_iota(jnp.int32, (rest, width), 0)
-            tailing = jnp.where(row == 0, end_b_two, jnp.where(row == 1, dg[...], jnp.where(row == 2, db[...], 0.0)))
-            high = dl[...].astype(bf16).astype(f32)
-            tailing = tailing + jnp.where(row == 3, high, jnp.where(row == 4, dl[...] - high, 0.0))
+            sums = [jnp.sum(r[...], axis=0, keepdims=True) for r in (dg, db, dl)]
+            tailing = jnp.where(row == 0, end_b_two, jnp.where(row == 1, sums[0], jnp.where(row == 2, sums[1], 0.0)))
+            high = sums[2].astype(bf16).astype(f32)
+            tailing = tailing + jnp.where(row == 3, high, jnp.where(row == 4, sums[2] - high, 0.0))
             ends[pl.ds(AUG + width, rest), :] = jnp.concatenate([tailing] * 4, axis=1).astype(bf16)
             share_block(0)
             for slab in slabs:
@@ -774,8 +775,8 @@
                         pltpu.VMEM((AUG, hidden), f32), pltpu.VMEM((width, hidden), f32), pltpu.VMEM((1, width), f32),
                         pltpu.VMEM((2 * MINI, hidden), bf16), pltpu.VMEM((2 * MINI, AUG), bf16),
                         pltpu.VMEM((3 * MINI, width), bf16), pltpu.VMEM((3 * MINI, hidden), bf16),
-                        pltpu.VMEM((1, width), f32), pltpu.VMEM((1, width), f32), pltpu.VMEM((1, width), f32),
-                        pltpu.VMEM((1, 1), f32),
+                        pltpu.VMEM((1, width), f32), pltpu.VMEM((MINI, width), f32), pltpu.VMEM((MINI, width), f32),
+                        pltpu.VMEM((MINI, 1), f32),
                         dma((heads,)), dma((CHAIN,)), dma, dma, dma, three, three, seven, seven, dma,
                         dma, dma((heads,)), seven, dma((heads,)), seven, dma((heads,))],
         compiler_params=pltpu.CompilerParams(collective_id=1, has_side_effects=True),
@@ -1149,7 +1150,6 @@
     for d in range(1, CHAIN):
         pl.semaphore_signal(
             barrier, inc=1, device_id={"seq": base + lax.rem(pos + d, CHAIN)}, device_id_type=MESH)
-    pl.semaphore_wait(barrier, count - 1 + CHAIN - 1)
     part = rows // count
     width = PACK // 4
     pre_gain = gain_ref[...][None, :]
@@ -1174,9 +1174,6 @@
             mine[c, r, :] = back[:, c * cols : (c + 1) * cols]
         return 0
 
-    lax.fori_loop(0, count, back_rows, 0)
-    for d, peer in peers:
-        push_head(mine.at[peer], got.at[d - 1], ib_s.at[d - 1], ib_r.at[d - 1], peer).start()
     lane = lax.broadcasted_iota(jnp.int32, (share, 128), 1)
     line = lax.broadcasted_iota(jnp.int32, (8, 128), 0)
     w_rows = pl.ds(pl.multiple_of(pos * share, share), share)
@@ -1198,8 +1195,12 @@
     table = jnp.where(lane == heads, gain, table)
     flat = jnp.concatenate([table, jnp.zeros((128 - share, 128), f32)], axis=0).T[0:8]
     tile[...] = flat
+    pl.semaphore_wait(barrier, count - 1 + CHAIN - 1)
     for d, peer in peers:
         push_head(tile, tile_got.at[d - 1], th_s.at[d - 1], th_r.at[d - 1], peer).start()
+    lax.fori_loop(0, count, back_rows, 0)
+    for d, peer in peers:
+        push_head(mine.at[peer], got.at[d - 1], ib_s.at[d - 1], ib_r.at[d - 1], peer).start()
     back = mine[me].astype(f32)
     for d, peer in peers:
         push_head(tile, tile_got.at[d - 1], th_s.at[d - 1], th_r.at[d - 1], peer).wait()

time: 304 us -> 298 us (0.980)
  Pallas kernels: 301 us -> 295 us
    pallas_call x1, Pallas kernels: 18.8 us -> 13.5 us  [tail(): pl.pallas_call(functools.partial(tail_kernel, count, at_mix), in_specs=[v...]
where the time goes in v6:
time: 298 us
  Pallas kernels  295 us (99%)
    pallas_call x1, Pallas kernels, chain_backward(): pl.pallas_call(functools.partial(bwd_kernel, block, heads, turn), grid=(n...  131 us
    pallas_call x1, Pallas kernels, middle(): pl.pallas_call(functools.partial(mid_kernel, count), in_specs=[vmem] * le...  105 us
    pallas_call x1, Pallas kernels, chain_forward(): pl.pallas_call(functools.partial(fwd_kernel, block, heads, count), grid=(...  32 us
    pallas_call x1, Pallas kernels, tail(): pl.pallas_call(functools.partial(tail_kernel, count, at_mix), in_specs=[v...  13.5 us
    pallas_call x1, Pallas kernels, front(): pl.pallas_call(functools.partial(front_kernel, count), in_specs=[vmem] *...  12.5 us

profile of v6, /device:TPU:0, one launch (start us, length us, event | category | flops | bytes accessed | tf_op | source)
XLA Modules:
  0.0 298.1 jit_solution(9837241676153685509)
XLA Ops:
  0.7 12.5 %front.1 = (bf16[256,768]{1,0:T(8,128)(2,1)}, bf16[256,768]{1,0:T(8,128)(2,1)}, bf16[256,768]{1,0:T(8,128)(2,1)}) custom-call(bf16[192,256]{1,0:T(8,128)(2,1)} %bitcast.29, f32[768]{0:T(1024)} %gain_ref.3, f32[3]{0:T(128)} %bias_ref.1, bf16[192,768]{1,0:T(8,128)(2,1)} %bitcast.21, bf16[192,768]{1,0:T(8,128)(2,1)} %bitcast.23, bf16[192,768]{1,0:T(8,128)(2,1)} %bitcast.25, ...), custom_call_target="tpu_custom_call" | custom-call | tf_op jit(solution)/shard_map/front/pallas_call | solution.py:1123
  13.2 32.0 %inner_forward.1 = (bf16[3,256,64]{2,1,0:T(8,128)(2,1)}, bf16[4,192,256]{2,1,0:T(8,128)(2,1)}, bf16[2048,80]{1,0:T(8,128)(2,1)}, bf16[2048,80]{1,0:T(8,128)(2,1)...) custom-call(bf16[256,768]{1,0:T(8,128)(2,1)} %get-tuple-element.75.p, ...), custom_call_target="tpu_custom_call" | custom-call | tf_op jit(solution)/shard_map/inner_forward/pallas_call | solution.py:510
  45.2 104.9 %middle.1 = (bf16[3,256,64]{2,1,0:T(8,128)(2,1)}, bf16[768,1920]{1,0:T(8,128)(2,1)}, bf16[256,192]{1,0:T(8,128)(2,1)}, f32[256,192]{1,0:T(8,128)}, f32[256,192]{...) custom-call(bf16[3,256,64]{2,1,0:T(8,128)(2,1)} %get-tuple-element.76.mixed_ref, ...), custom_call_target="tpu_custom_call" | custom-call | tf_op jit(solution)/shard_map/middle/pallas_call | solution.py:1041
  150.1 131.0 %inner_backward.1 = (bf16[3,256,256]{2,1,0:T(8,128)(2,1)}, bf16[3,160,256]{2,1,0:T(8,128)(2,1)}, bf16[3,96,256]{2,1,0:T(8,128)(2,1)}, f32[96,1920]{1,0:T(8,128)}, f32[8,8,768]{2,1,0:T(8,128)}) custom-call(bf16[3,256,64]{2,1,0:T(8,128)(2,1)} %get-tuple-element.82.gm_ref, bf16[4,2,96,1920]{3,2,1,0:T(8,128)(2,1)} %bitcast.18, ...), custom_call_target="tpu_custom_call" | custom-call | tf_op jit(solution)/shard_map/inner_backward/pallas_call | solution.py:758
  281.1 0.0 copy-start
  281.1 0.0 copy-start.1
  281.1 0.0 copy-start.2
  281.1 0.0 copy-start.3
  281.1 0.0 copy-start.4
  281.1 0.0 copy-start.6
  281.1 0.0 copy-start.7
  281.2 13.5 %tail.1 = (f32[256,192]{1,0:T(8,128)}, f32[8,8,128]{2,1,0:T(8,128)}) custom-call(bf16[3,256,256]{2,1,0:T(8,128)(2,1)} %get-tuple-element.97.grads_ref, bf16[192,768]{1,0:T(8,128)(2,1)} %bitcast.22, bf16[192,768]{1,0:T(8,128)(2,1)} %bitcast.24, bf16[192,768]{1,0:T(8,128)(2,1)} %bitcast.26, bf16[3,768]{1,0:T(4,128)(2,1)} %bitcast.32, ...), custom_call_target="tpu_custom_call" | custom-call | tf_op jit(solution)/shard_map/tail/pallas_call | solution.py:1232
  294.6 0.0 copy-done
  294.6 0.0 copy-done.1
  294.6 0.0 copy-done.2
  294.7 0.0 copy-done.3
  294.7 0.0 copy-done.4
  294.7 0.0 copy-done.6
  294.7 0.0 copy-done.7
  294.7 0.0 copy-start.5
  294.7 0.9 copy-done.5
  295.7 0.0 copy-start.8
  295.7 0.8 copy-done.8
  296.4 1.5 final.1
Async XLA Ops:
  281.1 13.5 %copy-start = (f32[96,1920]{1,0:T(8,128)S(1)}, f32[96,1920]{1,0:T(8,128)}, u32[]{:S(2)}) copy-start(f32[96,1920]{1,0:T(8,128)} %get-tuple-element.100.early_ref) | copy-start | bytes 2211844
  281.1 13.5 %copy-start.1 = (bf16[3,96,256]{2,1,0:T(8,128)(2,1)S(1)}, bf16[3,96,256]{2,1,0:T(8,128)(2,1)}, u32[]{:S(2)}) copy-start(bf16[3,96,256]{2,1,0:T(8,128)(2,1)} %get-tuple-element.99.late_ref) | copy-start | bytes 442372
  281.1 13.5 %copy-start.2 = (f32[256,192]{1,0:T(8,128)S(1)}, f32[256,192]{1,0:T(8,128)}, u32[]{:S(2)}) copy-start(f32[256,192]{1,0:T(8,128)} %get-tuple-element.80.down_ref) | copy-start | bytes 589828
  281.1 13.5 %copy-start.3 = (f32[256,192]{1,0:T(8,128)S(1)}, f32[256,192]{1,0:T(8,128)}, u32[]{:S(2)}) copy-start(f32[256,192]{1,0:T(8,128)} %get-tuple-element.81.resid_ref) | copy-start | bytes 589828
  281.1 13.5 %copy-start.4 = (f32[256,192]{1,0:T(8,128)S(1)}, f32[256,192]{1,0:T(8,128)}, u32[]{:S(2)}) copy-start(f32[256,192]{1,0:T(8,128)} %get-tuple-element.102.grc_ref) | copy-start | bytes 589828
  281.1 13.5 %copy-start.6 = (bf16[3,160,256]{2,1,0:T(8,128)(2,1)S(1)}, bf16[3,160,256]{2,1,0:T(8,128)(2,1)}, u32[]{:S(2)}) copy-start(bf16[3,160,256]{2,1,0:T(8,128)(2,1)} %get-tuple-element.103.ends_ref) | copy-start | bytes 737284
  281.1 13.5 %copy-start.7 = (f32[8,8,768]{2,1,0:T(8,128)S(1)}, f32[8,8,768]{2,1,0:T(8,128)}, u32[]{:S(2)}) copy-start(f32[8,8,768]{2,1,0:T(8,128)} %get-tuple-element.105.small_ref) | copy-start | bytes 589828
  294.7 1.0 copy-start.5
  295.7 0.8 copy-start.8

commit v7 on v6

--- a/solution.py
+++ b/solution.py
@@ -242,7 +242,7 @@
     coef2 = dot_nt(act, right).astype(bf16)
     p2 = p2 + dsum
     base2 = pre["c2"] + p2 + dot_nt(act, p2_h)
-    fill(2)
+    fill(5)
     side = base2 + dot_nn(coef2, left)
     p1 = p1 + dot_tn(kq, dz)
     p2t = p2t + dot_tn(left, right)
@@ -259,7 +259,7 @@
     d_fac = d_s2 * pre["fac"]
     main = dot_nn(d_fac.astype(bf16), w2_h)
     a1, a2, a3, a4 = (jnp.sum(d_s2 * w, axis=1, keepdims=True) for w in pre["weights"])
-    fill(5)
+    fill(2)
     y1, y2, y3, y4 = pre["prods"]
     d_act = (main + rest) - ((a1 * y1 + a2 * y2) + (a3 * y3 + a4 * y4))
     d_z1_h = (d_act * der + bend).astype(bf16)

time: 298 us -> 287 us (0.963)
  Pallas kernels: 295 us -> 283 us
    pallas_call x1, Pallas kernels: 131 us -> 118 us  [chain_backward(): pl.pallas_call(functools.partial(bwd_kernel, block, heads, turn), grid=(n...]
where the time goes in v7:
time: 287 us; the launch traced here: 286 us
  Pallas kernels  283 us (99%)
    pallas_call x1, Pallas kernels, chain_backward(): pl.pallas_call(functools.partial(bwd_kernel, block, heads, turn), grid=(n...  118 us
    pallas_call x1, Pallas kernels, middle(): pl.pallas_call(functools.partial(mid_kernel, count), in_specs=[vmem] * le...  105 us
    pallas_call x1, Pallas kernels, chain_forward(): pl.pallas_call(functools.partial(fwd_kernel, block, heads, count), grid=(...  32 us
    pallas_call x1, Pallas kernels, tail(): pl.pallas_call(functools.partial(tail_kernel, count, at_mix), in_specs=[v...  13.7 us
    pallas_call x1, Pallas kernels, front(): pl.pallas_call(functools.partial(front_kernel, count), in_specs=[vmem] *...  12.5 us

profile of v7, /device:TPU:0, one launch (start us, length us, event | category | flops | bytes accessed | tf_op | source)
XLA Modules:
  0.0 285.8 jit_solution(4097523202745798369)
XLA Ops:
  0.7 12.5 %front.1 = (bf16[256,768]{1,0:T(8,128)(2,1)}, bf16[256,768]{1,0:T(8,128)(2,1)}, bf16[256,768]{1,0:T(8,128)(2,1)}) custom-call(bf16[192,256]{1,0:T(8,128)(2,1)} %bitcast.29, f32[768]{0:T(1024)} %gain_ref.3, f32[3]{0:T(128)} %bias_ref.1, bf16[192,768]{1,0:T(8,128)(2,1)} %bitcast.21, bf16[192,768]{1,0:T(8,128)(2,1)} %bitcast.23, bf16[192,768]{1,0:T(8,128)(2,1)} %bitcast.25, ...), custom_call_target="tpu_custom_call" | custom-call | tf_op jit(solution)/shard_map/front/pallas_call | solution.py:1123
  13.2 32.0 %inner_forward.1 = (bf16[3,256,64]{2,1,0:T(8,128)(2,1)}, bf16[4,192,256]{2,1,0:T(8,128)(2,1)}, bf16[2048,80]{1,0:T(8,128)(2,1)}, bf16[2048,80]{1,0:T(8,128)(2,1)...) custom-call(bf16[256,768]{1,0:T(8,128)(2,1)} %get-tuple-element.75.p, ...), custom_call_target="tpu_custom_call" | custom-call | tf_op jit(solution)/shard_map/inner_forward/pallas_call | solution.py:510
  45.2 104.9 %middle.1 = (bf16[3,256,64]{2,1,0:T(8,128)(2,1)}, bf16[768,1920]{1,0:T(8,128)(2,1)}, bf16[256,192]{1,0:T(8,128)(2,1)}, f32[256,192]{1,0:T(8,128)}, f32[256,192]{...) custom-call(bf16[3,256,64]{2,1,0:T(8,128)(2,1)} %get-tuple-element.76.mixed_ref, ...), custom_call_target="tpu_custom_call" | custom-call | tf_op jit(solution)/shard_map/middle/pallas_call | solution.py:1041
  150.1 118.5 %inner_backward.1 = (bf16[3,256,256]{2,1,0:T(8,128)(2,1)}, bf16[3,160,256]{2,1,0:T(8,128)(2,1)}, bf16[3,96,256]{2,1,0:T(8,128)(2,1)}, f32[96,1920]{1,0:T(8,128)}, f32[8,8,768]{2,1,0:T(8,128)}) custom-call(bf16[3,256,64]{2,1,0:T(8,128)(2,1)} %get-tuple-element.82.gm_ref, bf16[4,2,96,1920]{3,2,1,0:T(8,128)(2,1)} %bitcast.18, ...), custom_call_target="tpu_custom_call" | custom-call | tf_op jit(solution)/shard_map/inner_backward/pallas_call | solution.py:758
  268.5 0.0 copy-start
  268.6 0.0 copy-start.1
  268.6 0.0 copy-start.2
  268.6 0.0 copy-start.3
  268.6 0.0 copy-start.4
  268.6 0.0 copy-start.6
  268.6 0.0 copy-start.7
  268.6 13.7 %tail.1 = (f32[256,192]{1,0:T(8,128)}, f32[8,8,128]{2,1,0:T(8,128)}) custom-call(bf16[3,256,256]{2,1,0:T(8,128)(2,1)} %get-tuple-element.97.grads_ref, bf16[192,768]{1,0:T(8,128)(2,1)} %bitcast.22, bf16[192,768]{1,0:T(8,128)(2,1)} %bitcast.24, bf16[192,768]{1,0:T(8,128)(2,1)} %bitcast.26, bf16[3,768]{1,0:T(4,128)(2,1)} %bitcast.32, ...), custom_call_target="tpu_custom_call" | custom-call | tf_op jit(solution)/shard_map/tail/pallas_call | solution.py:1232
  282.3 0.0 copy-done
  282.3 0.0 copy-done.1
  282.3 0.0 copy-done.2
  282.3 0.0 copy-done.3
  282.4 0.0 copy-done.4
  282.4 0.0 copy-done.6
  282.4 0.0 copy-done.7
  282.4 0.0 copy-start.5
  282.4 0.9 copy-done.5
  283.3 0.0 copy-start.8
  283.3 0.8 copy-done.8
  284.1 1.5 final.1
Async XLA Ops:
  268.5 13.8 %copy-start = (f32[96,1920]{1,0:T(8,128)S(1)}, f32[96,1920]{1,0:T(8,128)}, u32[]{:S(2)}) copy-start(f32[96,1920]{1,0:T(8,128)} %get-tuple-element.100.early_ref) | copy-start | bytes 2211844
  268.6 13.8 %copy-start.1 = (bf16[3,96,256]{2,1,0:T(8,128)(2,1)S(1)}, bf16[3,96,256]{2,1,0:T(8,128)(2,1)}, u32[]{:S(2)}) copy-start(bf16[3,96,256]{2,1,0:T(8,128)(2,1)} %get-tuple-element.99.late_ref) | copy-start | bytes 442372
  268.6 13.8 %copy-start.2 = (f32[256,192]{1,0:T(8,128)S(1)}, f32[256,192]{1,0:T(8,128)}, u32[]{:S(2)}) copy-start(f32[256,192]{1,0:T(8,128)} %get-tuple-element.80.down_ref) | copy-start | bytes 589828
  268.6 13.8 %copy-start.3 = (f32[256,192]{1,0:T(8,128)S(1)}, f32[256,192]{1,0:T(8,128)}, u32[]{:S(2)}) copy-start(f32[256,192]{1,0:T(8,128)} %get-tuple-element.81.resid_ref) | copy-start | bytes 589828
  268.6 13.8 %copy-start.4 = (f32[256,192]{1,0:T(8,128)S(1)}, f32[256,192]{1,0:T(8,128)}, u32[]{:S(2)}) copy-start(f32[256,192]{1,0:T(8,128)} %get-tuple-element.102.grc_ref) | copy-start | bytes 589828
  268.6 13.8 %copy-start.6 = (bf16[3,160,256]{2,1,0:T(8,128)(2,1)S(1)}, bf16[3,160,256]{2,1,0:T(8,128)(2,1)}, u32[]{:S(2)}) copy-start(bf16[3,160,256]{2,1,0:T(8,128)(2,1)} %get-tuple-element.103.ends_ref) | copy-start | bytes 737284
  268.6 13.8 %copy-start.7 = (f32[8,8,768]{2,1,0:T(8,128)S(1)}, f32[8,8,768]{2,1,0:T(8,128)}, u32[]{:S(2)}) copy-start(f32[8,8,768]{2,1,0:T(8,128)} %get-tuple-element.105.small_ref) | copy-start | bytes 589828
  282.4 1.0 copy-start.5
  283.3 0.8 copy-start.8

commit v8 on v7

--- a/solution.py
+++ b/solution.py
@@ -247,7 +247,7 @@
     p1 = p1 + dot_tn(kq, dz)
     p2t = p2t + dot_tn(left, right)
     next(after, None)
-    fill(1)
+    fill(2)
     d_upd = d_s1 * der
     d_upd_h = d_upd.astype(bf16)
     d_s2 = dot_nt(d_upd_h, w2_h) - side
@@ -255,7 +255,7 @@
     p1_h = p1.astype(bf16)
     bend = d_s1 * pre["bend"]
     next(after, None)
-    fill(3)
+    fill(2)
     d_fac = d_s2 * pre["fac"]
     main = dot_nn(d_fac.astype(bf16), w2_h)
     a1, a2, a3, a4 = (jnp.sum(d_s2 * w, axis=1, keepdims=True) for w in pre["weights"])

time: 287 us -> 284 us (0.990)
  Pallas kernels: 283 us -> 280 us
    pallas_call x1, Pallas kernels: 118 us -> 115 us  [chain_backward(): pl.pallas_call(functools.partial(bwd_kernel, block, heads, turn), grid=(n...]
where the time goes in v8:
time: 284 us; the launch traced here: 283 us
  Pallas kernels  280 us (99%)
    pallas_call x1, Pallas kernels, chain_backward(): pl.pallas_call(functools.partial(bwd_kernel, block, heads, turn), grid=(n...  115 us
    pallas_call x1, Pallas kernels, middle(): pl.pallas_call(functools.partial(mid_kernel, count), in_specs=[vmem] * le...  105 us
    pallas_call x1, Pallas kernels, chain_forward(): pl.pallas_call(functools.partial(fwd_kernel, block, heads, count), grid=(...  32 us
    pallas_call x1, Pallas kernels, tail(): pl.pallas_call(functools.partial(tail_kernel, count, at_mix), in_specs=[v...  13.7 us
    pallas_call x1, Pallas kernels, front(): pl.pallas_call(functools.partial(front_kernel, count), in_specs=[vmem] *...  12.5 us

profile of v8, /device:TPU:0, one launch (start us, length us, event | category | flops | bytes accessed | tf_op | source)
XLA Modules:
  0.0 282.6 jit_solution(5197247862879625671)
XLA Ops:
  0.7 12.5 %front.1 = (bf16[256,768]{1,0:T(8,128)(2,1)}, bf16[256,768]{1,0:T(8,128)(2,1)}, bf16[256,768]{1,0:T(8,128)(2,1)}) custom-call(bf16[192,256]{1,0:T(8,128)(2,1)} %bitcast.29, f32[768]{0:T(1024)} %gain_ref.3, f32[3]{0:T(128)} %bias_ref.1, bf16[192,768]{1,0:T(8,128)(2,1)} %bitcast.21, bf16[192,768]{1,0:T(8,128)(2,1)} %bitcast.23, bf16[192,768]{1,0:T(8,128)(2,1)} %bitcast.25, ...), custom_call_target="tpu_custom_call" | custom-call | tf_op jit(solution)/shard_map/front/pallas_call | solution.py:1123
  13.2 32.0 %inner_forward.1 = (bf16[3,256,64]{2,1,0:T(8,128)(2,1)}, bf16[4,192,256]{2,1,0:T(8,128)(2,1)}, bf16[2048,80]{1,0:T(8,128)(2,1)}, bf16[2048,80]{1,0:T(8,128)(2,1)...) custom-call(bf16[256,768]{1,0:T(8,128)(2,1)} %get-tuple-element.75.p, ...), custom_call_target="tpu_custom_call" | custom-call | tf_op jit(solution)/shard_map/inner_forward/pallas_call | solution.py:510
  45.2 104.9 %middle.1 = (bf16[3,256,64]{2,1,0:T(8,128)(2,1)}, bf16[768,1920]{1,0:T(8,128)(2,1)}, bf16[256,192]{1,0:T(8,128)(2,1)}, f32[256,192]{1,0:T(8,128)}, f32[256,192]{...) custom-call(bf16[3,256,64]{2,1,0:T(8,128)(2,1)} %get-tuple-element.76.mixed_ref, ...), custom_call_target="tpu_custom_call" | custom-call | tf_op jit(solution)/shard_map/middle/pallas_call | solution.py:1041
  150.1 115.3 %inner_backward.1 = (bf16[3,256,256]{2,1,0:T(8,128)(2,1)}, bf16[3,160,256]{2,1,0:T(8,128)(2,1)}, bf16[3,96,256]{2,1,0:T(8,128)(2,1)}, f32[96,1920]{1,0:T(8,128)}, f32[8,8,768]{2,1,0:T(8,128)}) custom-call(bf16[3,256,64]{2,1,0:T(8,128)(2,1)} %get-tuple-element.82.gm_ref, bf16[4,2,96,1920]{3,2,1,0:T(8,128)(2,1)} %bitcast.18, ...), custom_call_target="tpu_custom_call" | custom-call | tf_op jit(solution)/shard_map/inner_backward/pallas_call | solution.py:758
  265.4 0.0 copy-start
  265.4 0.0 copy-start.1
  265.4 0.0 copy-start.2
  265.4 0.0 copy-start.3
  265.4 0.0 copy-start.4
  265.4 0.0 copy-start.6
  265.4 0.0 copy-start.7
  265.4 13.7 %tail.1 = (f32[256,192]{1,0:T(8,128)}, f32[8,8,128]{2,1,0:T(8,128)}) custom-call(bf16[3,256,256]{2,1,0:T(8,128)(2,1)} %get-tuple-element.97.grads_ref, bf16[192,768]{1,0:T(8,128)(2,1)} %bitcast.22, bf16[192,768]{1,0:T(8,128)(2,1)} %bitcast.24, bf16[192,768]{1,0:T(8,128)(2,1)} %bitcast.26, bf16[3,768]{1,0:T(4,128)(2,1)} %bitcast.32, ...), custom_call_target="tpu_custom_call" | custom-call | tf_op jit(solution)/shard_map/tail/pallas_call | solution.py:1232
  279.1 0.0 copy-done
  279.2 0.0 copy-done.1
  279.2 0.0 copy-done.2
  279.2 0.0 copy-done.3
  279.2 0.0 copy-done.4
  279.2 0.0 copy-done.6
  279.2 0.0 copy-done.7
  279.2 0.0 copy-start.5
  279.2 0.9 copy-done.5
  280.2 0.0 copy-start.8
  280.2 0.8 copy-done.8
  280.9 1.5 final.1
Async XLA Ops:
  265.4 13.8 %copy-start = (f32[96,1920]{1,0:T(8,128)S(1)}, f32[96,1920]{1,0:T(8,128)}, u32[]{:S(2)}) copy-start(f32[96,1920]{1,0:T(8,128)} %get-tuple-element.100.early_ref) | copy-start | bytes 2211844
  265.4 13.8 %copy-start.1 = (bf16[3,96,256]{2,1,0:T(8,128)(2,1)S(1)}, bf16[3,96,256]{2,1,0:T(8,128)(2,1)}, u32[]{:S(2)}) copy-start(bf16[3,96,256]{2,1,0:T(8,128)(2,1)} %get-tuple-element.99.late_ref) | copy-start | bytes 442372
  265.4 13.8 %copy-start.2 = (f32[256,192]{1,0:T(8,128)S(1)}, f32[256,192]{1,0:T(8,128)}, u32[]{:S(2)}) copy-start(f32[256,192]{1,0:T(8,128)} %get-tuple-element.80.down_ref) | copy-start | bytes 589828
  265.4 13.8 %copy-start.3 = (f32[256,192]{1,0:T(8,128)S(1)}, f32[256,192]{1,0:T(8,128)}, u32[]{:S(2)}) copy-start(f32[256,192]{1,0:T(8,128)} %get-tuple-element.81.resid_ref) | copy-start | bytes 589828
  265.4 13.8 %copy-start.4 = (f32[256,192]{1,0:T(8,128)S(1)}, f32[256,192]{1,0:T(8,128)}, u32[]{:S(2)}) copy-start(f32[256,192]{1,0:T(8,128)} %get-tuple-element.102.grc_ref) | copy-start | bytes 589828
  265.4 13.8 %copy-start.6 = (bf16[3,160,256]{2,1,0:T(8,128)(2,1)S(1)}, bf16[3,160,256]{2,1,0:T(8,128)(2,1)}, u32[]{:S(2)}) copy-start(bf16[3,160,256]{2,1,0:T(8,128)(2,1)} %get-tuple-element.103.ends_ref) | copy-start | bytes 737284
  265.4 13.8 %copy-start.7 = (f32[8,8,768]{2,1,0:T(8,128)S(1)}, f32[8,8,768]{2,1,0:T(8,128)}, u32[]{:S(2)}) copy-start(f32[8,8,768]{2,1,0:T(8,128)} %get-tuple-element.105.small_ref) | copy-start | bytes 589828
  279.2 1.0 copy-start.5
  280.2 0.8 copy-start.8
